TPU v7x, 32 devices: a whole 2x2x4 slice. The times are simulated.
32 devices in a mesh: brick: 8 (over z, y), depth: 4 (over x, core).
Axes of the slice: x: 2, y: 2, z: 4, core: 2. Of those that a mesh axis runs over, the one named last changes fastest.
Arguments:
- conductivity: float32 [64, 64, 256], P('brick', 'depth'), may hold values from 0.03 to 10.5, as said below
- initial_field: float32 [2, 64, 64, 256], P(None, 'brick', 'depth'), may hold values from -1.2 to 1.2
- adjoint_initial: float32 [2, 64, 64, 256], P(None, 'brick', 'depth'), may hold values from -0.36 to 0.36
- src_cell: int32 [8, 4, 64], P('brick', 'depth'), may hold values from 0 to 32767
- src_amp: float32 [8, 4, 2, 64], P('brick', 'depth'), may hold values from -24 to 24
- rec_cell: int32 [8, 4, 64], P('brick', 'depth'), may hold values from 0 to 32767
- observed: float32 [8, 4, 2, 64], P('brick', 'depth'), may hold values from -12 to 12
- cov_blocks: bfloat16 [8, 4, 16, 512, 512], P('brick', 'depth'), may hold values from -0.25 to 0.25
- cov_rows: int32 [8, 4, 16], P('brick', 'depth'), may hold values from 0 to 63
- cov_cols: int32 [8, 4, 16], P('brick', 'depth'), may hold values from 0 to 255
Outputs:
- forward: float32 [2, 64, 64, 256], P(None, 'brick', 'depth')
- preconditioned: float32 [64, 64, 256], P('brick', 'depth')
Inputs may be any that keep to these rules, and one draw needn't show every extreme that they name: `conductivity`: positive everywhere.
All inputs are finite; a program needn't handle non-finite values.
Results may differ from a plain program's by a relative error of at most 0.0032.
Values may be sent and summed in bfloat16 or wider, within the bound.
No kernel may reach another device: no remote copies, remote signals or barrier semaphores. Data moves between devices by JAX's collectives and lax.ppermute only.
A program may use at most 128 MiB of HBM per device.

v0:
```python
import jax
import jax.numpy as jnp
from jax import lax
from jax.sharding import PartitionSpec as P

ITERS = 3


LAPLACE_SHIFTS = (0.5, 2.0)


def padded_2(shard, sides, width):
    for axis, dim in sides:
        size, length = (lax.axis_size(axis), shard.shape[dim])
        up = [(i, (i + 1) % size) for i in range(size - 1)]
        down = [(j, i) for i, j in up]
        last = lax.slice_in_dim(shard, length - width, length, axis=dim)
        initial = lax.slice_in_dim(shard, 0, width, axis=dim)
        before = lax.ppermute(last, axis, up)
        after = lax.ppermute(initial, axis, down)
        shard = jnp.concatenate([before, shard, after], axis=dim)
    return shard


def spread(values):
    return values[:, None, None, None]


def local_inner(first, second):
    return jnp.sum(first * second, axis=(1, 2, 3))


def operate(volume, damping):
    padded = padded_2(volume, (("brick", 1), ("depth", 2)), 1)
    beside = padded[:, 2:, 1:-1, :] + padded[:, :-2, 1:-1, :]
    beside = beside + padded[:, 1:-1, 2:, :] + padded[:, 1:-1, :-2, :]
    lateral = jnp.pad(volume, ((0, 0), (0, 0), (0, 0), (1, 1)))
    beside = beside + lateral[:, :, :, 2:] + lateral[:, :, :, :-2]
    return (6.0 + damping) * volume - beside


def paired_sums(residual, applied):
    return lax.psum(
        (local_inner(residual, residual), local_inner(residual, applied)), ("brick", "depth")
    )


def conjugate(source_term, initial, damping):
    solution = initial
    residual = source_term - operate(initial, damping)
    applied = operate(residual, damping)
    norm_now, product = paired_sums(residual, applied)
    step_len = norm_now / product
    direction = residual
    along = applied
    for iteration in range(ITERS):
        solution = solution + spread(step_len) * direction
        residual = residual - spread(step_len) * along
        if iteration + 1 < ITERS:
            applied = operate(residual, damping)
            norm_next, product = paired_sums(residual, applied)
            ratio = norm_next / norm_now
            step_len = norm_next / (product - ratio * norm_next / step_len)
            direction = residual + spread(ratio) * direction
            along = applied + spread(ratio) * along
            norm_now = norm_next
    return solution


def local(
    conductivity,
    initial_field,
    adjoint_initial,
    src_cell,
    src_amp,
    rec_cell,
    observed,
    cov_blocks,
    cov_rows,
    cov_cols,
):
    size_x, size_z, size_y = conductivity.shape
    total_cells = size_x * size_z * size_y
    block_size = cov_blocks.shape[-1]
    blocks_here = total_cells // block_size
    shifts = jnp.array(LAPLACE_SHIFTS, jnp.float32)
    damping = spread(shifts) * conductivity[None]
    positions = jnp.arange(total_cells, dtype=jnp.int32)

    def place_points(cell_list, amount_list):
        onehot = (cell_list[:, None] == positions[None, :]).astype(jnp.float32)
        placed = jnp.dot(amount_list, onehot, precision=lax.Precision.HIGHEST)
        return placed.reshape(2, size_x, size_z, size_y)

    forward = conjugate(place_points(src_cell[0, 0], src_amp[0, 0]), initial_field, damping)
    flat_forward = forward.reshape(2, total_cells)
    misfit = flat_forward[:, rec_cell[0, 0]] - observed[0, 0]
    adjoint = conjugate(place_points(rec_cell[0, 0], misfit), adjoint_initial, damping)
    gradient = (-jnp.sum(spread(shifts) * forward * adjoint, axis=0)).astype(jnp.bfloat16)
    grad_blocks = gradient.reshape(blocks_here, block_size)
    columns = cov_cols[0, 0]
    every_block = lax.all_gather(grad_blocks, "depth", axis=0, tiled=True)
    picked = jnp.take(every_block, columns, axis=0)
    terms = jnp.einsum("kij,kj->ki", cov_blocks[0, 0], picked, preferred_element_type=jnp.float32)
    row_table = (
        jnp.arange(blocks_here, dtype=jnp.int32)[:, None] == cov_rows[0, 0][None, :]
    ).astype(jnp.float32)
    added = jnp.dot(row_table, terms, precision=lax.Precision.HIGHEST)
    preconditioned = (grad_blocks.astype(jnp.float32) + added).reshape(size_x, size_z, size_y)
    return (forward, preconditioned)


def solution(mesh):
    return jax.shard_map(
        local,
        mesh=mesh,
        in_specs=(
            P("brick", "depth", None),
            P(None, "brick", "depth", None),
            P(None, "brick", "depth", None),
            P("brick", "depth", None),
            P("brick", "depth", None, None),
            P("brick", "depth", None),
            P("brick", "depth", None, None),
            P("brick", "depth", None, None, None),
            P("brick", "depth", None),
            P("brick", "depth", None),
        ),
        out_specs=(P(None, "brick", "depth", None), P("brick", "depth", None)),
        check_vma=False,
    )
```

profile of v0, /device:TPU:0, one launch (start us, length us, event | category | flops | bytes accessed | tf_op | source)
XLA Modules:
  0.0 414.1 jit_solution(8782699796489954295)
XLA Ops:
  1.9 4.9 %collective-permute-start.1 = (f32[2,1,16,256]{3,0,2,1:T(2,128)S(1)}, f32[2,1,16,256]{3,0,2,1:T(2,128)S(1)}, u32[]{:S(2)}, u32[]{:S(2)}) collective-permute-start(f32[2,1,16,256]{3,0,2,1:T(2,128)S(1)} %get-tuple-element.75), channel_id=1, source_target_pairs={{0,4},{4,8},{8,12},{12,16},{16,20},{20,24},{24,28},{1,5},{5,9},{9,... | collective-permute-start | bytes 98312 | tf_op jit(solution)/shard_map/ppermute | solution.py:19
  6.8 1.3 collective-permute-start
  9.3 4.5 %collective-permute-start.17 = (f32[2,1,16,256]{3,0,2,1:T(2,128)S(1)}, f32[2,1,16,256]{3,0,2,1:T(2,128)S(1)}, u32[]{:S(2)}, u32[]{:S(2)}) collective-permute-start(f32[2,1,16,256]{3,0,2,1:T(2,128)S(1)} %get-tuple-element.67), channel_id=1, source_target_pairs={{0,4},{4,8},{8,12},{12,16},{16,20},{20,24},{24,28},{1,5},{5,9},{9,... | collective-permute-start | bytes 98312 | tf_op jit(solution)/shard_map/ppermute | solution.py:19
  13.9 1.3 collective-permute-start.16
  15.2 3.4 fusion.2
  19.8 1.3 collective-permute-start.2
  21.1 3.0 collective-permute-start.3
  25.0 1.5 fusion.14
  26.5 1.3 collective-permute-start.4
  27.8 5.6 %collective-permute-start.5 = (f32[2,1,16,256]{3,0,2,1:T(2,128)S(1)}, f32[2,1,16,256]{3,0,2,1:T(2,128)S(1)}, u32[]{:S(2)}, u32[]{:S(2)}) collective-permute-start(f32[2,1,16,256]{3,0,2,1:T(2,128)S(1)} %get-tuple-element.72), channel_id=1, source_target_pairs={{0,4},{4,8},{8,12},{12,16},{16,20},{20,24},{24,28},{1,5},{5,9},{9,... | collective-permute-start | bytes 98312 | tf_op jit(solution)/shard_map/ppermute | solution.py:19
  33.4 1.5 collective-permute-done.5
  35.0 1.3 collective-permute-start.6
  36.3 3.0 collective-permute-start.7
  40.2 1.8 multiply_reduce_fusion.9
  41.9 46.9 %all-reduce.13 = (f32[2]{0:T(128)S(1)}, f32[2]{0:T(128)S(1)}) all-reduce(f32[2]{0:T(128)S(1)} %get-tuple-element.17, f32[2]{0:T(128)S(1)} %get-tuple-element.16), channel_id=1, replica_groups=mesh['brick'=8,'depth'=4] {'brick','depth'}, use_global_device_ids=true, to_apply=%region_1.2 | all-reduce | flops 4 | bytes 32 | tf_op jit(solution)/shard_map/psum | solution.py:43
  89.1 1.3 collective-permute-start.8
  90.4 4.8 %collective-permute-start.9 = (f32[2,1,16,256]{3,0,2,1:T(2,128)S(1)}, f32[2,1,16,256]{3,0,2,1:T(2,128)S(1)}, u32[]{:S(2)}, u32[]{:S(2)}) collective-permute-start(f32[2,1,16,256]{3,0,2,1:T(2,128)S(1)} %get-tuple-element.70), channel_id=1, source_target_pairs={{0,4},{4,8},{8,12},{12,16},{16,20},{20,24},{24,28},{1,5},{5,9},{9,... | collective-permute-start | bytes 98312 | tf_op jit(solution)/shard_map/ppermute | solution.py:19
  95.2 1.5 collective-permute-done.9
  96.8 1.3 collective-permute-start.10
  98.1 3.0 collective-permute-start.11
  102.8 43.5 %all-reduce.12 = (f32[2]{0:T(128)S(1)}, f32[2]{0:T(128)S(1)}) all-reduce(f32[2]{0:T(128)S(1)} %get-tuple-element.15, f32[2]{0:T(128)S(1)} %get-tuple-element.14), channel_id=1, replica_groups=mesh['brick'=8,'depth'=4] {'brick','depth'}, use_global_device_ids=true, to_apply=%region_5.6 | all-reduce | flops 4 | bytes 32 | tf_op jit(solution)/shard_map/psum | solution.py:43
  146.6 1.3 collective-permute-start.12
  147.9 4.8 %collective-permute-start.13 = (f32[2,1,16,256]{3,0,2,1:T(2,128)S(1)}, f32[2,1,16,256]{3,0,2,1:T(2,128)S(1)}, u32[]{:S(2)}, u32[]{:S(2)}) collective-permute-start(f32[2,1,16,256]{3,0,2,1:T(2,128)S(1)} %get-tuple-element.68), channel_id=1, source_target_pairs={{0,4},{4,8},{8,12},{12,16},{16,20},{20,24},{24,28},{1,5},{5,9},{9,... | collective-permute-start | bytes 98312 | tf_op jit(solution)/shard_map/ppermute | solution.py:19
  152.7 1.5 collective-permute-done.13
  154.3 1.3 collective-permute-start.14
  155.6 3.0 collective-permute-start.15
  158.7 1.3 collective-permute-start.18
  160.0 4.2 %collective-permute-start.19 = (f32[2,10,1,256]{3,0,2,1:T(2,128)S(1)}, f32[2,10,1,256]{3,0,2,1:T(2,128)S(1)}, u32[]{:S(2)}, u32[]{:S(2)}) collective-permute-start(f32[2,10,1,256]{3,0,2,1:T(2,128)S(1)} %get-tuple-element.51), channel_id=1, source_target_pairs={{0,1},{1,2},{2,3},{4,5},{5,6},{6,7},{8,9},{9,10},{10,11},{12,13},{... | collective-permute-start | bytes 61448 | tf_op jit(solution)/shard_map/ppermute | solution.py:19
  165.0 42.4 %all-reduce.11 = (f32[2]{0:T(128)S(1)}, f32[2]{0:T(128)S(1)}) all-reduce(f32[2]{0:T(128)S(1)} %get-tuple-element.13, f32[2]{0:T(128)S(1)} %get-tuple-element.12), channel_id=1, replica_groups=mesh['brick'=8,'depth'=4] {'brick','depth'}, use_global_device_ids=true, to_apply=%region_9.10 | all-reduce | flops 4 | bytes 32 | tf_op jit(solution)/shard_map/psum | solution.py:43
  207.9 8.3 %copy.41 = f32[2,32768]{0,1:T(8,128)} copy(f32[2,32768]{1,0:T(2,128)S(1)} %bitcast.41) | data formatting | bytes 524288 | tf_op jit(solution)/shard_map/reshape | solution.py:96
  216.3 6.4 %gather_fusion = f32[64,2]{1,0:T(8,128)S(1)} fusion(f32[2,32768]{0,1:T(8,128)} %copy.41, s32[1024]{0:T(1024)S(1)} %pad_clamp_fusion.1), kind=kCustom, calls=%fused_computation | custom fusion | bytes 1280 | tf_op jit(solution)/shard_map/gather | solution.py:97
  222.7 2.7 fusion.8
  226.8 4.8 %collective-permute-start.21 = (f32[2,1,16,256]{3,0,2,1:T(2,128)S(1)}, f32[2,1,16,256]{3,0,2,1:T(2,128)S(1)}, u32[]{:S(2)}, u32[]{:S(2)}) collective-permute-start(f32[2,1,16,256]{3,0,2,1:T(2,128)S(1)} %get-tuple-element.64), channel_id=1, source_target_pairs={{0,4},{4,8},{8,12},{12,16},{16,20},{20,24},{24,28},{1,5},{5,9},{9,... | collective-permute-start | bytes 98312 | tf_op jit(solution)/shard_map/ppermute | solution.py:19
  231.6 1.6 collective-permute-done.21
  233.2 1.3 collective-permute-start.22
  234.5 3.0 collective-permute-start.23
  239.2 43.9 %all-reduce.10 = (f32[2]{0:T(128)S(1)}, f32[2]{0:T(128)S(1)}) all-reduce(f32[2]{0:T(128)S(1)} %get-tuple-element.11, f32[2]{0:T(128)S(1)} %get-tuple-element.10), channel_id=1, replica_groups=mesh['brick'=8,'depth'=4] {'brick','depth'}, use_global_device_ids=true, to_apply=%region_13.14 | all-reduce | flops 4 | bytes 32 | tf_op jit(solution)/shard_map/psum | solution.py:43
  283.4 1.3 collective-permute-start.24
  284.7 4.8 %collective-permute-start.25 = (f32[2,1,16,256]{3,0,2,1:T(2,128)S(1)}, f32[2,1,16,256]{3,0,2,1:T(2,128)S(1)}, u32[]{:S(2)}, u32[]{:S(2)}) collective-permute-start(f32[2,1,16,256]{3,0,2,1:T(2,128)S(1)} %get-tuple-element.62), channel_id=1, source_target_pairs={{0,4},{4,8},{8,12},{12,16},{16,20},{20,24},{24,28},{1,5},{5,9},{9,... | collective-permute-start | bytes 98312 | tf_op jit(solution)/shard_map/ppermute | solution.py:19
  289.5 1.6 collective-permute-done.25
  292.4 3.0 collective-permute-start.27
  297.0 44.2 %all-reduce.9 = (f32[2]{0:T(128)S(1)}, f32[2]{0:T(128)S(1)}) all-reduce(f32[2]{0:T(128)S(1)} %get-tuple-element.9, f32[2]{0:T(128)S(1)} %get-tuple-element.8), channel_id=1, replica_groups=mesh['brick'=8,'depth'=4] {'brick','depth'}, use_global_device_ids=true, to_apply=%region_17.18 | all-reduce | flops 4 | bytes 32 | tf_op jit(solution)/shard_map/psum | solution.py:43
  342.9 4.8 %collective-permute-start.29 = (f32[2,1,16,256]{3,0,2,1:T(2,128)S(1)}, f32[2,1,16,256]{3,0,2,1:T(2,128)S(1)}, u32[]{:S(2)}, u32[]{:S(2)}) collective-permute-start(f32[2,1,16,256]{3,0,2,1:T(2,128)S(1)} %get-tuple-element.60), channel_id=1, source_target_pairs={{0,4},{4,8},{8,12},{12,16},{16,20},{20,24},{24,28},{1,5},{5,9},{9,... | collective-permute-start | bytes 98312 | tf_op jit(solution)/shard_map/ppermute | solution.py:19
  347.7 1.6 collective-permute-done.29
  350.6 3.0 collective-permute-start.31
  355.3 44.2 %all-reduce.8 = (f32[2]{0:T(128)S(1)}, f32[2]{0:T(128)S(1)}) all-reduce(f32[2]{0:T(128)S(1)} %get-tuple-element.7, f32[2]{0:T(128)S(1)} %get-tuple-element.6), channel_id=1, replica_groups=mesh['brick'=8,'depth'=4] {'brick','depth'}, use_global_device_ids=true, to_apply=%region_21.22 | all-reduce | flops 4 | bytes 32 | tf_op jit(solution)/shard_map/psum | solution.py:43
  400.4 6.5 %all_gather.3 = bf16[256,512]{1,0:T(8,128)(2,1)S(1)} all-gather(bf16[64,512]{1,0:T(8,128)(2,1)S(1)} %convert_element_type.23), channel_id=1, replica_groups=mesh['brick'=8,'depth'=4] {'depth'}, dimensions={0}, use_global_device_ids=true | all-gather | bytes 327680 | tf_op jit(solution)/shard_map/all_gather | solution.py:102
  407.6 5.6 %fusion = f32[16,1,512]{2,1,0:T(1,128)S(1)} fusion(bf16[1,1,16,512,512]{4,3,2,1,0:T(8,128)(2,1)} %param.18, bf16[16,512,1]{1,0,2:T(8,128)(2,1)S(1)} %select_bitcast_fusion), kind=kOutput, calls=%fused_computation.2 | convolution fusion | flops 8388608 | bytes 8437760 | tf_op jit(solution)/shard_map/kij,kj->ki/dot_general | solution.py:104
  (103 shorter events, 22.0 us)
Async XLA Ops:
  0.6 14.5 %copy-start = (f32[1,1,2,64]{3,2,1,0:T(2,128)S(1)}, f32[1,1,2,64]{3,2,1,0:T(2,128)}, u32[]{:S(2)}) copy-start(f32[1,1,2,64]{3,2,1,0:T(2,128)} %param.15) | copy-start | bytes 1540
  0.6 101.3 %copy-start.4 = (f32[2]{0:T(128)S(1)}, f32[2]{0:T(128)}, u32[]{:S(2)}) copy-start(f32[2]{0:T(128)} %constant.30.clone) | copy-start | bytes 28
  0.7 206.8 %copy-start.2 = (f32[2,8,16,256]{3,2,1,0:T(8,128)S(1)}, f32[2,8,16,256]{3,2,1,0:T(8,128)}, u32[]{:S(2)}) copy-start(f32[2,8,16,256]{3,2,1,0:T(8,128)} %param.12) | copy-start | bytes 786436
  0.7 100.5 %copy-start.3 = (f32[2,8,16,256]{3,2,1,0:T(8,128)S(1)}, f32[2,8,16,256]{3,2,1,0:T(8,128)}, u32[]{:S(2)}) copy-start(f32[2,8,16,256]{3,2,1,0:T(8,128)} %param.13) | copy-start | bytes 786436
  0.7 101.3 %copy-start.1 = (f32[8,16,256]{2,1,0:T(8,128)S(1)}, f32[8,16,256]{2,1,0:T(8,128)}, u32[]{:S(2)}) copy-start(f32[8,16,256]{2,1,0:T(8,128)} %param.11) | copy-start | bytes 393220
  1.9 16.6 %collective-permute-start.1 = (f32[2,1,16,256]{3,0,2,1:T(2,128)S(1)}, f32[2,1,16,256]{3,0,2,1:T(2,128)S(1)}, u32[]{:S(2)}, u32[]{:S(2)}) collective-permute-start(f32[2,1,16,256]{3,0,2,1:T(2,128)S(1)} %get-tuple-element.75), channel_id=1, source_target_pairs={{0,4},{4,8},{8,12},{12,16},{16,20},{20,24},{24,28},{1,5},{5,9},{9,... | collective-permute-start | bytes 98312 | tf_op jit(solution)/shard_map/ppermute | solution.py:19
  6.8 12.9 %collective-permute-start = (f32[2,1,16,256]{3,0,2,1:T(2,128)S(1)}, f32[2,1,16,256]{3,0,2,1:T(2,128)S(1)}, u32[]{:S(2)}, u32[]{:S(2)}) collective-permute-start(f32[2,1,16,256]{3,0,2,1:T(2,128)S(1)} %get-tuple-element.74), channel_id=1, source_target_pairs={{4,0},{8,4},{12,8},{16,12},{20,16},{24,20},{28,24},{5,1},{9,5},{13... | collective-permute-start | bytes 98312 | tf_op jit(solution)/shard_map/ppermute | solution.py:20
  9.3 85.9 %collective-permute-start.17 = (f32[2,1,16,256]{3,0,2,1:T(2,128)S(1)}, f32[2,1,16,256]{3,0,2,1:T(2,128)S(1)}, u32[]{:S(2)}, u32[]{:S(2)}) collective-permute-start(f32[2,1,16,256]{3,0,2,1:T(2,128)S(1)} %get-tuple-element.67), channel_id=1, source_target_pairs={{0,4},{4,8},{8,12},{12,16},{16,20},{20,24},{24,28},{1,5},{5,9},{9,... | collective-permute-start | bytes 98312 | tf_op jit(solution)/shard_map/ppermute | solution.py:19
  13.9 138.8 %collective-permute-start.16 = (f32[2,1,16,256]{3,0,2,1:T(2,128)S(1)}, f32[2,1,16,256]{3,0,2,1:T(2,128)S(1)}, u32[]{:S(2)}, u32[]{:S(2)}) collective-permute-start(f32[2,1,16,256]{3,0,2,1:T(2,128)S(1)} %get-tuple-element.66), channel_id=1, source_target_pairs={{4,0},{8,4},{12,8},{16,12},{20,16},{24,20},{28,24},{5,1},{9,5},{13... | collective-permute-start | bytes 98312 | tf_op jit(solution)/shard_map/ppermute | solution.py:20
  19.8 5.0 %collective-permute-start.2 = (f32[2,10,1,256]{3,0,2,1:T(2,128)S(1)}, f32[2,10,1,256]{3,0,2,1:T(2,128)S(1)}, u32[]{:S(2)}, u32[]{:S(2)}) collective-permute-start(f32[2,10,1,256]{3,0,2,1:T(2,128)S(1)} %get-tuple-element.58), channel_id=1, source_target_pairs={{1,0},{2,1},{3,2},{5,4},{6,5},{7,6},{9,8},{10,9},{11,10},{13,12},{... | collective-permute-start | bytes 61448 | tf_op jit(solution)/shard_map/ppermute | solution.py:20
  21.1 3.9 collective-permute-start.3
  26.5 6.9 %collective-permute-start.4 = (f32[2,1,16,256]{3,0,2,1:T(2,128)S(1)}, f32[2,1,16,256]{3,0,2,1:T(2,128)S(1)}, u32[]{:S(2)}, u32[]{:S(2)}) collective-permute-start(f32[2,1,16,256]{3,0,2,1:T(2,128)S(1)} %get-tuple-element.73), channel_id=1, source_target_pairs={{4,0},{8,4},{12,8},{16,12},{20,16},{24,20},{28,24},{5,1},{9,5},{13... | collective-permute-start | bytes 98312 | tf_op jit(solution)/shard_map/ppermute | solution.py:20
  27.8 7.2 %collective-permute-start.5 = (f32[2,1,16,256]{3,0,2,1:T(2,128)S(1)}, f32[2,1,16,256]{3,0,2,1:T(2,128)S(1)}, u32[]{:S(2)}, u32[]{:S(2)}) collective-permute-start(f32[2,1,16,256]{3,0,2,1:T(2,128)S(1)} %get-tuple-element.72), channel_id=1, source_target_pairs={{0,4},{4,8},{8,12},{12,16},{16,20},{20,24},{24,28},{1,5},{5,9},{9,... | collective-permute-start | bytes 98312 | tf_op jit(solution)/shard_map/ppermute | solution.py:19
  35.0 4.4 %collective-permute-start.6 = (f32[2,10,1,256]{3,0,2,1:T(2,128)S(1)}, f32[2,10,1,256]{3,0,2,1:T(2,128)S(1)}, u32[]{:S(2)}, u32[]{:S(2)}) collective-permute-start(f32[2,10,1,256]{3,0,2,1:T(2,128)S(1)} %get-tuple-element.56), channel_id=1, source_target_pairs={{1,0},{2,1},{3,2},{5,4},{6,5},{7,6},{9,8},{10,9},{11,10},{13,12},{... | collective-permute-start | bytes 61448 | tf_op jit(solution)/shard_map/ppermute | solution.py:20
  36.3 3.9 collective-permute-start.7
  89.1 6.1 %collective-permute-start.8 = (f32[2,1,16,256]{3,0,2,1:T(2,128)S(1)}, f32[2,1,16,256]{3,0,2,1:T(2,128)S(1)}, u32[]{:S(2)}, u32[]{:S(2)}) collective-permute-start(f32[2,1,16,256]{3,0,2,1:T(2,128)S(1)} %get-tuple-element.71), channel_id=1, source_target_pairs={{4,0},{8,4},{12,8},{16,12},{20,16},{24,20},{28,24},{5,1},{9,5},{13... | collective-permute-start | bytes 98312 | tf_op jit(solution)/shard_map/ppermute | solution.py:20
  90.4 6.4 %collective-permute-start.9 = (f32[2,1,16,256]{3,0,2,1:T(2,128)S(1)}, f32[2,1,16,256]{3,0,2,1:T(2,128)S(1)}, u32[]{:S(2)}, u32[]{:S(2)}) collective-permute-start(f32[2,1,16,256]{3,0,2,1:T(2,128)S(1)} %get-tuple-element.70), channel_id=1, source_target_pairs={{0,4},{4,8},{8,12},{12,16},{16,20},{20,24},{24,28},{1,5},{5,9},{9,... | collective-permute-start | bytes 98312 | tf_op jit(solution)/shard_map/ppermute | solution.py:19
  96.8 4.6 %collective-permute-start.10 = (f32[2,10,1,256]{3,0,2,1:T(2,128)S(1)}, f32[2,10,1,256]{3,0,2,1:T(2,128)S(1)}, u32[]{:S(2)}, u32[]{:S(2)}) collective-permute-start(f32[2,10,1,256]{3,0,2,1:T(2,128)S(1)} %get-tuple-element.54), channel_id=1, source_target_pairs={{1,0},{2,1},{3,2},{5,4},{6,5},{7,6},{9,8},{10,9},{11,10},{13,12},{... | collective-permute-start | bytes 61448 | tf_op jit(solution)/shard_map/ppermute | solution.py:20
  98.1 3.9 collective-permute-start.11
  146.6 6.1 %collective-permute-start.12 = (f32[2,1,16,256]{3,0,2,1:T(2,128)S(1)}, f32[2,1,16,256]{3,0,2,1:T(2,128)S(1)}, u32[]{:S(2)}, u32[]{:S(2)}) collective-permute-start(f32[2,1,16,256]{3,0,2,1:T(2,128)S(1)} %get-tuple-element.69), channel_id=1, source_target_pairs={{4,0},{8,4},{12,8},{16,12},{20,16},{24,20},{28,24},{5,1},{9,5},{13... | collective-permute-start | bytes 98312 | tf_op jit(solution)/shard_map/ppermute | solution.py:20
  147.9 6.4 %collective-permute-start.13 = (f32[2,1,16,256]{3,0,2,1:T(2,128)S(1)}, f32[2,1,16,256]{3,0,2,1:T(2,128)S(1)}, u32[]{:S(2)}, u32[]{:S(2)}) collective-permute-start(f32[2,1,16,256]{3,0,2,1:T(2,128)S(1)} %get-tuple-element.68), channel_id=1, source_target_pairs={{0,4},{4,8},{8,12},{12,16},{16,20},{20,24},{24,28},{1,5},{5,9},{9,... | collective-permute-start | bytes 98312 | tf_op jit(solution)/shard_map/ppermute | solution.py:19
  154.3 9.8 %collective-permute-start.14 = (f32[2,10,1,256]{3,0,2,1:T(2,128)S(1)}, f32[2,10,1,256]{3,0,2,1:T(2,128)S(1)}, u32[]{:S(2)}, u32[]{:S(2)}) collective-permute-start(f32[2,10,1,256]{3,0,2,1:T(2,128)S(1)} %get-tuple-element.52), channel_id=1, source_target_pairs={{1,0},{2,1},{3,2},{5,4},{6,5},{7,6},{9,8},{10,9},{11,10},{13,12},{... | collective-permute-start | bytes 61448 | tf_op jit(solution)/shard_map/ppermute | solution.py:20
  155.6 8.6 %collective-permute-start.15 = (f32[2,10,1,256]{3,0,2,1:T(2,128)S(1)}, f32[2,10,1,256]{3,0,2,1:T(2,128)S(1)}, u32[]{:S(2)}, u32[]{:S(2)}) collective-permute-start(f32[2,10,1,256]{3,0,2,1:T(2,128)S(1)} %get-tuple-element.53), channel_id=1, source_target_pairs={{0,1},{1,2},{2,3},{4,5},{5,6},{6,7},{8,9},{9,10},{10,11},{12,13},{... | collective-permute-start | bytes 61448 | tf_op jit(solution)/shard_map/ppermute | solution.py:19
  158.7 64.1 %collective-permute-start.18 = (f32[2,10,1,256]{3,0,2,1:T(2,128)S(1)}, f32[2,10,1,256]{3,0,2,1:T(2,128)S(1)}, u32[]{:S(2)}, u32[]{:S(2)}) collective-permute-start(f32[2,10,1,256]{3,0,2,1:T(2,128)S(1)} %get-tuple-element.50), channel_id=1, source_target_pairs={{1,0},{2,1},{3,2},{5,4},{6,5},{7,6},{9,8},{10,9},{11,10},{13,12},{... | collective-permute-start | bytes 61448 | tf_op jit(solution)/shard_map/ppermute | solution.py:20
  160.0 62.8 %collective-permute-start.19 = (f32[2,10,1,256]{3,0,2,1:T(2,128)S(1)}, f32[2,10,1,256]{3,0,2,1:T(2,128)S(1)}, u32[]{:S(2)}, u32[]{:S(2)}) collective-permute-start(f32[2,10,1,256]{3,0,2,1:T(2,128)S(1)} %get-tuple-element.51), channel_id=1, source_target_pairs={{0,1},{1,2},{2,3},{4,5},{5,6},{6,7},{8,9},{9,10},{10,11},{12,13},{... | collective-permute-start | bytes 61448 | tf_op jit(solution)/shard_map/ppermute | solution.py:19
  207.9 14.8 %copy-start.6 = (f32[1,1,2,64]{3,2,1,0:T(2,128)S(1)}, f32[1,1,2,64]{3,2,1,0:T(2,128)}, u32[]{:S(2)}) copy-start(f32[1,1,2,64]{3,2,1,0:T(2,128)} %param.17) | copy-start | bytes 1540
  207.9 14.8 %copy-start.7 = (s32[1,1,64]{2,1,0:T(1,128)S(1)}, s32[1,1,64]{2,1,0:T(1,128)}, u32[]{:S(2)}) copy-start(s32[1,1,64]{2,1,0:T(1,128)} %param.16) | copy-start | bytes 772
  216.3 79.2 %copy-start.8 = (s32[1,1,16]{2,1,0:T(1,128)S(1)}, s32[1,1,16]{2,1,0:T(1,128)}, u32[]{:S(2)}) copy-start(s32[1,1,16]{2,1,0:T(1,128)} %param.20) | copy-start | bytes 196
  225.5 187.8 %copy-start.5 = (s32[1,1,16]{2,1,0:T(1,128)S(1)}, s32[1,1,16]{2,1,0:T(1,128)}, u32[]{:S(2)}) copy-start(s32[1,1,16]{2,1,0:T(1,128)} %param.19) | copy-start | bytes 196
  225.5 6.1 %collective-permute-start.20 = (f32[2,1,16,256]{3,0,2,1:T(2,128)S(1)}, f32[2,1,16,256]{3,0,2,1:T(2,128)S(1)}, u32[]{:S(2)}, u32[]{:S(2)}) collective-permute-start(f32[2,1,16,256]{3,0,2,1:T(2,128)S(1)} %get-tuple-element.65), channel_id=1, source_target_pairs={{4,0},{8,4},{12,8},{16,12},{20,16},{24,20},{28,24},{5,1},{9,5},{13... | collective-permute-start | bytes 98312 | tf_op jit(solution)/shard_map/ppermute | solution.py:20
  226.8 6.4 %collective-permute-start.21 = (f32[2,1,16,256]{3,0,2,1:T(2,128)S(1)}, f32[2,1,16,256]{3,0,2,1:T(2,128)S(1)}, u32[]{:S(2)}, u32[]{:S(2)}) collective-permute-start(f32[2,1,16,256]{3,0,2,1:T(2,128)S(1)} %get-tuple-element.64), channel_id=1, source_target_pairs={{0,4},{4,8},{8,12},{12,16},{16,20},{20,24},{24,28},{1,5},{5,9},{9,... | collective-permute-start | bytes 98312 | tf_op jit(solution)/shard_map/ppermute | solution.py:19
  233.2 4.3 %collective-permute-start.22 = (f32[2,10,1,256]{3,0,2,1:T(2,128)S(1)}, f32[2,10,1,256]{3,0,2,1:T(2,128)S(1)}, u32[]{:S(2)}, u32[]{:S(2)}) collective-permute-start(f32[2,10,1,256]{3,0,2,1:T(2,128)S(1)} %get-tuple-element.48), channel_id=1, source_target_pairs={{1,0},{2,1},{3,2},{5,4},{6,5},{7,6},{9,8},{10,9},{11,10},{13,12},{... | collective-permute-start | bytes 61448 | tf_op jit(solution)/shard_map/ppermute | solution.py:20
  234.5 3.9 collective-permute-start.23
  283.4 6.1 %collective-permute-start.24 = (f32[2,1,16,256]{3,0,2,1:T(2,128)S(1)}, f32[2,1,16,256]{3,0,2,1:T(2,128)S(1)}, u32[]{:S(2)}, u32[]{:S(2)}) collective-permute-start(f32[2,1,16,256]{3,0,2,1:T(2,128)S(1)} %get-tuple-element.63), channel_id=1, source_target_pairs={{4,0},{8,4},{12,8},{16,12},{20,16},{24,20},{28,24},{5,1},{9,5},{13... | collective-permute-start | bytes 98312 | tf_op jit(solution)/shard_map/ppermute | solution.py:20
  284.7 6.4 %collective-permute-start.25 = (f32[2,1,16,256]{3,0,2,1:T(2,128)S(1)}, f32[2,1,16,256]{3,0,2,1:T(2,128)S(1)}, u32[]{:S(2)}, u32[]{:S(2)}) collective-permute-start(f32[2,1,16,256]{3,0,2,1:T(2,128)S(1)} %get-tuple-element.62), channel_id=1, source_target_pairs={{0,4},{4,8},{8,12},{12,16},{16,20},{20,24},{24,28},{1,5},{5,9},{9,... | collective-permute-start | bytes 98312 | tf_op jit(solution)/shard_map/ppermute | solution.py:19
  291.1 4.4 %collective-permute-start.26 = (f32[2,10,1,256]{3,0,2,1:T(2,128)S(1)}, f32[2,10,1,256]{3,0,2,1:T(2,128)S(1)}, u32[]{:S(2)}, u32[]{:S(2)}) collective-permute-start(f32[2,10,1,256]{3,0,2,1:T(2,128)S(1)} %get-tuple-element.46), channel_id=1, source_target_pairs={{1,0},{2,1},{3,2},{5,4},{6,5},{7,6},{9,8},{10,9},{11,10},{13,12},{... | collective-permute-start | bytes 61448 | tf_op jit(solution)/shard_map/ppermute | solution.py:20
  292.4 3.9 collective-permute-start.27
  341.6 6.1 %collective-permute-start.28 = (f32[2,1,16,256]{3,0,2,1:T(2,128)S(1)}, f32[2,1,16,256]{3,0,2,1:T(2,128)S(1)}, u32[]{:S(2)}, u32[]{:S(2)}) collective-permute-start(f32[2,1,16,256]{3,0,2,1:T(2,128)S(1)} %get-tuple-element.61), channel_id=1, source_target_pairs={{4,0},{8,4},{12,8},{16,12},{20,16},{24,20},{28,24},{5,1},{9,5},{13... | collective-permute-start | bytes 98312 | tf_op jit(solution)/shard_map/ppermute | solution.py:20
  342.9 6.4 %collective-permute-start.29 = (f32[2,1,16,256]{3,0,2,1:T(2,128)S(1)}, f32[2,1,16,256]{3,0,2,1:T(2,128)S(1)}, u32[]{:S(2)}, u32[]{:S(2)}) collective-permute-start(f32[2,1,16,256]{3,0,2,1:T(2,128)S(1)} %get-tuple-element.60), channel_id=1, source_target_pairs={{0,4},{4,8},{8,12},{12,16},{16,20},{20,24},{24,28},{1,5},{5,9},{9,... | collective-permute-start | bytes 98312 | tf_op jit(solution)/shard_map/ppermute | solution.py:19
  349.3 5.1 %collective-permute-start.30 = (f32[2,10,1,256]{3,0,2,1:T(2,128)S(1)}, f32[2,10,1,256]{3,0,2,1:T(2,128)S(1)}, u32[]{:S(2)}, u32[]{:S(2)}) collective-permute-start(f32[2,10,1,256]{3,0,2,1:T(2,128)S(1)} %get-tuple-element.44), channel_id=1, source_target_pairs={{1,0},{2,1},{3,2},{5,4},{6,5},{7,6},{9,8},{10,9},{11,10},{13,12},{... | collective-permute-start | bytes 61448 | tf_op jit(solution)/shard_map/ppermute | solution.py:20
  350.6 3.9 collective-permute-start.31
where the time goes:
time: 416 us; the launch traced here: 414 us
  blocking collectives  272 us (65%)
  starting transfers between devices  85.1 us (20%)
  local copies, waits for them, and re-layouts  20.7 us (5%)
  waiting for transfers between devices  12.6 us (3%)
  matrix products  11.9 us (3%)
  other arithmetic  10.6 us (3%)
    psum x6, blocking collectives, paired_sums(): lax.psum((local_inner(residual, residual), local_inner(residual, applied)...  265 us
    ppermute x16, starting transfers between devices, padded_2(): before = lax.ppermute(last, axis, up)  64.4 us
    ppermute x16, starting transfers between devices, padded_2(): after = lax.ppermute(initial, axis, down)  20.7 us
    ppermute x16, waiting for transfers between devices, padded_2(): before = lax.ppermute(last, axis, up)  12.6 us
    reshape x1, local copies, waits for them, and re-layouts, local(): flat_forward = forward.reshape(2, total_cells)  8.34 us
  transfers between devices with their start and end apart: 32, of which 12 were waited for; matrix products, arithmetic and copies ran while one was open for 7% of the time, Pallas kernels for 0%

commit v1 on v0

v1 whole, which is shorter than its diff:
```python
import jax
import jax.numpy as jnp
from jax import lax
from jax.sharding import PartitionSpec as P

LAPLACE_SHIFTS = (0.5, 2.0)
HX = 6
HC = 5
HA = 4
THETA = 6.0
BOTH = ("brick", "depth")


def spread(values):
    return values[:, None, None, None]


def exchange(to_low, to_high, axis):
    size = lax.axis_size(axis)
    odd = lax.axis_index(axis) % 2 == 1
    first = [(i, i ^ 1) for i in range(size) if (i ^ 1) < size]
    second = [(i, j) for i in range(size) for j in [((i + 1) ^ 1) - 1] if 0 <= j < size]
    got_first = lax.ppermute(jnp.where(odd, to_low, to_high), axis, first)
    got_second = lax.ppermute(jnp.where(odd, to_high, to_low), axis, second)
    from_low = jnp.where(odd, got_first, got_second)
    from_high = jnp.where(odd, got_second, got_first)
    return from_low, from_high


def widen(fields, lists, axis, dim):
    lows = [lax.slice_in_dim(a, 0, w, axis=dim).reshape(-1) for a, w in fields]
    highs = [lax.slice_in_dim(a, a.shape[dim] - w, a.shape[dim], axis=dim).reshape(-1) for a, w in fields]
    flat = lists.reshape(-1)
    from_low, from_high = exchange(jnp.concatenate(lows + [flat]), jnp.concatenate(highs + [flat]), axis)
    out = []
    at = 0
    for a, w in fields:
        shape = list(a.shape)
        shape[dim] = w
        count = 1
        for n in shape:
            count *= n
        before = from_low[at : at + count].reshape(shape)
        after = from_high[at : at + count].reshape(shape)
        out.append(jnp.concatenate([before, a, after], axis=dim))
        at += count
    n = flat.shape[0]
    low_list = from_low[at : at + n].reshape(lists.shape)
    high_list = from_high[at : at + n].reshape(lists.shape)
    return out, (low_list, lists, high_list)


def trim(a, w):
    return a[..., w : a.shape[-3] - w, w : a.shape[-2] - w, :]


def shifted(v, damping, inside):
    c = v[..., 1:-1, 1:-1, :]
    beside = v[..., 2:, 1:-1, :] + v[..., :-2, 1:-1, :] + v[..., 1:-1, 2:, :] + v[..., 1:-1, :-2, :]
    pad = [(0, 0)] * (v.ndim - 1) + [(1, 1)]
    lateral = jnp.pad(c, pad)
    beside = beside + lateral[..., 2:] + lateral[..., :-2]
    return inside * (damping * c - beside)


def coefficients(mu):
    a = [[mu[i + j + 1] + THETA * mu[i + j] for j in range(3)] for i in range(3)]

    def inverse(pivot, size):
        good = pivot > 1e-6 * size
        return jnp.where(good, 1.0 / jnp.where(good, pivot, 1.0), 0.0)

    i0 = inverse(a[0][0], 0.0)
    l10 = a[0][1] * i0
    l20 = a[0][2] * i0
    i1 = inverse(a[1][1] - l10 * a[0][1], a[1][1])
    e21 = a[1][2] - l10 * a[0][2]
    l21 = e21 * i1
    i2 = inverse(a[2][2] - l20 * a[0][2] - l21 * e21, a[2][2])
    y0 = mu[0]
    y1 = mu[1] - l10 * y0
    y2 = mu[2] - l20 * y0 - l21 * y1
    c2 = y2 * i2
    c1 = y1 * i1 - l21 * c2
    c0 = y0 * i0 - l10 * c1 - l20 * c2
    return c0, c1, c2


def local(
    conductivity,
    initial_field,
    adjoint_initial,
    src_cell,
    src_amp,
    rec_cell,
    observed,
    cov_blocks,
    cov_rows,
    cov_cols,
):
    size_x, size_z, size_y = conductivity.shape
    total_cells = size_x * size_z * size_y
    block_size = cov_blocks.shape[-1]
    blocks_here = total_cells // block_size
    shifts = jnp.array(LAPLACE_SHIFTS, jnp.float32)
    n_src = src_cell.shape[-1]
    n_rec = rec_cell.shape[-1]

    table = jnp.concatenate(
        [
            src_cell[0, 0][None].astype(jnp.float32),
            src_amp[0, 0],
            rec_cell[0, 0][None].astype(jnp.float32),
            jnp.ones((1, n_rec), jnp.float32),
            observed[0, 0],
        ]
    )
    fields = [(initial_field, HX), (conductivity[None], HC), (adjoint_initial, HA)]
    wide, lists_x = widen(fields, table, "brick", 1)
    wide = [(a, w) for a, (_, w) in zip(wide, fields)]
    stacked = jnp.stack(lists_x)
    (x0, cond, a0), lists = widen(wide, stacked, "depth", 2)
    lists = jnp.stack(lists)

    def inside_of(axis, size):
        at = lax.axis_index(axis) * size + jnp.arange(size + 2 * HX) - HX
        return ((at >= 0) & (at < lax.axis_size(axis) * size)).astype(jnp.float32)

    inside = inside_of("brick", size_x)[:, None, None] * inside_of("depth", size_z)[None, :, None]
    damping = spread(shifts) * cond

    def split3(v):
        one = lax.reduce_precision(v, 8, 7)
        two = lax.reduce_precision(v - one, 8, 7)
        three = v - one - two
        return jnp.stack([one, two, three]).astype(jnp.bfloat16)

    def place(cells, amounts, halo):
        idx = cells.astype(jnp.int32)
        off = jnp.arange(3) - 1
        ix = idx // (size_z * size_y) + halo + size_x * off[None, :, None]
        iz = (idx // size_y) % size_z + halo + size_z * off[:, None, None]
        iy = (idx % size_y).reshape(-1)
        nx = size_x + 2 * halo
        nz = size_z + 2 * halo
        ok = (ix >= 0) & (ix < nx) & (iz >= 0) & (iz < nz)
        row = jnp.where(ok, ix * nz + iz, -1).reshape(-1)
        rows = (jnp.arange(nx * nz)[:, None] == row[None, :]).astype(jnp.bfloat16)
        cols = iy[:, None] == jnp.arange(size_y)[None, :]
        parts = split3(amounts.reshape(amounts.shape[0], -1))
        right = jnp.where(cols[None, None], parts[..., None], 0)
        placed = jnp.einsum("rp,scpy->crsy", rows, right, preferred_element_type=jnp.float32)
        return jnp.sum(placed, axis=2).reshape(-1, nx, nz, size_y)

    source = place(lists[:, :, 0], jnp.moveaxis(lists[:, :, 1:3], 2, 0), HX - 1)
    placed = place(lists[:, :, 3], jnp.moveaxis(lists[:, :, 4:7], 2, 0), HA - 1)
    many = placed[0]
    obs = placed[1:3]

    def window(a, w):
        return trim(a, HX - w)

    def damp_at(w):
        return trim(damping, HC - w)

    v0 = source - window(inside, HX - 1) * THETA * trim(x0, 1) - shifted(x0, damp_at(5), window(inside, 5))
    v1 = shifted(v0, damp_at(4), window(inside, 4))
    v2 = shifted(v1, damp_at(3), window(inside, 3))
    v3 = shifted(trim(v2, 2), damp_at(0), 1.0)
    own = [trim(v0, 5), trim(v1, 4), trim(v2, 3), v3]

    u0 = many * trim(x0, 3) - obs - window(inside, 3) * THETA * trim(a0, 1) - shifted(a0, damp_at(3), window(inside, 3))
    u = jnp.stack([u0, many * trim(v0, 2), many * trim(v1, 1), many * v2], axis=1)
    w1 = shifted(u, damp_at(2)[:, None], window(inside, 2))
    w2 = shifted(w1, damp_at(1)[:, None], window(inside, 1))
    w3 = shifted(w2, damp_at(0)[:, None], 1.0)
    owna = [trim(u, 3), trim(w1, 2), trim(w2, 1), w3]

    def dot(a, b):
        return jnp.sum(a * b, axis=(-3, -2, -1))

    mu = jnp.stack([dot(own[j // 2], own[j - j // 2]) for j in range(6)])
    pairs = [(k, l) for k in range(4) for l in range(k, 4)]
    gram = jnp.stack(
        [
            jnp.stack([dot(owna[j // 2][:, k], owna[j - j // 2][:, l]) for k, l in pairs])
            for j in range(6)
        ]
    )
    sums = jnp.concatenate([mu.reshape(-1), gram.reshape(-1)])
    count = sums.shape[0]
    lanes = -(-count // 128) * 128
    sums = jnp.pad(sums, (0, lanes - count)).reshape(1, lanes)
    n_dev = lax.axis_size("brick") * lax.axis_size("depth")
    every = lax.all_to_all(jnp.broadcast_to(sums, (n_dev, lanes)), BOTH, 0, 0, tiled=True)
    sums = jnp.sum(every, axis=0)[:count]
    mu = sums[:12].reshape(6, 2)
    gram = sums[12:].reshape(6, len(pairs), 2)
    c = coefficients([mu[j] for j in range(6)])
    g = (1.0,) + c
    nu = []
    for j in range(6):
        total = 0.0
        for i, (k, l) in enumerate(pairs):
            total = total + (1.0 if k == l else 2.0) * g[k] * g[l] * gram[j, i]
        nu.append(total)
    d = coefficients(nu)
    forward = initial_field + sum(spread(c[k]) * own[k] for k in range(3))
    adjoint = adjoint_initial
    for j in range(3):
        level = owna[j][:, 0] + sum(spread(c[k]) * owna[j][:, k + 1] for k in range(3))
        adjoint = adjoint + spread(d[j]) * level

    gradient = (-jnp.sum(spread(shifts) * forward * adjoint, axis=0)).astype(jnp.bfloat16)
    grad_blocks = gradient.reshape(blocks_here, block_size)
    columns = cov_cols[0, 0]
    every_block = lax.all_gather(grad_blocks, "depth", axis=0, tiled=True)
    picked = jnp.take(every_block, columns, axis=0)
    terms = jnp.einsum("kij,kj->ki", cov_blocks[0, 0], picked, preferred_element_type=jnp.float32)
    row_table = (
        jnp.arange(blocks_here, dtype=jnp.int32)[:, None] == cov_rows[0, 0][None, :]
    ).astype(jnp.float32)
    added = jnp.dot(row_table, terms, precision=lax.Precision.HIGHEST)
    preconditioned = (grad_blocks.astype(jnp.float32) + added).reshape(size_x, size_z, size_y)
    return (forward, preconditioned)


def solution(mesh):
    return jax.shard_map(
        local,
        mesh=mesh,
        in_specs=(
            P("brick", "depth", None),
            P(None, "brick", "depth", None),
            P(None, "brick", "depth", None),
            P("brick", "depth", None),
            P("brick", "depth", None, None),
            P("brick", "depth", None),
            P("brick", "depth", None, None),
            P("brick", "depth", None, None, None),
            P("brick", "depth", None),
            P("brick", "depth", None),
        ),
        out_specs=(P(None, "brick", "depth", None), P("brick", "depth", None)),
        check_vma=False,
    )
```

time: 416 us -> 186 us (0.45)
  blocking collectives: 272 us -> 5.78 us
  starting transfers between devices: 85.1 us -> 21.3 us
  local copies, waits for them, and re-layouts: 20.7 us -> 77.9 us
  other arithmetic: 10.6 us -> 48.2 us
  waiting for transfers between devices: 12.6 us -> 20.5 us
    psum x6 -> x0, blocking collectives: 265 us -> none  [paired_sums(): lax.psum((local_inner(residual, residual), local_inner(residual, applied)...]
    ppermute x32 -> x4, starting transfers between devices: 85.1 us -> 7.26 us  [the longest x2 5.88 us: exchange(): got_first = lax.ppermute(jnp.where(odd, to_low, to_high), axis, first)]
    another operation x0 -> x73, local copies, waits for them, and re-layouts: none -> 49.5 us  [the longest x66 49 us: local(): jnp.stack([dot(owna[j // 2][:, k], owna[j - j // 2][:, l]) for k, l in pa...]
    mul x0 -> x12, other arithmetic: none -> 16.9 us  [the longest x3 11.6 us: shifted(): return inside * (damping * c - beside)]
    all_to_all x0 -> x1, starting transfers between devices: none -> 14 us  [local(): lax.all_to_all(jnp.broadcast_to(sums, (n_dev, lanes)), BOTH, 0, 0, tiled=...]
    slice x10 -> x39, local copies, waits for them, and re-layouts: 0.07 us -> 12.3 us  [the longest x6 4.77 us: trim(): return a[..., w:a.shape[-3] - w, w:a.shape[-2] - w, :]]
    all_to_all x0 -> x1, waiting for transfers between devices: none -> 6.65 us  [local(): lax.all_to_all(jnp.broadcast_to(sums, (n_dev, lanes)), BOTH, 0, 0, tiled=...]
    gather x2 -> x0, local copies, waits for them, and re-layouts: 6.45 us -> none  [local(): misfit = flat_forward[:, rec_cell[0, 0]] - observed[0, 0]]
  transfers between devices with their start and end apart: 32 -> 5, of which waited for: 12 -> 3; matrix products, arithmetic and copies ran while one was open for 7% -> 3% of each run, Pallas kernels for 0% -> 0%
where the time goes in v1:
time: 186 us; the launch traced here: 185 us
  local copies, waits for them, and re-layouts  77.9 us (42%)
  other arithmetic  48.2 us (26%)
  starting transfers between devices  21.3 us (11%)
  waiting for transfers between devices  20.5 us (11%)
  matrix products  9.03 us (5%)
  blocking collectives  5.78 us (3%)
  between operations  1.9 us (1%)
    another operation x66, local copies, waits for them, and re-layouts, local(): jnp.stack([dot(owna[j // 2][:, k], owna[j - j // 2][:, l]) for k, l in pa...  49 us
    all_to_all x1, starting transfers between devices, local(): lax.all_to_all(jnp.broadcast_to(sums, (n_dev, lanes)), BOTH, 0, 0, tiled=...  14 us
    ppermute x2, waiting for transfers between devices, exchange(): got_first = lax.ppermute(jnp.where(odd, to_low, to_high), axis, first)  13.9 us
    reduce_sum x4, other arithmetic, dot(): return jnp.sum(a * b, axis=(-3, -2, -1))  11.9 us
    mul x3, other arithmetic, shifted(): return inside * (damping * c - beside)  11.6 us
    all_to_all x1, waiting for transfers between devices, local(): lax.all_to_all(jnp.broadcast_to(sums, (n_dev, lanes)), BOTH, 0, 0, tiled=...  6.65 us
    ppermute x2, starting transfers between devices, exchange(): got_first = lax.ppermute(jnp.where(odd, to_low, to_high), axis, first)  5.88 us
    all_gather x1, blocking collectives, local(): every_block = lax.all_gather(grad_blocks, 'depth', axis=0, tiled=True)  5.78 us
  transfers between devices with their start and end apart: 5, of which 3 were waited for; matrix products, arithmetic and copies ran while one was open for 3% of the time, Pallas kernels for 0%

profile of v1, /device:TPU:0, one launch (start us, length us, event | category | flops | bytes accessed | tf_op | source)
XLA Modules:
  0.0 184.6 jit_solution(10583514477934943047)
XLA Ops:
  5.6 5.8 %collective-permute-start = (f32[102848]{0:T(1024)S(1)}, f32[102848]{0:T(1024)S(1)}, u32[]{:S(2)}, u32[]{:S(2)}) collective-permute-start(f32[102848]{0:T(1024)S(1)} %get-tuple-element.144), channel_id=1, source_target_pairs={{0,4},{4,0},{8,12},{12,8},{16,20},{20,16},{24,28},{28,24},{1,5},{5... | collective-permute-start | bytes 1234184 | tf_op jit(solution)/shard_map/ppermute | solution.py:23
  14.5 13.8 %collective-permute-done = f32[102848]{0:T(1024)S(1)} collective-permute-done((f32[102848]{0:T(1024)S(1)}, f32[102848]{0:T(1024)S(1)}, u32[]{:S(2)}, u32[]{:S(2)}) %collective-permute-start) | collective-permute-done | bytes 411424 | tf_op jit(solution)/shard_map/ppermute | solution.py:23
  35.5 1.5 fusion.15
  40.1 1.6 fusion.12
  43.5 4.2 %broadcast_multiply_fusion = (f32[2,18,26,256]{3,0,2,1:T(2,128)S(1)}, f32[2,18,26,256]{3,0,2,1:T(2,128)S(1)}) fusion(f32[18,26,256]{2,1,0:T(8,128)S(1)} %maximum_bitcast_fusion, f32[2]{0:T(128)S(1)} %copy-done.31, f32[2,18,26,256]{3,0,2,1:T(2,128)S(1)} %slice.942, f32[2,20,28,256]{3,0,2,1:T(2,128)S(1)} %pad_maximum_fusion.1, ...), kind=kLoop, calls=%fused_computation.98 | loop fusion | flops 2875392 | bytes 8150696 | tf_op jit(solution)/shard_map/mul | solution.py:130
  50.7 1.5 pad_maximum_fusion.2
  53.2 1.2 copy.250
  56.6 2.5 %fusion.39 = f32[2,16,24,256]{3,0,2,1:T(2,128)S(1)} fusion(f32[2,16,24,256]{3,0,2,1:T(2,128)S(1)} %slice.952, f32[2,18,26,256]{3,0,2,1:T(2,128)S(1)} %get-tuple-element.150, f32[2,18,26,256]{3,0,2,1:T(2,128)S(1)} %copy-done.3, f32[16,24]{1,0:T(8,128)S(1)} %copy-done.29), kind=kLoop, calls=%fused_computation.71 | loop fusion | flops 1572864 | bytes 5506560 | tf_op jit(solution)/shard_map/mul | solution.py:63
  60.7 4.2 %multiply_bitcast_fusion = (f32[2,1,14,22,256]{4,0,3,2,1:T(2,128)S(1)}, f32[2,14,22,256]{3,0,2,1:T(2,128)S(1)}, f32[2,1,14,22,256]{4,0,3,2,1:T(2,128)S(1)}) fusion(f32[14,22,256]{2,1,0:T(8,128)S(1)} %mul.973, f32[2,14,22,256]{3,0,2,1:T(2,128)S(1)} %get-tuple-element.145, f32[2,16,24,256]{3,0,2,1:T(2,128)S(1)} %fusion.39, ...), kind=kLoop, calls=%fused_computation.90 | loop fusion | flops 3469312 | bytes 10410400 | tf_op jit(solution)/shard_map/stack | solution.py:173
  65.0 1.4 pad_maximum_fusion
  67.4 5.3 %fusion.8 = f32[2,4,12,20,256]{4,0,3,2,1:T(2,128)S(1)} fusion(f32[2,4,12,20,256]{4,0,3,2,1:T(2,128)S(1)} %slice.988, f32[2,4,14,22,256]{4,0,3,2,1:T(2,128)S(1)} %pad_maximum_fusion, f32[2,12,20,256]{3,0,2,1:T(2,128)S(1)} %copy-done.13, f32[12,20]{1,0:T(8,128)S(1)} %copy-done.30), kind=kLoop, calls=%fused_computation.17 | loop fusion | flops 3932160 | bytes 12288960 | tf_op jit(solution)/shard_map/mul | solution.py:63
  72.7 2.9 %multiply_reduce_fusion.50 = (f32[2]{0:T(128)S(1)}, f32[2]{0:T(128)S(1)}, f32[2]{0:T(128)S(1)}, f32[2]{0:T(128)S(1)}, f32[2]{0:T(128)}, /*index=5*/f32[2]{0:T(12...) fusion(f32[2,1,14,22,256]{4,0,3,2,1:T(2,128)S(1)} %get-tuple-el, ...), kind=kLoop, calls=%fused_computation.179 | loop fusion | flops 2490330 | bytes 2097304 | tf_op jit(solution)/shard_map/reduce_sum | solution.py:180
  76.6 3.8 %fusion.21 = f32[2,4,10,18,256]{4,0,3,2,1:T(2,128)S(1)} fusion(f32[2,4,10,18,256]{4,0,3,2,1:T(2,128)S(1)} %slice.999, f32[2,4,12,20,256]{4,0,3,2,1:T(2,128)S(1)} %fusion.8, f32[2,10,18,256]{3,0,2,1:T(2,128)S(1)} %copy-done.15, f32[10,18]{1,0:T(8,128)S(1)} %copy-done.28), kind=kLoop, calls=%fused_computation.29 | loop fusion | flops 2949120 | bytes 9216720 | tf_op jit(solution)/shard_map/mul | solution.py:63
  80.4 3.4 %multiply_reduce_fusion.20 = (f32[2]{0:T(128)}, f32[2]{0:T(128)}, f32[2]{0:T(128)}, f32[2]{0:T(128)}, f32[2]{0:T(128)}, /*index=5*/f32[2]{0:T(128)}, f32[2]{0:T(...) fusion(f32[2,4,12,20,256]{4,0,3,2,1:T(2,128)S(1)} %fusion.8, ...), kind=kLoop, calls=%fused_computation.149 | loop fusion | flops 2752470 | bytes 2359464 | tf_op jit(solution)/shard_map/reduce_sum | solution.py:180
  83.8 1.6 slice.1008
  85.4 2.6 %multiply_reduce_fusion.61 = (f32[2]{0:T(128)S(1)}, f32[2]{0:T(128)S(1)}, f32[2]{0:T(128)S(1)}, f32[2]{0:T(128)S(1)}, f32[2]{0:T(128)S(1)}, /*index=5*/f32[2]{0:T(128)S(1)}, f32[2,8,16,256]{3,0,2,1:T(2,128)}) fusion(f32[2,16,24,256]{3,0,2,1:T(2,128)S(1)} %fusion.39, f32[2,14,22,256]{3,0,2,1:T(2,128)S(1)} %get-tuple-element.103, ...), kind=kLoop, calls=%fused_computation.190 | loop fusion | flops 1245172 | bytes 2621488 | tf_op jit(solution)/shard_map/reduce_sum | solution.py:180
  100.0 1.2 copy.278
  101.2 1.2 copy.279
  102.4 1.2 copy.280
  105.0 1.3 copy.268
  106.4 1.3 copy.267
  107.6 1.3 copy.269
  108.9 4.0 %fusion.28 = f32[2,4,8,16,256]{4,0,3,2,1:T(2,128)S(1)} fusion(f32[2,4,8,16,256]{4,0,3,2,1:T(2,128)} %slice.1008, f32[2,4,10,18,256]{4,0,3,2,1:T(2,128)S(1)} %fusion.21, f32[2,8,16,256]{3,0,2,1:T(2,128)} %get-tuple-element.136), kind=kLoop, calls=%fused_computation.44 | loop fusion | flops 1835008 | bytes 6553600 | tf_op jit(solution)/shard_map/sub | solution.py:63
  112.9 3.0 %multiply_reduce_fusion.1 = (f32[2]{0:T(128)}, f32[2]{0:T(128)}, f32[2]{0:T(128)}, f32[2]{0:T(128)}, f32[2]{0:T(128)}, /*index=5*/f32[2]{0:T(128)}, f32[2]{0:T(1...) fusion(f32[2,4,8,16,256]{4,0,3,2,1:T(2,128)S(1)} %fusion.28, ...), kind=kLoop, calls=%fused_computation.130 | loop fusion | flops 2621400 | bytes 2097312 | tf_op jit(solution)/shard_map/reduce_sum | solution.py:180
  116.0 1.3 copy.309
  117.2 1.3 copy.312
  118.5 1.3 copy.311
  119.8 1.3 copy.308
  121.1 1.2 copy.310
  122.4 1.2 copy.307
  123.6 1.3 copy.306
  124.9 1.3 copy.305
  126.2 1.3 copy.304
  127.5 1.3 copy.302
  128.8 1.3 copy.296
  130.1 1.3 copy.295
  131.4 1.2 copy.294
  132.6 1.3 copy.293
  133.9 1.3 copy.299
  135.2 1.3 copy.298
  136.5 1.3 copy.297
  137.7 1.2 copy.301
  139.0 1.3 copy.300
  145.2 14.0 %all-to-all-start = ((f32[32,1,256]{2,1,0:T(1,128)}), f32[32,1,256]{2,1,0:T(1,128)S(1)}, u32[]{:S(2)}, u32[]{:S(2)}) async-start(f32[32,1,256]{2,1,0:T(1,128)} %broadcast_in_dim.77), calls=%async_computation | async-start | bytes 65536 | tf_op jit(solution)/shard_map/all_to_all | solution.py:195
  159.8 6.7 %all-to-all-done = f32[32,1,256]{2,1,0:T(1,128)S(1)} async-done(((f32[32,1,256]{2,1,0:T(1,128)}), f32[32,1,256]{2,1,0:T(1,128)S(1)}, u32[]{:S(2)}, u32[]{:S(2)}) %all-to-all-start) | async-done | bytes 32800 | tf_op jit(solution)/shard_map/all_to_all | solution.py:195
  167.1 3.7 %multiply_reduce_fusion = (f32[8,16,256]{2,1,0:T(8,128)S(1)}, f32[2,8,16,256]{3,0,2,1:T(2,128)}) fusion(f32[2,8,16,256]{3,2,1,0:T(8,128)} %param.13, f32[2]{0:T(128)S(1)} %copy-done.32, f32[2]{0:T(128)S(1)} %get-tuple-element.90, f32[2]{0:T(128)S(1)} %get-tuple-element.89, f32[2]{0:T(128)S(1)} %get-tuple-element.88, f32[2]{0:T(128)S(1)} %get-tuple-element.94, ...), kind=kLoop, calls=%fused_computation.128 | loop fusion | flops 2129920 | bytes 4849720 | tf_op jit(solution)/shard_map/reduce_sum | solution.py:214
  170.8 5.8 %all_gather.3 = bf16[256,512]{1,0:T(8,128)(2,1)S(1)} all-gather(bf16[64,512]{1,0:T(8,128)(2,1)S(1)} %convert_element_type.125), channel_id=1, replica_groups=mesh['brick'=8,'depth'=4] {'depth'}, dimensions={0}, use_global_device_ids=true | all-gather | bytes 327680 | tf_op jit(solution)/shard_map/all_gather | solution.py:217
  177.3 5.7 %fusion = f32[16,1,512]{2,1,0:T(1,128)S(1)} fusion(bf16[1,1,16,512,512]{4,3,2,1,0:T(8,128)(2,1)} %param.18, bf16[16,512,1]{1,0,2:T(8,128)(2,1)S(1)} %select_bitcast_fusion), kind=kOutput, calls=%fused_computation.1 | convolution fusion | flops 8388608 | bytes 8437760 | tf_op jit(solution)/shard_map/kij,kj->ki/dot_general | solution.py:219
  (281 shorter events, 50.8 us)
Async XLA Ops:
  0.6 3.8 %copy-start.9 = (f32[2,8,16,256]{3,2,1,0:T(8,128)S(1)}, f32[2,8,16,256]{3,2,1,0:T(8,128)}, u32[]{:S(2)}) copy-start(f32[2,8,16,256]{3,2,1,0:T(8,128)} %param.12) | copy-start | bytes 786436
  4.6 8.3 %copy-start.35 = (s32[1,1,16]{2,1,0:T(1,128)S(1)}, s32[1,1,16]{2,1,0:T(1,128)}, u32[]{:S(2)}) copy-start(s32[1,1,16]{2,1,0:T(1,128)} %param.20) | copy-start | bytes 196
  4.9 9.6 %collective-permute-start.1 = (f32[102848]{0:T(1024)S(1)}, f32[102848]{0:T(1024)S(1)}, u32[]{:S(2)}, u32[]{:S(2)}) collective-permute-start(f32[102848]{0:T(1024)S(1)} %get-tuple-element.143), channel_id=1, source_target_pairs={{4,8},{8,4},{12,16},{16,12},{20,24},{24,20},{5,9},{9,5},{13,17},{1... | collective-permute-start | bytes 1234184 | tf_op jit(solution)/shard_map/ppermute | solution.py:24
  5.6 22.8 %collective-permute-start = (f32[102848]{0:T(1024)S(1)}, f32[102848]{0:T(1024)S(1)}, u32[]{:S(2)}, u32[]{:S(2)}) collective-permute-start(f32[102848]{0:T(1024)S(1)} %get-tuple-element.144), channel_id=1, source_target_pairs={{0,4},{4,0},{8,12},{12,8},{16,20},{20,16},{24,28},{28,24},{1,5},{5... | collective-permute-start | bytes 1234184 | tf_op jit(solution)/shard_map/ppermute | solution.py:23
  28.4 0.9 copy-start.16
  28.6 1.0 copy-start.12
  28.9 1.1 copy-start.18
  28.9 1.0 copy-start.20
  29.9 0.8 copy-start.14
  31.4 1.9 %collective-permute-start.2 = (f32[118592]{0:T(1024)S(1)}, f32[118592]{0:T(1024)S(1)}, u32[]{:S(2)}, u32[]{:S(2)}) collective-permute-start(f32[118592]{0:T(1024)S(1)} %get-tuple-element.139), channel_id=1, source_target_pairs={{0,1},{1,0},{2,3},{3,2},{4,5},{5,4},{6,7},{7,6},{8,9},{9,8},{10,11... | collective-permute-start | bytes 1423112 | tf_op jit(solution)/shard_map/ppermute | solution.py:23
  31.5 1.8 collective-permute-start.3
  42.2 0.9 copy-start.19
  42.2 0.9 copy-start.21
  42.2 1.0 copy-start.22
  42.2 1.0 copy-start.23
  42.8 0.7 copy-start.31
  43.5 6.2 %copy-start.25 = (f32[32768]{0:T(1024)S(1)}, f32[32768]{0:T(1024)}, u32[]{:S(2)}) copy-start(f32[32768]{0:T(1024)} %slice.974) | copy-start | bytes 393220
  47.7 1.1 copy-start.2
  47.7 11.4 %copy-start = (f32[2,18,26,256]{3,0,2,1:T(2,128)}, f32[2,18,26,256]{3,0,2,1:T(2,128)S(1)}, u32[]{:S(2)}) copy-start(f32[2,18,26,256]{3,0,2,1:T(2,128)S(1)} %get-tuple-element.150) | copy-start | bytes 2875396
  47.7 2.8 %copy-start.24 = (f32[32768]{0:T(1024)S(1)}, f32[32768]{0:T(1024)}, u32[]{:S(2)}) copy-start(f32[32768]{0:T(1024)} %slice.975) | copy-start | bytes 393220
  53.2 2.6 %copy-start.29 = (f32[16,24]{1,0:T(8,128)S(1)}, f32[16,24]{1,0:T(8,128)}, u32[]{:S(2)}) copy-start(f32[16,24]{1,0:T(8,128)} %slice_bitcast_fusion.19) | copy-start | bytes 4612
  55.4 1.2 copy-start.3
  59.1 26.3 %copy-start.1 = (f32[2,16,24,256]{3,0,2,1:T(2,128)}, f32[2,16,24,256]{3,0,2,1:T(2,128)S(1)}, u32[]{:S(2)}) copy-start(f32[2,16,24,256]{3,0,2,1:T(2,128)S(1)} %fusion.39) | copy-start | bytes 2359300
  59.1 1.4 copy-start.10
  59.1 1.5 copy-start.11
  59.1 1.5 copy-start.26
  59.1 1.5 copy-start.27
  59.8 12.8 %copy-start.8 = (f32[2,1,14,22,256]{4,0,3,2,1:T(2,128)}, f32[2,1,14,22,256]{4,0,3,2,1:T(2,128)S(1)}, u32[]{:S(2)}) copy-start(f32[2,1,14,22,256]{4,0,3,2,1:T(2,128)S(1)} %get-tuple-element.146) | copy-start | bytes 1892356
  59.8 20.6 %copy-start.5 = (f32[2,1,14,22,256]{4,0,3,2,1:T(2,128)}, f32[2,1,14,22,256]{4,0,3,2,1:T(2,128)S(1)}, u32[]{:S(2)}) copy-start(f32[2,1,14,22,256]{4,0,3,2,1:T(2,128)S(1)} %get-tuple-element.153) | copy-start | bytes 1892356
  64.9 7.7 %copy-start.6 = (f32[2,1,14,22,256]{4,0,3,2,1:T(2,128)}, f32[2,1,14,22,256]{4,0,3,2,1:T(2,128)S(1)}, u32[]{:S(2)}) copy-start(f32[2,1,14,22,256]{4,0,3,2,1:T(2,128)S(1)} %get-tuple-element.102) | copy-start | bytes 1892356
  64.9 7.7 %copy-start.7 = (f32[2,1,14,22,256]{4,0,3,2,1:T(2,128)}, f32[2,1,14,22,256]{4,0,3,2,1:T(2,128)S(1)}, u32[]{:S(2)}) copy-start(f32[2,1,14,22,256]{4,0,3,2,1:T(2,128)S(1)} %get-tuple-element.135) | copy-start | bytes 1892356
  65.0 20.4 %copy-start.4 = (f32[2,14,22,256]{3,0,2,1:T(2,128)}, f32[2,14,22,256]{3,0,2,1:T(2,128)S(1)}, u32[]{:S(2)}) copy-start(f32[2,14,22,256]{3,0,2,1:T(2,128)S(1)} %get-tuple-element.103) | copy-start | bytes 1892356
  66.3 1.0 copy-start.13
  66.3 1.0 copy-start.30
  75.6 1.0 copy-start.15
  75.6 1.0 copy-start.28
  112.9 54.2 %copy-start.32 = (f32[2]{0:T(128)S(1)}, f32[2]{0:T(128)}, u32[]{:S(2)}) copy-start(f32[2]{0:T(128)} %constant.162.clone) | copy-start | bytes 28
  145.2 21.3 %all-to-all-start = ((f32[32,1,256]{2,1,0:T(1,128)}), f32[32,1,256]{2,1,0:T(1,128)S(1)}, u32[]{:S(2)}, u32[]{:S(2)}) async-start(f32[32,1,256]{2,1,0:T(1,128)} %broadcast_in_dim.77), calls=%async_computation | async-start | bytes 65536 | tf_op jit(solution)/shard_map/all_to_all | solution.py:195
  167.1 10.1 %copy-start.34 = (pred[16]{0:T(512)(128)(4,1)S(1)}, pred[16]{0:T(512)(128)(4,1)}, u32[]{:S(2)}) copy-start(pred[16]{0:T(512)(128)(4,1)} %compare_and_fusion) | copy-start | bytes 52
  177.3 5.7 %copy-start.33 = (s32[1,1,16]{2,1,0:T(1,128)S(1)}, s32[1,1,16]{2,1,0:T(1,128)}, u32[]{:S(2)}) copy-start(s32[1,1,16]{2,1,0:T(1,128)} %param.19) | copy-start | bytes 196
  177.3 6.6 %copy-start.17 = (f32[2,8,16,256]{3,0,2,1:T(2,128)S(1)}, f32[2,8,16,256]{3,0,2,1:T(2,128)}, u32[]{:S(2)}) copy-start(f32[2,8,16,256]{3,0,2,1:T(2,128)} %get-tuple-element.87) | copy-start | bytes 786436

commit v2 on v1

--- a/solution.py
+++ b/solution.py
@@ -28,8 +28,8 @@
 
 
 def widen(fields, lists, axis, dim):
-    lows = [lax.slice_in_dim(a, 0, w, axis=dim).reshape(-1) for a, w in fields]
-    highs = [lax.slice_in_dim(a, a.shape[dim] - w, a.shape[dim], axis=dim).reshape(-1) for a, w in fields]
+    lows = [lax.slice_in_dim(a, 0, w, axis=dim).reshape(-1).astype(jnp.bfloat16) for a, w in fields]
+    highs = [lax.slice_in_dim(a, a.shape[dim] - w, a.shape[dim], axis=dim).reshape(-1).astype(jnp.bfloat16) for a, w in fields]
     flat = lists.reshape(-1)
     from_low, from_high = exchange(jnp.concatenate(lows + [flat]), jnp.concatenate(highs + [flat]), axis)
     out = []
@@ -40,8 +40,8 @@
         count = 1
         for n in shape:
             count *= n
-        before = from_low[at : at + count].reshape(shape)
-        after = from_high[at : at + count].reshape(shape)
+        before = from_low[at : at + count].reshape(shape).astype(jnp.float32)
+        after = from_high[at : at + count].reshape(shape).astype(jnp.float32)
         out.append(jnp.concatenate([before, a, after], axis=dim))
         at += count
     n = flat.shape[0]
@@ -106,13 +106,22 @@
     n_src = src_cell.shape[-1]
     n_rec = rec_cell.shape[-1]
 
+    def split3(v):
+        one = lax.reduce_precision(v, 8, 7)
+        two = lax.reduce_precision(v - one, 8, 7)
+        three = v - one - two
+        return jnp.stack([one, two, three]).astype(jnp.bfloat16)
+
+    def halves(cells):
+        return jnp.stack([cells // 256, cells % 256]).astype(jnp.bfloat16)
+
     table = jnp.concatenate(
         [
-            src_cell[0, 0][None].astype(jnp.float32),
-            src_amp[0, 0],
-            rec_cell[0, 0][None].astype(jnp.float32),
-            jnp.ones((1, n_rec), jnp.float32),
-            observed[0, 0],
+            halves(src_cell[0, 0]),
+            split3(src_amp[0, 0]).reshape(6, n_src),
+            halves(rec_cell[0, 0]),
+            jnp.ones((1, n_rec), jnp.bfloat16),
+            split3(observed[0, 0]).reshape(6, n_rec),
         ]
     )
     fields = [(initial_field, HX), (conductivity[None], HC), (adjoint_initial, HA)]
@@ -129,14 +138,15 @@
     inside = inside_of("brick", size_x)[:, None, None] * inside_of("depth", size_z)[None, :, None]
     damping = spread(shifts) * cond
 
-    def split3(v):
-        one = lax.reduce_precision(v, 8, 7)
-        two = lax.reduce_precision(v - one, 8, 7)
-        three = v - one - two
-        return jnp.stack([one, two, three]).astype(jnp.bfloat16)
+    def cells_of(pair):
+        return pair[:, :, 0].astype(jnp.int32) * 256 + pair[:, :, 1].astype(jnp.int32)
+
+    def joined(six):
+        three = six.astype(jnp.float32).reshape(six.shape[:2] + (3, 2, -1))
+        return jnp.moveaxis(three[:, :, 0] + three[:, :, 1] + three[:, :, 2], 2, 0)
 
     def place(cells, amounts, halo):
-        idx = cells.astype(jnp.int32)
+        idx = cells
         off = jnp.arange(3) - 1
         ix = idx // (size_z * size_y) + halo + size_x * off[None, :, None]
         iz = (idx // size_y) % size_z + halo + size_z * off[:, None, None]
@@ -152,8 +162,11 @@
         placed = jnp.einsum("rp,scpy->crsy", rows, right, preferred_element_type=jnp.float32)
         return jnp.sum(placed, axis=2).reshape(-1, nx, nz, size_y)
 
-    source = place(lists[:, :, 0], jnp.moveaxis(lists[:, :, 1:3], 2, 0), HX - 1)
-    placed = place(lists[:, :, 3], jnp.moveaxis(lists[:, :, 4:7], 2, 0), HA - 1)
+    source = place(cells_of(lists[:, :, 0:2]), joined(lists[:, :, 2:8]), HX - 1)
+    weights = lists[:, :, 10].astype(jnp.float32)[None]
+    placed = place(
+        cells_of(lists[:, :, 8:10]), jnp.concatenate([weights, joined(lists[:, :, 11:17])]), HA - 1
+    )
     many = placed[0]
     obs = placed[1:3]
 

time: 186 us -> 180 us (0.968)
  waiting for transfers between devices: 20.5 us -> 11.4 us
  other arithmetic: 48.2 us -> 53.3 us
  starting transfers between devices: 21.3 us -> 19.1 us
    ppermute x2, waiting for transfers between devices: 13.9 us -> 4.71 us  [exchange(): got_first = lax.ppermute(jnp.where(odd, to_low, to_high), axis, first)]
    another operation x2 -> x11, other arithmetic: 0.02 us -> 4.54 us
    reshape x20 -> x2, local copies, waits for them, and re-layouts: 3.23 us -> 0.02 us  [joined(): three = six.astype(jnp.float32).reshape(six.shape[:2] + (3, 2, -1))]
    convert_element_type x2 -> x22, local copies, waits for them, and re-layouts: 0.15 us -> 3.31 us  [the longest x8 1.24 us: widen(): after = from_high[at:at + count].reshape(shape).astype(jnp.float32)]
    unnamed x101 -> x97, local copies, waits for them, and re-layouts: 5.3 us -> 7.67 us
    all_to_all x1, starting transfers between devices: 14 us -> 11.8 us  [local(): lax.all_to_all(jnp.broadcast_to(sums, (n_dev, lanes)), BOTH, 0, 0, tiled=...]
    slice x5, local copies, waits for them, and re-layouts: 2.08 us -> 0.08 us  [widen(): lax.slice_in_dim(a, a.shape[dim] - w, a.shape[dim], axis=dim).reshape(-1)]
    slice x2, local copies, waits for them, and re-layouts: 1.2 us -> 3.12 us  [local(): obs = placed[1:3]]
where the time goes in v2:
time: 180 us; the launch traced here: 179 us
  local copies, waits for them, and re-layouts  78.2 us (43%)
  other arithmetic  53.3 us (30%)
  starting transfers between devices  19.1 us (11%)
  waiting for transfers between devices  11.4 us (6%)
  matrix products  9.03 us (5%)
  blocking collectives  5.78 us (3%)
  between operations  1.94 us (1%)
    another operation x66, local copies, waits for them, and re-layouts, local(): jnp.stack([dot(owna[j // 2][:, k], owna[j - j // 2][:, l]) for k, l in pa...  49.2 us
    mul x3, other arithmetic, shifted(): return inside * (damping * c - beside)  12.3 us
    reduce_sum x4, other arithmetic, dot(): return jnp.sum(a * b, axis=(-3, -2, -1))  12 us
    all_to_all x1, starting transfers between devices, local(): lax.all_to_all(jnp.broadcast_to(sums, (n_dev, lanes)), BOTH, 0, 0, tiled=...  11.8 us
    unnamed x97, local copies, waits for them, and re-layouts  7.67 us
    all_to_all x1, waiting for transfers between devices, local(): lax.all_to_all(jnp.broadcast_to(sums, (n_dev, lanes)), BOTH, 0, 0, tiled=...  6.65 us
    ppermute x2, starting transfers between devices, exchange(): got_first = lax.ppermute(jnp.where(odd, to_low, to_high), axis, first)  5.9 us
    all_gather x1, blocking collectives, local(): every_block = lax.all_gather(grad_blocks, 'depth', axis=0, tiled=True)  5.78 us
  transfers between devices with their start and end apart: 5, of which 3 were waited for; matrix products, arithmetic and copies ran while one was open for 3% of the time, Pallas kernels for 0%

profile of v2, /device:TPU:0, one launch (start us, length us, event | category | flops | bytes accessed | tf_op | source)
XLA Modules:
  0.0 178.7 jit_solution(8026162257615483285)
XLA Ops:
  6.2 5.8 %collective-permute-start = (bf16[103488]{0:T(1024)(128)(2,1)S(1)}, bf16[103488]{0:T(1024)(128)(2,1)S(1)}, u32[]{:S(2)}, u32[]{:S(2)}) collective-permute-start(bf16[103488]{0:T(1024)(128)(2,1)S(1)} %get-tuple-element.148), channel_id=1, source_target_pairs={{0,4},{4,0},{8,12},{12,8},{16,20},{20,16},{24,28},{28,24},{1,5},{5... | collective-permute-start | bytes 620936 | tf_op jit(solution)/shard_map/ppermute | solution.py:23
  16.0 4.3 %collective-permute-done = bf16[103488]{0:T(1024)(128)(2,1)S(1)} collective-permute-done((bf16[103488]{0:T(1024)(128)(2,1)S(1)}, bf16[103488]{0:T(1024)(128)(2,1)S(1)}, u32[]{:S(2)}, u32[]{:S(2)}) %collective-permute-start) | collective-permute-done | bytes 207008 | tf_op jit(solution)/shard_map/ppermute | solution.py:23
  31.4 1.5 fusion.15
  36.8 1.6 fusion.12
  40.2 4.2 %broadcast_multiply_fusion = (f32[2,18,26,256]{3,0,2,1:T(2,128)S(1)}, f32[2,18,26,256]{3,0,2,1:T(2,128)S(1)}) fusion(f32[18,26,256]{2,1,0:T(8,128)S(1)} %maximum_bitcast_fusion, f32[2]{0:T(128)S(1)} %copy-done.29, f32[2,18,26,256]{3,0,2,1:T(2,128)S(1)} %slice.1004, f32[2,20,28,256]{3,0,2,1:T(2,128)S(1)} %pad_maximum_fusion.1, ...), kind=kLoop, calls=%fused_computation.98 | loop fusion | flops 2875392 | bytes 8150696 | tf_op jit(solution)/shard_map/mul | solution.py:139
  47.2 1.1 slice.1041
  48.3 2.2 %copy.272 = f32[2,308,256]{2,0,1:T(2,128)} copy(f32[2,308,256]{2,1,0:T(8,128)} %slice.1038) | data formatting | bytes 1261568 | tf_op jit(solution)/shard_map/slice | solution.py:171
  51.8 3.2 %fusion.39 = f32[2,16,24,256]{3,0,2,1:T(2,128)S(1)} fusion(f32[2,16,24,256]{3,0,2,1:T(2,128)S(1)} %slice.1014, f32[2,18,26,256]{3,0,2,1:T(2,128)S(1)} %get-tuple-element.140, f32[2,18,26,256]{3,0,2,1:T(2,128)S(1)} %copy-done.3, f32[16,24]{1,0:T(8,128)} %slice_bitcast_fusion.19), kind=kLoop, calls=%fused_computation.71 | loop fusion | flops 1572864 | bytes 5506560 | tf_op jit(solution)/shard_map/mul | solution.py:63
  56.6 4.2 %multiply_bitcast_fusion = (f32[2,1,14,22,256]{4,0,3,2,1:T(2,128)S(1)}, f32[2,14,22,256]{3,0,2,1:T(2,128)S(1)}, f32[2,1,14,22,256]{4,0,3,2,1:T(2,128)S(1)}) fusion(f32[14,22,256]{2,1,0:T(8,128)S(1)} %mul.999, f32[2,14,22,256]{3,0,2,1:T(2,128)S(1)} %get-tuple-element.137, f32[2,16,24,256]{3,0,2,1:T(2,128)S(1)} %fusion.39, ...), kind=kLoop, calls=%fused_computation.90 | loop fusion | flops 3469312 | bytes 10410400 | tf_op jit(solution)/shard_map/stack | solution.py:186
  60.9 1.4 pad_maximum_fusion
  63.2 5.3 %fusion.8 = f32[2,4,12,20,256]{4,0,3,2,1:T(2,128)S(1)} fusion(f32[2,4,12,20,256]{4,0,3,2,1:T(2,128)S(1)} %slice.1053, f32[2,4,14,22,256]{4,0,3,2,1:T(2,128)S(1)} %pad_maximum_fusion, f32[2,12,20,256]{3,0,2,1:T(2,128)S(1)} %copy-done.13, f32[12,20]{1,0:T(8,128)S(1)} %copy-done.28), kind=kLoop, calls=%fused_computation.17 | loop fusion | flops 3932160 | bytes 12288960 | tf_op jit(solution)/shard_map/mul | solution.py:63
  68.6 2.9 %multiply_reduce_fusion.50 = (f32[2]{0:T(128)S(1)}, f32[2]{0:T(128)S(1)}, f32[2]{0:T(128)S(1)}, f32[2]{0:T(128)S(1)}, f32[2]{0:T(128)}, /*index=5*/f32[2]{0:T(12...) fusion(f32[2,1,14,22,256]{4,0,3,2,1:T(2,128)S(1)} %get-tuple-el, ...), kind=kLoop, calls=%fused_computation.179 | loop fusion | flops 2490330 | bytes 2097304 | tf_op jit(solution)/shard_map/reduce_sum | solution.py:193
  72.5 3.8 %fusion.21 = f32[2,4,10,18,256]{4,0,3,2,1:T(2,128)S(1)} fusion(f32[2,4,10,18,256]{4,0,3,2,1:T(2,128)S(1)} %slice.1064, f32[2,4,12,20,256]{4,0,3,2,1:T(2,128)S(1)} %fusion.8, f32[2,10,18,256]{3,0,2,1:T(2,128)S(1)} %copy-done.14, f32[10,18]{1,0:T(8,128)S(1)} %copy-done.27), kind=kLoop, calls=%fused_computation.29 | loop fusion | flops 2949120 | bytes 9216720 | tf_op jit(solution)/shard_map/mul | solution.py:63
  76.3 3.4 %multiply_reduce_fusion.20 = (f32[2]{0:T(128)}, f32[2]{0:T(128)}, f32[2]{0:T(128)}, f32[2]{0:T(128)}, f32[2]{0:T(128)}, /*index=5*/f32[2]{0:T(128)}, f32[2]{0:T(...) fusion(f32[2,4,12,20,256]{4,0,3,2,1:T(2,128)S(1)} %fusion.8, ...), kind=kLoop, calls=%fused_computation.149 | loop fusion | flops 2752470 | bytes 2359464 | tf_op jit(solution)/shard_map/reduce_sum | solution.py:193
  79.7 1.6 slice.1073
  81.3 2.6 %multiply_reduce_fusion.61 = (f32[2]{0:T(128)S(1)}, f32[2]{0:T(128)S(1)}, f32[2]{0:T(128)S(1)}, f32[2]{0:T(128)S(1)}, f32[2]{0:T(128)S(1)}, /*index=5*/f32[2]{0:T(128)S(1)}, f32[2,8,16,256]{3,0,2,1:T(2,128)}) fusion(f32[2,16,24,256]{3,0,2,1:T(2,128)S(1)} %fusion.39, f32[2,14,22,256]{3,0,2,1:T(2,128)S(1)} %get-tuple-element.103, ...), kind=kLoop, calls=%fused_computation.190 | loop fusion | flops 1245172 | bytes 2621488 | tf_op jit(solution)/shard_map/reduce_sum | solution.py:193
  95.8 1.3 copy.300
  97.1 1.2 copy.301
  98.4 1.2 copy.302
  101.0 1.2 copy.290
  102.2 1.2 copy.289
  103.5 1.3 copy.291
  104.8 4.0 %fusion.28 = f32[2,4,8,16,256]{4,0,3,2,1:T(2,128)S(1)} fusion(f32[2,4,8,16,256]{4,0,3,2,1:T(2,128)} %slice.1073, f32[2,4,10,18,256]{4,0,3,2,1:T(2,128)S(1)} %fusion.21, f32[2,8,16,256]{3,0,2,1:T(2,128)} %get-tuple-element.136), kind=kLoop, calls=%fused_computation.44 | loop fusion | flops 1835008 | bytes 6553600 | tf_op jit(solution)/shard_map/sub | solution.py:63
  108.9 3.1 %multiply_reduce_fusion.1 = (f32[2]{0:T(128)}, f32[2]{0:T(128)}, f32[2]{0:T(128)}, f32[2]{0:T(128)}, f32[2]{0:T(128)}, /*index=5*/f32[2]{0:T(128)}, f32[2]{0:T(1...) fusion(f32[2,4,8,16,256]{4,0,3,2,1:T(2,128)S(1)} %fusion.28, ...), kind=kLoop, calls=%fused_computation.130 | loop fusion | flops 2621400 | bytes 2097312 | tf_op jit(solution)/shard_map/reduce_sum | solution.py:193
  112.0 1.3 copy.331
  113.2 1.3 copy.334
  114.5 1.3 copy.333
  115.8 1.3 copy.330
  117.1 1.3 copy.332
  118.4 1.2 copy.329
  119.7 1.3 copy.328
  120.9 1.3 copy.327
  122.3 1.3 copy.326
  123.6 1.3 copy.324
  124.9 1.3 copy.318
  126.2 1.3 copy.317
  127.5 1.3 copy.316
  128.8 1.2 copy.315
  130.0 1.2 copy.321
  131.2 1.3 copy.320
  132.6 1.3 copy.319
  133.9 1.3 copy.323
  135.2 1.3 copy.322
  141.5 11.8 %all-to-all-start = ((f32[32,1,256]{2,1,0:T(1,128)}), f32[32,1,256]{2,1,0:T(1,128)S(1)}, u32[]{:S(2)}, u32[]{:S(2)}) async-start(f32[32,1,256]{2,1,0:T(1,128)} %broadcast_in_dim.77), calls=%async_computation | async-start | bytes 65536 | tf_op jit(solution)/shard_map/all_to_all | solution.py:208
  153.9 6.7 %all-to-all-done = f32[32,1,256]{2,1,0:T(1,128)S(1)} async-done(((f32[32,1,256]{2,1,0:T(1,128)}), f32[32,1,256]{2,1,0:T(1,128)S(1)}, u32[]{:S(2)}, u32[]{:S(2)}) %all-to-all-start) | async-done | bytes 32800 | tf_op jit(solution)/shard_map/all_to_all | solution.py:208
  161.2 3.7 %multiply_reduce_fusion = (f32[8,16,256]{2,1,0:T(8,128)S(1)}, f32[2,8,16,256]{3,0,2,1:T(2,128)}) fusion(f32[2,8,16,256]{3,2,1,0:T(8,128)} %param.13, f32[2]{0:T(128)S(1)} %copy-done.30, f32[2]{0:T(128)S(1)} %get-tuple-element.90, f32[2]{0:T(128)S(1)} %get-tuple-element.89, f32[2]{0:T(128)S(1)} %get-tuple-element.88, f32[2]{0:T(128)S(1)} %get-tuple-element.94, ...), kind=kLoop, calls=%fused_computation.128 | loop fusion | flops 2129920 | bytes 4849720 | tf_op jit(solution)/shard_map/reduce_sum | solution.py:227
  164.9 5.8 %all_gather.3 = bf16[256,512]{1,0:T(8,128)(2,1)S(1)} all-gather(bf16[64,512]{1,0:T(8,128)(2,1)S(1)} %convert_element_type.336), channel_id=1, replica_groups=mesh['brick'=8,'depth'=4] {'depth'}, dimensions={0}, use_global_device_ids=true | all-gather | bytes 327680 | tf_op jit(solution)/shard_map/all_gather | solution.py:230
  171.4 5.7 %fusion = f32[16,1,512]{2,1,0:T(1,128)S(1)} fusion(bf16[1,1,16,512,512]{4,3,2,1,0:T(8,128)(2,1)} %param.18, bf16[16,512,1]{1,0,2:T(8,128)(2,1)S(1)} %select_bitcast_fusion), kind=kOutput, calls=%fused_computation.1 | convolution fusion | flops 8388608 | bytes 8437760 | tf_op jit(solution)/shard_map/kij,kj->ki/dot_general | solution.py:232
  (294 shorter events, 54.8 us)
Async XLA Ops:
  0.6 4.7 %copy-start.11 = (f32[2,8,16,256]{3,2,1,0:T(8,128)S(1)}, f32[2,8,16,256]{3,2,1,0:T(8,128)}, u32[]{:S(2)}) copy-start(f32[2,8,16,256]{3,2,1,0:T(8,128)} %param.13) | copy-start | bytes 786436
  4.1 10.8 %copy-start.33 = (s32[1,1,16]{2,1,0:T(1,128)S(1)}, s32[1,1,16]{2,1,0:T(1,128)}, u32[]{:S(2)}) copy-start(s32[1,1,16]{2,1,0:T(1,128)} %param.20) | copy-start | bytes 196
  5.6 10.4 %collective-permute-start.1 = (bf16[103488]{0:T(1024)(128)(2,1)S(1)}, bf16[103488]{0:T(1024)(128)(2,1)S(1)}, u32[]{:S(2)}, u32[]{:S(2)}) collective-permute-start(bf16[103488]{0:T(1024)(128)(2,1)S(1)} %get-tuple-element.147), channel_id=1, source_target_pairs={{4,8},{8,4},{12,16},{16,12},{20,24},{24,20},{5,9},{9,5},{13,17},{1... | collective-permute-start | bytes 620936 | tf_op jit(solution)/shard_map/ppermute | solution.py:24
  6.2 14.0 %collective-permute-start = (bf16[103488]{0:T(1024)(128)(2,1)S(1)}, bf16[103488]{0:T(1024)(128)(2,1)S(1)}, u32[]{:S(2)}, u32[]{:S(2)}) collective-permute-start(bf16[103488]{0:T(1024)(128)(2,1)S(1)} %get-tuple-element.148), channel_id=1, source_target_pairs={{0,4},{4,0},{8,12},{12,8},{16,20},{20,16},{24,28},{28,24},{1,5},{5... | collective-permute-start | bytes 620936 | tf_op jit(solution)/shard_map/ppermute | solution.py:23
  12.1 8.9 %copy-start.16 = (f32[8,16,256]{2,1,0:T(8,128)S(1)}, f32[8,16,256]{2,1,0:T(8,128)}, u32[]{:S(2)}) copy-start(f32[8,16,256]{2,1,0:T(8,128)} %param.11) | copy-start | bytes 393220
  20.7 1.0 copy-start.18
  21.0 1.9 %copy-start.12 = (f32[2,8,16,256]{3,2,1,0:T(8,128)S(1)}, f32[2,8,16,256]{3,2,1,0:T(8,128)}, u32[]{:S(2)}) copy-start(f32[2,8,16,256]{3,2,1,0:T(8,128)} %param.12) | copy-start | bytes 786436
  22.9 1.1 copy-start.24
  27.4 1.6 collective-permute-start.2
  27.5 1.5 collective-permute-start.3
  38.9 0.9 copy-start.19
  39.0 0.9 copy-start.20
  39.0 1.0 copy-start.21
  39.5 0.7 copy-start.29
  40.2 6.2 %copy-start.23 = (f32[32768]{0:T(1024)S(1)}, f32[32768]{0:T(1024)}, u32[]{:S(2)}) copy-start(f32[32768]{0:T(1024)} %slice_convert_fusion.5) | copy-start | bytes 393220
  44.4 1.1 copy-start.2
  44.4 10.6 %copy-start = (f32[2,18,26,256]{3,0,2,1:T(2,128)}, f32[2,18,26,256]{3,0,2,1:T(2,128)S(1)}, u32[]{:S(2)}) copy-start(f32[2,18,26,256]{3,0,2,1:T(2,128)S(1)} %get-tuple-element.140) | copy-start | bytes 2875396
  44.4 2.2 %copy-start.22 = (f32[32768]{0:T(1024)S(1)}, f32[32768]{0:T(1024)}, u32[]{:S(2)}) copy-start(f32[32768]{0:T(1024)} %slice_convert_fusion.4) | copy-start | bytes 393220
  47.2 3.3 %copy-start.15 = (f32[1,308,256]{2,1,0:T(8,128)S(1)}, f32[1,308,256]{2,1,0:T(8,128)}, u32[]{:S(2)}) copy-start(f32[1,308,256]{2,1,0:T(8,128)} %slice.1036) | copy-start | bytes 946180
  50.6 1.2 copy-start.3
  55.0 26.3 %copy-start.1 = (f32[2,16,24,256]{3,0,2,1:T(2,128)}, f32[2,16,24,256]{3,0,2,1:T(2,128)S(1)}, u32[]{:S(2)}) copy-start(f32[2,16,24,256]{3,0,2,1:T(2,128)S(1)} %fusion.39) | copy-start | bytes 2359300
  55.0 1.4 copy-start.9
  55.0 1.5 copy-start.10
  55.0 1.5 copy-start.25
  55.0 1.5 copy-start.26
  55.7 12.8 %copy-start.8 = (f32[2,1,14,22,256]{4,0,3,2,1:T(2,128)}, f32[2,1,14,22,256]{4,0,3,2,1:T(2,128)S(1)}, u32[]{:S(2)}) copy-start(f32[2,1,14,22,256]{4,0,3,2,1:T(2,128)S(1)} %get-tuple-element.138) | copy-start | bytes 1892356
  55.7 20.6 %copy-start.5 = (f32[2,1,14,22,256]{4,0,3,2,1:T(2,128)}, f32[2,1,14,22,256]{4,0,3,2,1:T(2,128)S(1)}, u32[]{:S(2)}) copy-start(f32[2,1,14,22,256]{4,0,3,2,1:T(2,128)S(1)} %get-tuple-element.149) | copy-start | bytes 1892356
  60.8 7.7 %copy-start.6 = (f32[2,1,14,22,256]{4,0,3,2,1:T(2,128)}, f32[2,1,14,22,256]{4,0,3,2,1:T(2,128)S(1)}, u32[]{:S(2)}) copy-start(f32[2,1,14,22,256]{4,0,3,2,1:T(2,128)S(1)} %get-tuple-element.102) | copy-start | bytes 1892356
  60.8 7.7 %copy-start.7 = (f32[2,1,14,22,256]{4,0,3,2,1:T(2,128)}, f32[2,1,14,22,256]{4,0,3,2,1:T(2,128)S(1)}, u32[]{:S(2)}) copy-start(f32[2,1,14,22,256]{4,0,3,2,1:T(2,128)S(1)} %get-tuple-element.135) | copy-start | bytes 1892356
  60.8 20.5 %copy-start.4 = (f32[2,14,22,256]{3,0,2,1:T(2,128)}, f32[2,14,22,256]{3,0,2,1:T(2,128)S(1)}, u32[]{:S(2)}) copy-start(f32[2,14,22,256]{3,0,2,1:T(2,128)S(1)} %get-tuple-element.103) | copy-start | bytes 1892356
  62.2 1.0 copy-start.13
  62.2 1.0 copy-start.28
  71.5 1.0 copy-start.14
  71.5 1.0 copy-start.27
  108.9 52.3 %copy-start.30 = (f32[2]{0:T(128)S(1)}, f32[2]{0:T(128)}, u32[]{:S(2)}) copy-start(f32[2]{0:T(128)} %constant.193.clone) | copy-start | bytes 28
  141.5 19.1 %all-to-all-start = ((f32[32,1,256]{2,1,0:T(1,128)}), f32[32,1,256]{2,1,0:T(1,128)S(1)}, u32[]{:S(2)}, u32[]{:S(2)}) async-start(f32[32,1,256]{2,1,0:T(1,128)} %broadcast_in_dim.77), calls=%async_computation | async-start | bytes 65536 | tf_op jit(solution)/shard_map/all_to_all | solution.py:208
  161.2 10.1 %copy-start.32 = (pred[16]{0:T(512)(128)(4,1)S(1)}, pred[16]{0:T(512)(128)(4,1)}, u32[]{:S(2)}) copy-start(pred[16]{0:T(512)(128)(4,1)} %compare_and_fusion) | copy-start | bytes 52
  171.4 5.7 %copy-start.31 = (s32[1,1,16]{2,1,0:T(1,128)S(1)}, s32[1,1,16]{2,1,0:T(1,128)}, u32[]{:S(2)}) copy-start(s32[1,1,16]{2,1,0:T(1,128)} %param.19) | copy-start | bytes 196
  171.4 6.6 %copy-start.17 = (f32[2,8,16,256]{3,0,2,1:T(2,128)S(1)}, f32[2,8,16,256]{3,0,2,1:T(2,128)}, u32[]{:S(2)}) copy-start(f32[2,8,16,256]{3,0,2,1:T(2,128)} %get-tuple-element.87) | copy-start | bytes 786436

commit v3 on v2

v3 whole, which is shorter than its diff:
```python
import functools

import jax
import jax.numpy as jnp
from jax import lax
from jax.experimental import pallas as pl
from jax.experimental.pallas import tpu as pltpu
from jax.sharding import PartitionSpec as P

LAPLACE_SHIFTS = (0.5, 2.0)
HX = 6
HC = 5
HA = 4
HU = 3
ZP = 8
THETA = 6.0
BOTH = ("brick", "depth")
PAIRS = tuple((k, l) for k in range(4) for l in range(k, 4))
VMEM = pl.BlockSpec(memory_space=pltpu.VMEM)
SMEM = pl.BlockSpec(memory_space=pltpu.SMEM)
NT = (((1,), (1,)), ((), ()))


def exchange(to_low, to_high, axis):
    size = lax.axis_size(axis)
    odd = lax.axis_index(axis) % 2 == 1
    first = [(i, i ^ 1) for i in range(size) if (i ^ 1) < size]
    second = [(i, j) for i in range(size) for j in [((i + 1) ^ 1) - 1] if 0 <= j < size]
    got_first = lax.ppermute(jnp.where(odd, to_low, to_high), axis, first)
    got_second = lax.ppermute(jnp.where(odd, to_high, to_low), axis, second)
    from_low = jnp.where(odd, got_first, got_second)
    from_high = jnp.where(odd, got_second, got_first)
    return from_low, from_high


def widen(fields, lists, axis, dim):
    lows = [lax.slice_in_dim(a, 0, w, axis=dim).reshape(-1).astype(jnp.bfloat16) for a, w in fields]
    highs = [lax.slice_in_dim(a, a.shape[dim] - w, a.shape[dim], axis=dim).reshape(-1).astype(jnp.bfloat16) for a, w in fields]
    flat = lists.reshape(-1)
    from_low, from_high = exchange(jnp.concatenate(lows + [flat]), jnp.concatenate(highs + [flat]), axis)
    out = []
    at = 0
    for a, w in fields:
        shape = list(a.shape)
        shape[dim] = w
        count = 1
        for n in shape:
            count *= n
        before = from_low[at : at + count].reshape(shape).astype(jnp.float32)
        after = from_high[at : at + count].reshape(shape).astype(jnp.float32)
        out.append(jnp.concatenate([before, a, after], axis=dim))
        at += count
    n = flat.shape[0]
    low_list = from_low[at : at + n].reshape(lists.shape)
    high_list = from_high[at : at + n].reshape(lists.shape)
    return out, (low_list, lists, high_list)


def beside_z_y(c):
    rows, width = c.shape
    half = width // 2
    total = pltpu.roll(c, 1, 0) + pltpu.roll(c, rows - 1, 0)
    lane = lax.broadcasted_iota(jnp.int32, (rows, half), 1)
    first = lane == 0
    last = lane == half - 1
    a, b = c[:, :half], c[:, half:]
    ra, rb = pltpu.roll(a, 1, 1), pltpu.roll(b, 1, 1)
    la, lb = pltpu.roll(a, half - 1, 1), pltpu.roll(b, half - 1, 1)
    ya = jnp.where(first, 0.0, ra) + jnp.where(last, lb, la)
    yb = jnp.where(first, ra, rb) + jnp.where(last, 0.0, lb)
    return total + jnp.concatenate([ya, yb], axis=1)


def chain_kernel(size_x, size_z, edges, x0, cond, a0, lists, v_out, w_out, sums_out,
                 src, rec, v0, v1, v2, u, w1, w2, w3, acc):
    rows_z = x0.shape[-2]
    size_y = x0.shape[-1]
    n_list = lists.shape[-1] // 3
    each = n_list // 4
    own = slice(ZP, ZP + size_z)

    lane = lax.broadcasted_iota(jnp.int32, (1, n_list), 1)
    dx = jnp.where(lane < each, -1, jnp.where(lane < 2 * each, 0, 1))

    def place(t, q, weights, halo, dst):
        nx = size_x + 2 * halo
        at = slice(t * n_list, (t + 1) * n_list)
        hi = lists[q : q + 1, at] - 1.0
        lo = lists[q + 1 : q + 2, at].astype(jnp.int32)
        x = jnp.floor((hi + 0.5) * (1.0 / size_z))
        z = (hi - x * size_z).astype(jnp.int32)
        row_x = x.astype(jnp.int32) + halo + size_x * dx
        ok = (hi >= 0.0) & (row_x >= 0) & (row_x < nx)
        if t == 1:
            depth, z0 = size_z, ZP
            target = row_x * size_z + z
        elif t == 0:
            depth, z0 = ZP, 0
            target = row_x * ZP + z - (size_z - ZP)
            ok = ok & (z >= size_z - ZP)
        else:
            depth, z0 = ZP, ZP + size_z
            target = row_x * ZP + z
            ok = ok & (z < ZP)
        target = jnp.where(ok, target, -1)
        hit = lax.broadcasted_iota(jnp.int32, (nx * depth, n_list), 0) == target
        right = (lax.broadcasted_iota(jnp.int32, (size_y, n_list), 0) == lo).astype(jnp.float32).astype(jnp.bfloat16)
        for at_out, parts in weights:
            total = None
            for p in parts:
                amount = 1.0 if p is None else lists[p : p + 1, at]
                left = jnp.where(hit, amount, 0.0).astype(jnp.bfloat16)
                d = lax.dot_general(left, right, NT, preferred_element_type=jnp.float32)
                total = d if total is None else total + d
            dst[at_out, :, z0 : z0 + depth, :] = total.reshape(nx, depth, size_y)

    for t in range(3):
        place(t, 0, ((0, (2, 4, 6)), (1, (3, 5, 7))), HC, src)
        place(t, 8, ((0, (10, 12, 14)), (1, (11, 13, 15)), (2, (None,))), HU, rec)

    row = lax.broadcasted_iota(jnp.int32, (rows_z, size_y), 0)
    in_z = jnp.where(row < ZP, edges[2], jnp.where(row >= ZP + size_z, edges[3], 1.0))

    def mask(i, halo):
        return in_z * jnp.where(i < halo, edges[0], jnp.where(i >= halo + size_x, edges[1], 1.0))

    def apply(ref, idx, i, damp):
        c = ref[idx + (i,)]
        return damp * c - (ref[idx + (i - 1,)] + ref[idx + (i + 1,)] + beside_z_y(c))

    def loop(n, body):
        def step(i, carry):
            body(i)
            return carry
        lax.fori_loop(0, n, step, 0)

    def first(i):
        m = mask(i, HC)
        for f, s in enumerate(LAPLACE_SHIFTS):
            v0[f, i] = m * (src[f, i] - apply(x0, (f,), i + 1, s * cond[i] + THETA))

    loop(size_x + 2 * HC, first)

    def second(i):
        m = mask(i, 4)
        for f, s in enumerate(LAPLACE_SHIFTS):
            v1[f, i] = m * apply(v0, (f,), i + 1, s * cond[i + 1])

    loop(size_x + 8, second)

    def third(i):
        m = mask(i, 3)
        for f, s in enumerate(LAPLACE_SHIFTS):
            v2[f, i] = m * apply(v1, (f,), i + 1, s * cond[i + 2])

    loop(size_x + 6, third)

    def start(i):
        m = mask(i, HU)
        many = rec[2, i]
        for f, s in enumerate(LAPLACE_SHIFTS):
            u[0, f, i] = m * (many * x0[f, i + 3] - rec[f, i] - apply(a0, (f,), i + 1, s * cond[i + 2] + THETA))
            u[1, f, i] = many * v0[f, i + 2]
            u[2, f, i] = many * v1[f, i + 1]
            u[3, f, i] = many * v2[f, i]

    loop(size_x + 2 * HU, start)

    def level(src_ref, dst_ref, halo):
        def body(i):
            m = mask(i, halo)
            for f, s in enumerate(LAPLACE_SHIFTS):
                damp = s * cond[i + HC - halo]
                for k in range(4):
                    dst_ref[k, f, i] = m * apply(src_ref, (k, f), i + 1, damp)
        loop(size_x + 2 * halo, body)

    level(u, w1, 2)
    level(w1, w2, 1)

    def last(i):
        for f, s in enumerate(LAPLACE_SHIFTS):
            damp = s * cond[i + HC]
            for k in range(4):
                w3[k, f, i] = apply(w2, (k, f), i + 1, damp)[own]

    loop(size_x, last)

    def tiles(a):
        total = None
        for z in range(0, a.shape[0], 8):
            for y in range(0, a.shape[1], 128):
                t = a[z : z + 8, y : y + 128]
                total = t if total is None else total + t
        return total

    zero = jnp.zeros((8, 128), jnp.float32)
    for f, s in enumerate(LAPLACE_SHIFTS):
        def forward_sums(i, carry, f=f, s=s):
            p0 = v0[f, i + 5, own]
            p1 = v1[f, i + 4, own]
            p2 = v2[f, i + 3, own]
            p3 = apply(v2, (f,), i + 3, s * cond[i + 5])[own]
            v_out[0, f, i] = p0
            v_out[1, f, i] = p1
            v_out[2, f, i] = p2
            made = (p0 * p0, p0 * p1, p1 * p1, p1 * p2, p2 * p2, p2 * p3)
            return tuple(c + tiles(a) for c, a in zip(carry, made))
        done = lax.fori_loop(0, size_x, forward_sums, (zero,) * 6)
        for j in range(6):
            acc[j * 2 + f] = done[j]

    levels = ((u, 3, own), (w1, 2, own), (w2, 1, own), (w3, 0, slice(0, size_z)))
    for j in range(6):
        ra, oa, za = levels[j // 2]
        rb, ob, zb = levels[j - j // 2]
        for f in range(2):
            def pair_sums(i, carry, f=f, j=j):
                a = [ra[k, f, i + oa, za] for k in range(4)]
                b = a if j % 2 == 0 else [rb[k, f, i + ob, zb] for k in range(4)]
                if j % 2 == 0:
                    for k in range(4):
                        w_out[j // 2, k, f, i] = a[k]
                return tuple(c + tiles(a[k] * b[l]) for c, (k, l) in zip(carry, PAIRS))
            done = lax.fori_loop(0, size_x, pair_sums, (zero,) * len(PAIRS))
            for n in range(len(PAIRS)):
                acc[12 + (j * len(PAIRS) + n) * 2 + f] = done[n]

    count = acc.shape[0]
    for n in range(12 + 12 * len(PAIRS), count):
        acc[n] = zero
    by_lane = jnp.sum(acc[...], axis=1)
    ones = jnp.ones((8, 128), jnp.float32)
    out = lax.dot_general(ones, by_lane, NT, precision=lax.Precision.HIGHEST, preferred_element_type=jnp.float32)
    sums_out[...] = jnp.broadcast_to(out[0:1][None], sums_out.shape)


def chain(edges, x0, cond, a0, lists, size_x, size_z, n_dev):
    f, _, rows_z, size_y = x0.shape
    f32 = jnp.float32
    slab = (rows_z, size_y)
    outs = (
        jax.ShapeDtypeStruct((3, 2, size_x, size_z, size_y), f32),
        jax.ShapeDtypeStruct((3, 4, 2, size_x, size_z, size_y), f32),
        jax.ShapeDtypeStruct((n_dev, 1, 256), f32),
    )
    scratch = [
        pltpu.VMEM((2, size_x + 2 * HC) + slab, f32),
        pltpu.VMEM((3, size_x + 2 * HU) + slab, f32),
        pltpu.VMEM((2, size_x + 2 * HC) + slab, f32),
        pltpu.VMEM((2, size_x + 8) + slab, f32),
        pltpu.VMEM((2, size_x + 6) + slab, f32),
        pltpu.VMEM((4, 2, size_x + 6) + slab, f32),
        pltpu.VMEM((4, 2, size_x + 4) + slab, f32),
        pltpu.VMEM((4, 2, size_x + 2) + slab, f32),
        pltpu.VMEM((4, 2, size_x, size_z, size_y), f32),
        pltpu.VMEM((256, 8, 128), f32),
    ]
    return pl.pallas_call(
        functools.partial(chain_kernel, size_x, size_z),
        out_shape=outs,
        in_specs=[SMEM, VMEM, VMEM, VMEM, VMEM],
        out_specs=(VMEM, VMEM, VMEM),
        scratch_shapes=scratch,
        name="chain",
    )(edges, x0, cond, a0, lists)


def combine_kernel(coef, x0, a0, v, w, forward, gradient):
    total = None
    for f, s in enumerate(LAPLACE_SHIFTS):
        field = x0[f]
        for k in range(3):
            field = field + coef[f, k] * v[k, f]
        other = a0[f]
        for j in range(3):
            for k in range(4):
                other = other + coef[f, 3 + 4 * j + k] * w[j, k, f]
        forward[f] = field
        part = s * field * other
        total = part if total is None else total + part
    gradient[...] = (-total).reshape(gradient.shape).astype(gradient.dtype)


def combine(coef, x0, a0, v, w):
    _, size_x, size_z, size_y = x0.shape
    return pl.pallas_call(
        combine_kernel,
        out_shape=(
            jax.ShapeDtypeStruct(x0.shape, jnp.float32),
            jax.ShapeDtypeStruct((size_x * size_z, size_y), jnp.bfloat16),
        ),
        in_specs=[SMEM, VMEM, VMEM, VMEM, VMEM],
        out_specs=(VMEM, VMEM),
        name="combine",
    )(coef, x0, a0, v, w)


def covariance_kernel(rows, cols, every, own, blocks, out, wide):
    n_dev, n_rows, width = every.shape
    per = blocks.shape[-1] // width
    for d in range(n_dev):
        wide[d * n_rows : (d + 1) * n_rows, :] = every[d].astype(jnp.float32)
    out[...] = own[...].astype(jnp.float32)
    for k in range(blocks.shape[0]):
        picked = jnp.concatenate([wide[pl.ds(cols[k] * per + i, 1), :] for i in range(per)], axis=1)
        picked = jnp.broadcast_to(picked, (16, picked.shape[1])).astype(jnp.bfloat16)
        term = lax.dot_general(picked, blocks[k], NT, preferred_element_type=jnp.float32)[0:1]
        for i in range(per):
            at = pl.ds(rows[k] * per + i, 1)
            out[at, :] = out[at, :] + term[:, i * width : (i + 1) * width]


def covariance(rows, cols, every, own, blocks):
    n_dev, n_rows, width = every.shape
    return pl.pallas_call(
        covariance_kernel,
        out_shape=jax.ShapeDtypeStruct((n_rows, width), jnp.float32),
        in_specs=[SMEM, SMEM, VMEM, VMEM, VMEM],
        out_specs=VMEM,
        scratch_shapes=[pltpu.VMEM((n_dev * n_rows, width), jnp.float32)],
        name="covariance",
    )(rows, cols, every, own, blocks)


def coefficients(mu):
    a = [[mu[i + j + 1] + THETA * mu[i + j] for j in range(3)] for i in range(3)]

    def inverse(pivot, size):
        good = pivot > 1e-6 * size
        return jnp.where(good, 1.0 / jnp.where(good, pivot, 1.0), 0.0)

    i0 = inverse(a[0][0], 0.0)
    l10 = a[0][1] * i0
    l20 = a[0][2] * i0
    i1 = inverse(a[1][1] - l10 * a[0][1], a[1][1])
    e21 = a[1][2] - l10 * a[0][2]
    l21 = e21 * i1
    i2 = inverse(a[2][2] - l20 * a[0][2] - l21 * e21, a[2][2])
    y0 = mu[0]
    y1 = mu[1] - l10 * y0
    y2 = mu[2] - l20 * y0 - l21 * y1
    c2 = y2 * i2
    c1 = y1 * i1 - l21 * c2
    c0 = y0 * i0 - l10 * c1 - l20 * c2
    return c0, c1, c2


def local(
    conductivity,
    initial_field,
    adjoint_initial,
    src_cell,
    src_amp,
    rec_cell,
    observed,
    cov_blocks,
    cov_rows,
    cov_cols,
):
    size_x, size_z, size_y = conductivity.shape
    n_src = src_cell.shape[-1]
    n_rec = rec_cell.shape[-1]

    def split3(v):
        one = lax.reduce_precision(v, 8, 7)
        two = lax.reduce_precision(v - one, 8, 7)
        three = v - one - two
        return jnp.stack([one, two, three]).astype(jnp.bfloat16)

    def halves(cells):
        return jnp.stack([cells // size_y + 1, cells % size_y]).astype(jnp.bfloat16)

    table = jnp.concatenate(
        [
            halves(src_cell[0, 0]),
            split3(src_amp[0, 0]).reshape(6, n_src),
            halves(rec_cell[0, 0]),
            split3(observed[0, 0]).reshape(6, n_rec),
        ]
    )
    fields = [(initial_field, HX), (conductivity[None], HC), (adjoint_initial, HA)]
    wide, lists_x = widen(fields, table, "brick", 1)
    wide = [(a, ZP) for a in wide]
    stacked = jnp.concatenate(lists_x + (jnp.zeros_like(table),), axis=1)
    (x0, cond, a0), lists = widen(wide, stacked, "depth", 2)
    lists = jnp.concatenate(lists, axis=1).astype(jnp.float32)

    def edge(axis):
        at = lax.axis_index(axis)
        return [at > 0, at < lax.axis_size(axis) - 1]

    edges = jnp.stack(edge("brick") + edge("depth")).astype(jnp.float32)
    n_dev = lax.axis_size("brick") * lax.axis_size("depth")
    own, owna, sums = chain(edges, x0, cond[0], a0, lists, size_x, size_z, n_dev)
    every = lax.all_to_all(sums, BOTH, 0, 0, tiled=True)
    sums = jnp.sum(every, axis=(0, 1))
    mu = sums[:12].reshape(6, 2)
    gram = sums[12 : 12 + 12 * len(PAIRS)].reshape(6, len(PAIRS), 2)
    c = coefficients([mu[j] for j in range(6)])
    g = (jnp.ones_like(c[0]),) + c
    nu = []
    for j in range(6):
        total = 0.0
        for i, (k, l) in enumerate(PAIRS):
            total = total + (1.0 if k == l else 2.0) * g[k] * g[l] * gram[j, i]
        nu.append(total)
    d = coefficients(nu)
    coef = jnp.stack(list(c) + [d[j] * g[k] for j in range(3) for k in range(4)], axis=1)
    forward, gradient = combine(coef, initial_field, adjoint_initial, own, owna)
    every_block = lax.all_gather(gradient, "depth", axis=0, tiled=False)
    out = covariance(cov_rows[0, 0], cov_cols[0, 0], every_block, gradient, cov_blocks[0, 0])
    return (forward, out.reshape(size_x, size_z, size_y))


def solution(mesh):
    return jax.shard_map(
        local,
        mesh=mesh,
        in_specs=(
            P("brick", "depth", None),
            P(None, "brick", "depth", None),
            P(None, "brick", "depth", None),
            P("brick", "depth", None),
            P("brick", "depth", None, None),
            P("brick", "depth", None),
            P("brick", "depth", None, None),
            P("brick", "depth", None, None, None),
            P("brick", "depth", None),
            P("brick", "depth", None),
        ),
        out_specs=(P(None, "brick", "depth", None), P("brick", "depth", None)),
        check_vma=False,
    )
```

time: 180 us -> 90.3 us (0.50)
  local copies, waits for them, and re-layouts: 78.2 us -> 5.48 us
  other arithmetic: 53.3 us -> 10.1 us
  Pallas kernels: 0 us -> 30.6 us
  blocking collectives: 5.78 us -> 26.6 us
  starting transfers between devices: 19.1 us -> 7.18 us
  matrix products: 9.03 us -> 0 us
  waiting for transfers between devices: 11.4 us -> 8.63 us
    another operation x73 -> x16, local copies, waits for them, and re-layouts: 49.7 us -> 2.05 us  [local(): jnp.stack(list(c) + [d[j] * g[k] for j in range(3) for k in range(4)], ax...]
    pallas_call x0 -> x3, Pallas kernels: none -> 30.6 us  [the longest x1 20.9 us: chain(): pl.pallas_call(functools.partial(chain_kernel, size_x, size_z), out_shape...]
    all_to_all x0 -> x1, blocking collectives: none -> 20.1 us  [local(): every = lax.all_to_all(sums, BOTH, 0, 0, tiled=True)]
    mul x12 -> x0, other arithmetic: 17.6 us -> none  [the longest x3 12.3 us: shifted(): return inside * (damping * c - beside)]
    reduce_sum x6 -> x1, other arithmetic: 15.7 us -> 0.05 us  [local(): sums = jnp.sum(every, axis=(0, 1))]
    all_to_all x1 -> x0, starting transfers between devices: 11.8 us -> none  [local(): lax.all_to_all(jnp.broadcast_to(sums, (n_dev, lanes)), BOTH, 0, 0, tiled=...]
    slice x13 -> x1, local copies, waits for them, and re-layouts: 10.4 us -> 0.07 us  [local(): gram = sums[12:12 + 12 * len(PAIRS)].reshape(6, len(PAIRS), 2)]
    dot_general x4 -> x0, matrix products: 9.03 us -> none  [the longest x1 5.68 us: local(): jnp.einsum('kij,kj->ki', cov_blocks[0, 0], picked, preferred_element_type...]
  transfers between devices with their start and end apart: 5 -> 4, of which waited for: 3 -> 2; matrix products, arithmetic and copies ran while one was open for 3% -> 1% of each run, Pallas kernels for 0% -> 0%
where the time goes in v3:
time: 90.3 us; the launch traced here: 89.9 us
  Pallas kernels  30.6 us (34%)
  blocking collectives  26.6 us (29%)
  other arithmetic  10.1 us (11%)
  waiting for transfers between devices  8.63 us (10%)
  starting transfers between devices  7.18 us (8%)
  local copies, waits for them, and re-layouts  5.48 us (6%)
  between operations  1.33 us (1%)
    pallas_call x1, Pallas kernels, chain(): pl.pallas_call(functools.partial(chain_kernel, size_x, size_z), out_shape...  20.9 us
    all_to_all x1, blocking collectives, local(): every = lax.all_to_all(sums, BOTH, 0, 0, tiled=True)  20.1 us
    ppermute x2, waiting for transfers between devices, exchange(): got_first = lax.ppermute(jnp.where(odd, to_low, to_high), axis, first)  8.63 us
    pallas_call x1, Pallas kernels, covariance(): pl.pallas_call(covariance_kernel, out_shape=jax.ShapeDtypeStruct((n_rows,...  6.48 us
    all_gather x1, blocking collectives, local(): every_block = lax.all_gather(gradient, 'depth', axis=0, tiled=False)  6.47 us
    ppermute x2, starting transfers between devices, exchange(): got_first = lax.ppermute(jnp.where(odd, to_low, to_high), axis, first)  5.83 us
    another operation x9, other arithmetic  4.1 us
    pallas_call x1, Pallas kernels, combine(): pl.pallas_call(combine_kernel, out_shape=(jax.ShapeDtypeStruct(x0.shape,...  3.23 us
  transfers between devices with their start and end apart: 4, of which 2 were waited for; matrix products, arithmetic and copies ran while one was open for 1% of the time, Pallas kernels for 0%

profile of v3, /device:TPU:0, one launch (start us, length us, event | category | flops | bytes accessed | tf_op | source)
XLA Modules:
  0.0 89.9 jit_solution(652684409726111861)
XLA Ops:
  0.7 0.7 reduce-precision_convert_fusion.3
  1.4 0.7 reduce-precision_convert_fusion.1
  2.1 0.7 fusion.4
  3.0 0.9 %bitcast_convert_fusion = bf16[1,8,16,256]{3,2,1,0:T(8,128)(2,1)S(1)} fusion(f32[8,16,256]{2,1,0:T(8,128)} %param.10), kind=kLoop, calls=%fused_computation.285 | loop fusion | flops 32768 | bytes 196608 | tf_op jit(solution)/shard_map/convert.32
  4.0 1.0 %convert.66 = bf16[2,8,16,256]{3,2,1,0:T(8,128)(2,1)S(1)} convert(f32[2,8,16,256]{3,2,1,0:T(8,128)} %x0.1) | non-fusion elementwise | flops 65536 | bytes 393216 | tf_op jit(solution)/shard_map/convert.33
  5.5 0.7 collective-permute-start.1
  6.1 5.8 %collective-permute-start = (bf16[103424]{0:T(1024)(128)(2,1)S(1)}, bf16[103424]{0:T(1024)(128)(2,1)S(1)}, u32[]{:S(2)}, u32[]{:S(2)}) collective-permute-start(bf16[103424]{0:T(1024)(128)(2,1)S(1)} %get-tuple-element.36), channel_id=1, source_target_pairs={{0,4},{4,0},{8,12},{12,8},{16,20},{20,16},{24,28},{28,24},{1,5},{5... | collective-permute-start | bytes 620552 | tf_op jit(solution)/shard_map/ppermute | solution.py:29
  12.0 8.1 %collective-permute-done = bf16[103424]{0:T(1024)(128)(2,1)S(1)} collective-permute-done((bf16[103424]{0:T(1024)(128)(2,1)S(1)}, bf16[103424]{0:T(1024)(128)(2,1)S(1)}, u32[]{:S(2)}, u32[]{:S(2)}) %collective-permute-start) | collective-permute-done | bytes 206880 | tf_op jit(solution)/shard_map/ppermute | solution.py:29
  20.8 0.3 copy-done.2
  21.4 0.1 copy.50
  21.5 0.1 copy.54
  21.6 0.6 copy-done
  22.4 0.1 copy.48
  22.5 0.1 copy.52
  22.7 0.8 broadcast_select_fusion.3
  23.6 0.7 collective-permute-start.3
  24.3 0.7 add_convert_fusion.edges
  24.9 0.5 collective-permute-done.2
  25.7 0.1 concatenate.53
  25.8 0.6 convert_element_type.195.lists
  26.5 0.1 reshape.469
  26.7 0.1 reshape.470
  26.9 0.9 maximum_bitcast_fusion.cond
  27.8 1.2 %pad_maximum_fusion.x0 = f32[2,20,32,256]{3,2,1,0:T(8,128)} fusion(f32[2,20,8,256]{3,2,1,0:T(8,128)S(1)} %reshape.470, f32[2,20,16,256]{3,2,1,0:T(8,128)S(1)} %constant_dynamic-update-slice_fusion.2, f32[2,20,8,256]{3,2,1,0:T(8,128)S(1)} %reshape.469), kind=kLoop, calls=%fused_computation | loop fusion | flops 655360 | bytes 2621440 | tf_op jit(solution)/shard_map/concatenate | solution.py:51
  29.0 1.1 %pad_maximum_fusion.1.a0 = f32[2,16,32,256]{3,2,1,0:T(8,128)} fusion(f32[2,16,8,256]{3,2,1,0:T(8,128)S(1)} %reshape.474, f32[2,16,16,256]{3,2,1,0:T(8,128)S(1)} %constant_dynamic-update-slice_fusion.5, f32[2,16,8,256]{3,2,1,0:T(8,128)S(1)} %reshape.473), kind=kLoop, calls=%fused_computation.1 | loop fusion | flops 524288 | bytes 2097152 | tf_op jit(solution)/shard_map/concatenate | solution.py:51
  30.1 20.9 %chain.1 = (f32[3,2,8,16,256]{4,3,2,1,0:T(8,128)}, f32[3,4,2,8,16,256]{5,4,3,2,1,0:T(8,128)}, f32[32,1,256]{2,1,0:T(1,128)}) custom-call(f32[4]{0:T(128)} %add_convert_fusion.edges, f32[2,20,32,256]{3,2,1,0:T(8,128)} %pad_maximum_fusion.x0, f32[18,32,256]{2,1,0:T(8,128)} %maximum_bitcast_fusion.cond, f32[2,16,32,256]{3,2,1,0:T(8,128)} %pad_maximum_fusion.1.a0, ...), custom_call_target="tpu_custom_call" | custom-call | tf_op jit(solution)/shard_map/chain/pallas_call | solution.py:259
  51.0 20.1 %all_to_all.5 = f32[32,1,256]{2,1,0:T(1,128)S(1)} all-to-all(f32[32,1,256]{2,1,0:T(1,128)} %get-tuple-element.7), channel_id=1, replica_groups=mesh['brick'=8,'depth'=4] {'brick','depth'}, dimensions={0} | all-to-all | bytes 65536 | tf_op jit(solution)/shard_map/all_to_all | solution.py:396
  71.3 0.1 reshape.461
  71.4 0.1 multiply_bitcast_fusion
  71.6 0.1 copy.41
  71.7 0.1 copy.29
  71.8 0.1 copy.28
  71.9 0.1 copy.27
  72.0 0.1 copy.38
  72.1 0.1 copy.32
  72.2 0.1 copy.40
  72.3 0.1 copy.37
  72.4 0.1 copy.31
  72.5 0.1 copy.36
  72.6 0.1 copy.33
  72.7 0.1 copy.35
  72.8 0.1 copy.39
  72.9 0.1 copy.30
  72.9 0.1 copy.34
  73.0 0.7 stack.107.coef
  73.7 3.2 %combine.1 = (f32[2,8,16,256]{3,2,1,0:T(8,128)}, bf16[128,256]{1,0:T(8,128)(2,1)}) custom-call(f32[2,15]{1,0:T(2,128)} %stack.107.coef, f32[2,8,16,256]{3,2,1,0:T(8,128)} %x0.1, f32[2,8,16,256]{3,2,1,0:T(8,128)} %a0.1, f32[3,2,8,16,256]{4,3,2,1,0:T(8,128)} %get-tuple-element.8.v, f32[3,4,2,8,16,256]{5,4,3,2,1,0:T(8,128)} %get-tuple-element.9.w), custom_call_target="tpu_custom_call" | custom-call | tf_op jit(solution)/shard_map/combine/pallas_call | solution.py:287
  76.9 6.5 %all-gather = bf16[512,256]{1,0:T(8,128)(2,1)} all-gather(bf16[128,256]{1,0:T(8,128)(2,1)} %get-tuple-element.11.own), channel_id=2, replica_groups=mesh['brick'=8,'depth'=4] {'depth'}, dimensions={0}, use_global_device_ids=true | all-gather | bytes 327680 | tf_op jit(solution)/shard_map/all_gather | solution.py:411
  83.4 6.5 %covariance.1 = f32[128,256]{1,0:T(8,128)} custom-call(s32[16]{0:T(128)} %bitcast.674, s32[16]{0:T(128)} %bitcast.675, bf16[4,128,256]{2,1,0:T(8,128)(2,1)} %bitcast.643, bf16[128,256]{1,0:T(8,128)(2,1)} %get-tuple-element.11.own, bf16[16,512,512]{2,1,0:T(8,128)(2,1)} %bitcast.640), custom_call_target="tpu_custom_call" | custom-call | tf_op jit(solution)/shard_map/covariance/pallas_call | solution.py:316
  (92 shorter events, 2.4 us)
Async XLA Ops:
  0.6 4.5 %copy-start.1 = (f32[2,8,16,256]{3,2,1,0:T(8,128)S(1)}, f32[2,8,16,256]{3,2,1,0:T(8,128)}, u32[]{:S(2)}) copy-start(f32[2,8,16,256]{3,2,1,0:T(8,128)} %a0.1) | copy-start | bytes 786436
  5.5 6.5 %collective-permute-start.1 = (bf16[103424]{0:T(1024)(128)(2,1)S(1)}, bf16[103424]{0:T(1024)(128)(2,1)S(1)}, u32[]{:S(2)}, u32[]{:S(2)}) collective-permute-start(bf16[103424]{0:T(1024)(128)(2,1)S(1)} %get-tuple-element.35), channel_id=1, source_target_pairs={{4,8},{8,4},{12,16},{16,12},{20,24},{24,20},{5,9},{9,5},{13,17},{1... | collective-permute-start | bytes 620552 | tf_op jit(solution)/shard_map/ppermute | solution.py:30
  6.1 13.9 %collective-permute-start = (bf16[103424]{0:T(1024)(128)(2,1)S(1)}, bf16[103424]{0:T(1024)(128)(2,1)S(1)}, u32[]{:S(2)}, u32[]{:S(2)}) collective-permute-start(bf16[103424]{0:T(1024)(128)(2,1)S(1)} %get-tuple-element.36), channel_id=1, source_target_pairs={{0,4},{4,0},{8,12},{12,8},{16,20},{20,16},{24,28},{28,24},{1,5},{5... | collective-permute-start | bytes 620552 | tf_op jit(solution)/shard_map/ppermute | solution.py:29
  20.1 0.9 %copy-start.2 = (f32[8,16,256]{2,1,0:T(8,128)S(1)}, f32[8,16,256]{2,1,0:T(8,128)}, u32[]{:S(2)}) copy-start(f32[8,16,256]{2,1,0:T(8,128)} %param.10) | copy-start | bytes 393220
  21.3 1.0 %copy-start = (f32[2,8,16,256]{3,2,1,0:T(8,128)S(1)}, f32[2,8,16,256]{3,2,1,0:T(8,128)}, u32[]{:S(2)}) copy-start(f32[2,8,16,256]{3,2,1,0:T(8,128)} %x0.1) | copy-start | bytes 786436
  23.5 1.9 %collective-permute-start.2 = (bf16[188416]{0:T(1024)(128)(2,1)}, bf16[188416]{0:T(1024)(128)(2,1)S(1)}, u32[]{:S(2)}, u32[]{:S(2)}) collective-permute-start(bf16[188416]{0:T(1024)(128)(2,1)} %get-tuple-element.31), channel_id=1, source_target_pairs={{0,1},{1,0},{2,3},{3,2},{4,5},{5,4},{6,7},{7,6},{8,9},{9,8},{10,11... | collective-permute-start | bytes 1130504 | tf_op jit(solution)/shard_map/ppermute | solution.py:29
  23.6 1.9 %collective-permute-start.3 = (bf16[188416]{0:T(1024)(128)(2,1)S(1)}, bf16[188416]{0:T(1024)(128)(2,1)S(1)}, u32[]{:S(2)}, u32[]{:S(2)}) collective-permute-start(bf16[188416]{0:T(1024)(128)(2,1)S(1)} %get-tuple-element.32), channel_id=1, source_target_pairs={{1,2},{2,1},{5,6},{6,5},{9,10},{10,9},{13,14},{14,13},{17,18},{18,... | collective-permute-start | bytes 1130504 | tf_op jit(solution)/shard_map/ppermute | solution.py:30

commit v4 on v3

v4 whole, which is shorter than its diff:
```python
import functools

import jax
import jax.numpy as jnp
from jax import lax
from jax.experimental import pallas as pl
from jax.experimental.pallas import tpu as pltpu
from jax.sharding import PartitionSpec as P

LAPLACE_SHIFTS = (0.5, 2.0)
BOTH = ("brick", "depth")
HX = 6
HC = 5
HA = 4
HU = 3
ZP = 8
THETA = 6.0
PAIRS = tuple((k, l) for k in range(4) for l in range(k, 4))
SLOTS = 32
VMEM = pl.BlockSpec(memory_space=pltpu.VMEM)
SMEM = pl.BlockSpec(memory_space=pltpu.SMEM)
ANY = pl.BlockSpec(memory_space=pl.ANY)
NT = (((1,), (1,)), ((), ()))
PARAMS = pltpu.CompilerParams(vmem_limit_bytes=28 * 1024 * 1024)


def held(a):
    return pltpu.with_memory_space_constraint(a, pltpu.VMEM)


def is_odd(axis):
    return lax.rem(lax.axis_index(axis), 2) == 1


def pairings(axis):
    size = lax.axis_size(axis)
    first = [(i, i ^ 1) for i in range(size) if (i ^ 1) < size]
    second = [(i, j) for i in range(size) for j in [((i + 1) ^ 1) - 1] if 0 <= j < size]
    return first, second


def swap(first, second, axis):
    one, two = pairings(axis)
    return lax.ppermute(first, axis, one), lax.ppermute(second, axis, two)


LX, LC, LA = 0, 2 * HX, 2 * HX + HC
LP = LA + 2 * HA


def pack_kernel(x0, cond, a0, src_cell, src_amp, rec_cell, observed, first, second, table):
    size_x, _, size_y = cond.shape
    odd = is_odd("brick")

    def split(v):
        one = v.astype(jnp.bfloat16).astype(jnp.float32)
        two = (v - one).astype(jnp.bfloat16).astype(jnp.float32)
        return one, two, v - one - two

    table[...] = jnp.zeros_like(table)
    for base, cells, amounts in ((0, src_cell, src_amp), (8, rec_cell, observed)):
        n = cells.shape[-1]
        at = cells[...].astype(jnp.float32)
        hi = jnp.floor((at + 0.5) * (1.0 / size_y))
        table[base : base + 1, :n] = hi + 1.0
        table[base + 1 : base + 2, :n] = at - hi * size_y
        for s, part in enumerate(split(amounts[...])):
            table[base + 2 + 2 * s : base + 4 + 2 * s, :n] = part
    points = table[...].astype(jnp.bfloat16)
    for out, low in ((first, odd), (second, jnp.logical_not(odd))):
        for f in range(2):
            for i in range(HX):
                out[LX + f * HX + i] = x0[f, jnp.where(low, i, size_x - HX + i)].astype(jnp.bfloat16)
            for i in range(HA):
                out[LA + f * HA + i] = a0[f, jnp.where(low, i, size_x - HA + i)].astype(jnp.bfloat16)
        for i in range(HC):
            out[LC + i] = cond[jnp.where(low, i, size_x - HC + i)].astype(jnp.bfloat16)
        out[LP] = points


def pack(x0, cond, a0, src_cell, src_amp, rec_cell, observed):
    shape = (LP + 1,) + cond.shape[1:]
    return pl.pallas_call(
        pack_kernel,
        out_shape=(jax.ShapeDtypeStruct(shape, jnp.bfloat16),) * 2,
        in_specs=[VMEM] * 7,
        out_specs=(VMEM, VMEM),
        scratch_shapes=[pltpu.VMEM(cond.shape[1:], jnp.float32)],
        compiler_params=PARAMS,
        name="pack",
    )(x0, cond, a0, src_cell, src_amp, rec_cell, observed)


def joined_rows(x0, cond, a0, first, second):
    size_x = cond.shape[0]
    odd = is_odd("brick")

    def low(at):
        return jnp.where(odd, first[at].astype(jnp.float32), second[at].astype(jnp.float32))

    def high(at):
        return jnp.where(odd, second[at].astype(jnp.float32), first[at].astype(jnp.float32))

    def reader(own, base, halo):
        def row(i):
            if i < halo:
                return low(base + i)
            if i >= halo + size_x:
                return high(base + i - halo - size_x)
            return own(i - halo)
        return row

    fields = [reader(lambda i, f=f: x0[f, i], LX + f * HX, HX) for f in range(2)]
    adjoints = [reader(lambda i, f=f: a0[f, i], LA + f * HA, HA) for f in range(2)]
    return fields, reader(lambda i: cond[i], LC, HC), adjoints, low, high


def mid_kernel(x0, cond, a0, sent, first, second, out_first, out_second):
    size_x, size_z, size_y = cond.shape
    fields, conds, adjoints, low, high = joined_rows(x0, cond, a0, first, second)
    odd = is_odd("depth")
    n = size_y // 4
    points = low(LP) + pltpu.roll(sent[LP].astype(jnp.float32), n, 1) + pltpu.roll(high(LP), 2 * n, 1)

    def put(at, down, up):
        down = jnp.concatenate(down, axis=0)
        up = jnp.concatenate(up, axis=0)
        out_first[at] = jnp.where(odd, down, up).astype(jnp.bfloat16)
        out_second[at] = jnp.where(odd, up, down).astype(jnp.bfloat16)

    at = 0
    for i in range(1, size_x + 2 * HX - 1):
        rows = [r(i) for r in fields]
        put(at, [r[:ZP] for r in rows], [r[size_z - ZP :] for r in rows])
        at += 1
    for i in range(1, size_x + 2 * HC - 1, 2):
        rows = [conds(i), conds(i + 1)]
        put(at, [r[:ZP] for r in rows], [r[size_z - ZP :] for r in rows])
        at += 1
    for i in range(1, size_x + 2 * HA - 1, 2):
        rows = [r(j) for j in (i, i + 1) for r in adjoints]
        put(at, [r[:HA] for r in rows], [r[size_z - HA :] for r in rows])
        at += 1
    out_first[at] = points.astype(jnp.bfloat16)
    out_second[at] = points.astype(jnp.bfloat16)


def depth_layers(size_x):
    return (size_x + 2 * HX - 2) + (size_x + 2 * HC - 2) // 2 + (size_x + 2 * HA - 2) // 2 + 1


def mid(x0, cond, a0, sent, first, second):
    size_x, size_z, size_y = cond.shape
    shape = (depth_layers(size_x), size_z, size_y)
    return pl.pallas_call(
        mid_kernel,
        out_shape=(jax.ShapeDtypeStruct(shape, jnp.bfloat16),) * 2,
        in_specs=[VMEM] * 6,
        out_specs=(VMEM, VMEM),
        compiler_params=PARAMS,
        name="mid",
    )(x0, cond, a0, sent, first, second)


def place(t, q, weights, halo, dst, lists, size_x, size_z, size_y):
    n_list = lists.shape[-1]
    each = n_list // 4
    lane = lax.broadcasted_iota(jnp.int32, (1, n_list), 1)
    dx = jnp.where(lane < each, -1, jnp.where(lane < 2 * each, 0, 1))
    nx = size_x + 2 * halo
    hi = lists[q : q + 1] - 1.0
    lo = lists[q + 1 : q + 2].astype(jnp.int32)
    x = jnp.floor((hi + 0.5) * (1.0 / size_z))
    z = (hi - x * size_z).astype(jnp.int32)
    row_x = x.astype(jnp.int32) + halo + size_x * dx
    ok = (hi >= 0.0) & (row_x >= 0) & (row_x < nx)
    if t == 1:
        depth, z0 = size_z, ZP
        target = row_x * size_z + z
    elif t == 0:
        depth, z0 = ZP, 0
        target = row_x * ZP + z - (size_z - ZP)
        ok = ok & (z >= size_z - ZP)
    else:
        depth, z0 = ZP, ZP + size_z
        target = row_x * ZP + z
        ok = ok & (z < ZP)
    target = jnp.where(ok, target, -1)
    hit = lax.broadcasted_iota(jnp.int32, (nx * depth, n_list), 0) == target
    right = (lax.broadcasted_iota(jnp.int32, (size_y, n_list), 0) == lo).astype(jnp.float32).astype(jnp.bfloat16)
    for at_out, parts in weights:
        total = None
        for p in parts:
            amount = 1.0 if p is None else lists[p : p + 1]
            left = jnp.where(hit, amount, 0.0).astype(jnp.bfloat16)
            d = lax.dot_general(left, right, NT, preferred_element_type=jnp.float32)
            total = d if total is None else total + d
        dst[at_out, :, z0 : z0 + depth, :] = total.reshape(nx, depth, size_y)


SRC_WEIGHTS = ((0, (2, 4, 6)), (1, (3, 5, 7)))
REC_WEIGHTS = ((0, (10, 12, 14)), (1, (11, 13, 15)), (2, (None,)))


def prep_kernel(x0, cond, a0, sent2, first, second, x0_w, cond_w, a0_w, src, rec):
    size_x, size_z, size_y = cond.shape
    fields, conds, adjoints, _, _ = joined_rows(x0, cond, a0, first, second)
    own = slice(ZP, ZP + size_z)
    for f in range(2):
        for i in range(size_x + 2 * HX):
            x0_w[f, i, own] = fields[f](i)
        for i in range(size_x + 2 * HA):
            a0_w[f, i, own] = adjoints[f](i)
    for i in range(size_x + 2 * HC):
        cond_w[i, own] = conds(i)
    lists = sent2[sent2.shape[0] - 1].astype(jnp.float32)
    place(1, 0, SRC_WEIGHTS, HC, src, lists, size_x, size_z, size_y)
    place(1, 8, REC_WEIGHTS, HU, rec, lists, size_x, size_z, size_y)


def wide_shapes(size_x, size_z, size_y):
    slab = (size_z + 2 * ZP, size_y)
    return (
        (2, size_x + 2 * HX) + slab,
        (size_x + 2 * HC,) + slab,
        (2, size_x + 2 * HA) + slab,
        (2, size_x + 2 * HC) + slab,
        (3, size_x + 2 * HU) + slab,
    )


def prep(x0, cond, a0, sent2, first, second):
    shapes = wide_shapes(*cond.shape)
    return pl.pallas_call(
        prep_kernel,
        out_shape=tuple(pltpu.VMEM(s, jnp.float32) for s in shapes),
        in_specs=[VMEM] * 6,
        out_specs=(VMEM,) * 5,
        compiler_params=PARAMS,
        name="prep",
    )(x0, cond, a0, sent2, first, second)


def beside_z_y(c):
    rows, width = c.shape
    half = width // 2
    total = pltpu.roll(c, 1, 0) + pltpu.roll(c, rows - 1, 0)
    lane = lax.broadcasted_iota(jnp.int32, (rows, half), 1)
    first = lane == 0
    last = lane == half - 1
    a, b = c[:, :half], c[:, half:]
    ra, rb = pltpu.roll(a, 1, 1), pltpu.roll(b, 1, 1)
    la, lb = pltpu.roll(a, half - 1, 1), pltpu.roll(b, half - 1, 1)
    ya = jnp.where(first, 0.0, ra) + jnp.where(last, lb, la)
    yb = jnp.where(first, ra, rb) + jnp.where(last, 0.0, lb)
    return total + jnp.concatenate([ya, yb], axis=1)


def chain_kernel(size_x, size_z, x0_in, cond_in, a0_in, src_in, rec_in, first, second, blocks,
                 x0, cond, a0, src, rec, v_out, w_out, sums_out, blocks_out,
                 v0, v1, v2, u, w1, w2, w3, acc, sem):
    prefetch = pltpu.make_async_copy(blocks, blocks_out, sem)
    prefetch.start()
    rows_z = x0.shape[-2]
    size_y = x0.shape[-1]
    own = slice(ZP, ZP + size_z)
    top = ZP + size_z

    odd = is_odd("depth")

    def low(at):
        return jnp.where(odd, first[at].astype(jnp.float32), second[at].astype(jnp.float32))

    def high(at):
        return jnp.where(odd, second[at].astype(jnp.float32), first[at].astype(jnp.float32))

    blank = jnp.zeros((ZP, size_y), jnp.float32)
    gap = jnp.zeros((ZP - HA, size_y), jnp.float32)
    at = 0
    for i in range(1, size_x + 2 * HX - 1):
        a, b = low(at), high(at)
        for f in range(2):
            x0[f, i, 0:ZP] = a[f * ZP : (f + 1) * ZP]
            x0[f, i, top : top + ZP] = b[f * ZP : (f + 1) * ZP]
        at += 1
    for i in range(1, size_x + 2 * HC - 1, 2):
        a, b = low(at), high(at)
        for j in range(2):
            cond[i + j, 0:ZP] = a[j * ZP : (j + 1) * ZP]
            cond[i + j, top : top + ZP] = b[j * ZP : (j + 1) * ZP]
        at += 1
    for i in range(1, size_x + 2 * HA - 1, 2):
        a, b = low(at), high(at)
        for j in range(2):
            for f in range(2):
                part = slice((2 * j + f) * HA, (2 * j + f + 1) * HA)
                a0[f, i + j, 0:ZP] = jnp.concatenate([gap, a[part]], axis=0)
                a0[f, i + j, top : top + ZP] = jnp.concatenate([b[part], gap], axis=0)
        at += 1
    for ref, lead in ((x0, 2), (cond, 0), (a0, 2)):
        n = ref.shape[-3]
        for i in (0, n - 1):
            for z in (slice(0, ZP), slice(top, top + ZP)):
                if lead:
                    for f in range(lead):
                        ref[f, i, z] = blank
                else:
                    ref[i, z] = blank
    for t, lists in ((0, low(at)), (2, high(at))):
        place(t, 0, SRC_WEIGHTS, HC, src, lists, size_x, size_z, size_y)
        place(t, 8, REC_WEIGHTS, HU, rec, lists, size_x, size_z, size_y)

    def edge(axis):
        at = lax.axis_index(axis)
        return (at > 0).astype(jnp.float32), (at < lax.axis_size(axis) - 1).astype(jnp.float32)

    low_x, high_x = edge("brick")
    low_z, high_z = edge("depth")
    row = lax.broadcasted_iota(jnp.int32, (rows_z, size_y), 0)
    in_z = jnp.where(row < ZP, low_z, jnp.where(row >= ZP + size_z, high_z, 1.0))

    def mask(i, halo):
        return in_z * jnp.where(i < halo, low_x, jnp.where(i >= halo + size_x, high_x, 1.0))

    def apply(ref, idx, i, damp):
        c = ref[idx + (i,)]
        return damp * c - (ref[idx + (i - 1,)] + ref[idx + (i + 1,)] + beside_z_y(c))

    def loop(n, body):
        def step(i, carry):
            body(i)
            return carry
        lax.fori_loop(0, n, step, 0)

    def first(i):
        m = mask(i, HC)
        for f, s in enumerate(LAPLACE_SHIFTS):
            v0[f, i] = m * (src[f, i] - apply(x0, (f,), i + 1, s * cond[i] + THETA))

    loop(size_x + 2 * HC, first)

    def second(i):
        m = mask(i, 4)
        for f, s in enumerate(LAPLACE_SHIFTS):
            v1[f, i] = m * apply(v0, (f,), i + 1, s * cond[i + 1])

    loop(size_x + 8, second)

    def third(i):
        m = mask(i, 3)
        for f, s in enumerate(LAPLACE_SHIFTS):
            v2[f, i] = m * apply(v1, (f,), i + 1, s * cond[i + 2])

    loop(size_x + 6, third)

    def start(i):
        m = mask(i, HU)
        many = rec[2, i]
        for f, s in enumerate(LAPLACE_SHIFTS):
            u[0, f, i] = m * (many * x0[f, i + 3] - rec[f, i] - apply(a0, (f,), i + 1, s * cond[i + 2] + THETA))
            u[1, f, i] = many * v0[f, i + 2]
            u[2, f, i] = many * v1[f, i + 1]
            u[3, f, i] = many * v2[f, i]

    loop(size_x + 2 * HU, start)

    def level(src_ref, dst_ref, halo):
        def body(i):
            m = mask(i, halo)
            for f, s in enumerate(LAPLACE_SHIFTS):
                damp = s * cond[i + HC - halo]
                for k in range(4):
                    dst_ref[k, f, i] = m * apply(src_ref, (k, f), i + 1, damp)
        loop(size_x + 2 * halo, body)

    level(u, w1, 2)
    level(w1, w2, 1)

    def last(i):
        for f, s in enumerate(LAPLACE_SHIFTS):
            damp = s * cond[i + HC]
            for k in range(4):
                w3[k, f, i] = apply(w2, (k, f), i + 1, damp)[own]

    loop(size_x, last)

    def tiles(a):
        total = None
        for z in range(0, a.shape[0], 8):
            for y in range(0, a.shape[1], 128):
                t = a[z : z + 8, y : y + 128]
                total = t if total is None else total + t
        return total

    zero = jnp.zeros((8, 128), jnp.float32)
    for f, s in enumerate(LAPLACE_SHIFTS):
        def forward_sums(i, carry, f=f, s=s):
            p0 = v0[f, i + 5, own]
            p1 = v1[f, i + 4, own]
            p2 = v2[f, i + 3, own]
            p3 = apply(v2, (f,), i + 3, s * cond[i + 5])[own]
            v_out[0, f, i] = p0
            v_out[1, f, i] = p1
            v_out[2, f, i] = p2
            made = (p0 * p0, p0 * p1, p1 * p1, p1 * p2, p2 * p2, p2 * p3)
            return tuple(c + tiles(a) for c, a in zip(carry, made))
        done = lax.fori_loop(0, size_x, forward_sums, (zero,) * 6)
        for j in range(6):
            acc[j * SLOTS + 2 * len(PAIRS) + f] = done[j]

    levels = ((u, 3, own), (w1, 2, own), (w2, 1, own), (w3, 0, slice(0, size_z)))
    for j in range(6):
        ra, oa, za = levels[j // 2]
        rb, ob, zb = levels[j - j // 2]
        for f in range(2):
            def pair_sums(i, carry, f=f, j=j):
                a = [ra[k, f, i + oa, za] for k in range(4)]
                b = a if j % 2 == 0 else [rb[k, f, i + ob, zb] for k in range(4)]
                if j % 2 == 0:
                    for k in range(4):
                        w_out[j // 2, k, f, i] = a[k]
                return tuple(c + tiles(a[k] * b[l]) for c, (k, l) in zip(carry, PAIRS))
            done = lax.fori_loop(0, size_x, pair_sums, (zero,) * len(PAIRS))
            for n in range(len(PAIRS)):
                acc[j * SLOTS + 2 * n + f] = done[n]

    for j in range(acc.shape[0] // SLOTS):
        for n in range(0 if j >= 6 else 2 * len(PAIRS) + 2, SLOTS):
            acc[j * SLOTS + n] = zero
    by_lane = jnp.sum(acc[...], axis=1)
    ones = jnp.ones((8, 128), jnp.float32)
    out = lax.dot_general(ones, by_lane, NT, precision=lax.Precision.HIGHEST, preferred_element_type=jnp.float32)
    sums_out[...] = jnp.broadcast_to(out[0:1][None], sums_out.shape)
    prefetch.wait()


def chain(wide, first, second, blocks, size_x, size_z, n_dev):
    size_y = wide[0].shape[-1]
    f32 = jnp.float32
    slab = (size_z + 2 * ZP, size_y)
    outs = tuple(pltpu.VMEM(a.shape, f32) for a in wide) + (
        pltpu.VMEM((3, 2, size_x, size_z, size_y), f32),
        pltpu.VMEM((3, 4, 2, size_x, size_z, size_y), f32),
        jax.ShapeDtypeStruct((n_dev, 1, 256), f32),
        pltpu.VMEM(blocks.shape, blocks.dtype),
    )
    scratch = [
        pltpu.VMEM((2, size_x + 2 * HC) + slab, f32),
        pltpu.VMEM((2, size_x + 8) + slab, f32),
        pltpu.VMEM((2, size_x + 6) + slab, f32),
        pltpu.VMEM((4, 2, size_x + 6) + slab, f32),
        pltpu.VMEM((4, 2, size_x + 4) + slab, f32),
        pltpu.VMEM((4, 2, size_x + 2) + slab, f32),
        pltpu.VMEM((4, 2, size_x, size_z, size_y), f32),
        pltpu.VMEM((256, 8, 128), f32),
        pltpu.SemaphoreType.DMA,
    ]
    return pl.pallas_call(
        functools.partial(chain_kernel, size_x, size_z),
        out_shape=outs,
        in_specs=[VMEM] * 7 + [ANY],
        out_specs=(VMEM,) * 9,
        scratch_shapes=scratch,
        input_output_aliases={i: i for i in range(5)},
        compiler_params=PARAMS,
        name="chain",
    )(*[held(a) for a in wide], first, second, blocks)[5:]


def coefficients(mu):
    a = [[mu[i + j + 1] + THETA * mu[i + j] for j in range(3)] for i in range(3)]

    def inverse(pivot, size):
        good = pivot > 1e-6 * size
        return jnp.where(good, 1.0 / jnp.where(good, pivot, 1.0), 0.0)

    i0 = inverse(a[0][0], 0.0)
    l10 = a[0][1] * i0
    l20 = a[0][2] * i0
    i1 = inverse(a[1][1] - l10 * a[0][1], a[1][1])
    e21 = a[1][2] - l10 * a[0][2]
    l21 = e21 * i1
    i2 = inverse(a[2][2] - l20 * a[0][2] - l21 * e21, a[2][2])
    y0 = mu[0]
    y1 = mu[1] - l10 * y0
    y2 = mu[2] - l20 * y0 - l21 * y1
    c2 = y2 * i2
    c1 = y1 * i1 - l21 * c2
    c0 = y0 * i0 - l10 * c1 - l20 * c2
    return c0, c1, c2


def combine_kernel(every, x0, a0, v, w, forward, gradient):
    total = jnp.sum(every[...], axis=0)
    rows = jnp.concatenate([total[:, j * SLOTS : (j + 1) * SLOTS] for j in range(6)], axis=0)
    rows = jnp.concatenate([rows, jnp.zeros((2, SLOTS), jnp.float32)], axis=0)
    rows = jnp.concatenate([rows, jnp.zeros((8, 128 - SLOTS), jnp.float32)], axis=1)
    n_pair = 2 * len(PAIRS)
    at = lax.broadcasted_iota(jnp.int32, (128, 128), 0)
    to = lax.broadcasted_iota(jnp.int32, (128, 128), 1)
    same = (at & 1) == (to & 1)

    def gather_lanes(values, chosen):
        table = jnp.where(same & chosen, 1.0, 0.0)
        return jnp.dot(values, table, precision=lax.Precision.HIGHEST, preferred_element_type=jnp.float32)

    mu = gather_lanes(rows, (at >= n_pair) & (at < n_pair + 2))
    c = coefficients([mu[j : j + 1] for j in range(6)])
    basis = (jnp.ones_like(c[0]),) + c
    pair = lax.broadcasted_iota(jnp.int32, (1, 128), 1) // 2
    weight = jnp.zeros((1, 128), jnp.float32)
    for n, (k, l) in enumerate(PAIRS):
        product = basis[k] * basis[l] * (1.0 if k == l else 2.0)
        weight = jnp.where(pair == n, product, weight)
    nu = gather_lanes(rows * weight, at < n_pair)
    d = coefficients([nu[j : j + 1] for j in range(6)])
    size_x = x0.shape[1]
    scale = []
    for f in range(2):
        up = [c[k][:, f : f + 1] for k in range(3)]
        down = [[(d[j] * basis[k])[:, f : f + 1] for k in range(4)] for j in range(3)]
        scale.append((up, down))
    for i in range(size_x):
        total = None
        for f, s in enumerate(LAPLACE_SHIFTS):
            up, down = scale[f]
            field = x0[f, i]
            for k in range(3):
                field = field + up[k] * v[k, f, i]
            other = a0[f, i]
            for j in range(3):
                for k in range(4):
                    other = other + down[j][k] * w[j, k, f, i]
            forward[f, i] = field
            part = s * field * other
            total = part if total is None else total + part
        gradient[i] = (-total).astype(gradient.dtype)


def combine(every, x0, a0, v, w):
    return pl.pallas_call(
        combine_kernel,
        out_shape=(
            jax.ShapeDtypeStruct(x0.shape, jnp.float32),
            jax.ShapeDtypeStruct(x0.shape[1:], jnp.bfloat16),
        ),
        in_specs=[VMEM] * 5,
        out_specs=(VMEM, VMEM),
        compiler_params=PARAMS,
        name="combine",
    )(every, x0, a0, held(v), held(w))


def covariance_kernel(rows, cols, every, own, blocks, out, wide):
    n_dev, size_x, size_z, width = every.shape
    n_rows = size_x * size_z
    per = blocks.shape[-1] // width
    for d in range(n_dev):
        wide[d * n_rows : (d + 1) * n_rows, :] = every[d].reshape(n_rows, width).astype(jnp.float32)
    out[...] = own[...].reshape(n_rows, width).astype(jnp.float32)
    for k in range(blocks.shape[0]):
        picked = jnp.concatenate([wide[pl.ds(cols[k] * per + i, 1), :] for i in range(per)], axis=1)
        picked = jnp.broadcast_to(picked, (16, picked.shape[1])).astype(jnp.bfloat16)
        term = lax.dot_general(picked, blocks[k], NT, preferred_element_type=jnp.float32)[0:1]
        for i in range(per):
            at = pl.ds(rows[k] * per + i, 1)
            out[at, :] = out[at, :] + term[:, i * width : (i + 1) * width]


def covariance(rows, cols, every, own, blocks):
    n_dev, size_x, size_z, width = every.shape
    return pl.pallas_call(
        covariance_kernel,
        out_shape=jax.ShapeDtypeStruct((size_x * size_z, width), jnp.float32),
        in_specs=[SMEM, SMEM, VMEM, VMEM, VMEM],
        out_specs=VMEM,
        scratch_shapes=[pltpu.VMEM((n_dev * size_x * size_z, width), jnp.float32)],
        compiler_params=PARAMS,
        name="covariance",
    )(rows, cols, every, own, held(blocks))


def local(
    conductivity,
    initial_field,
    adjoint_initial,
    src_cell,
    src_amp,
    rec_cell,
    observed,
    cov_blocks,
    cov_rows,
    cov_cols,
):
    size_x, size_z, size_y = conductivity.shape
    n_dev = lax.axis_size("brick") * lax.axis_size("depth")
    fields = (initial_field, conductivity, adjoint_initial)
    x0, cond, a0 = fields
    sent = pack(x0, cond, a0, src_cell[0], src_amp[0, 0], rec_cell[0], observed[0, 0])
    first, second = swap(*sent, "brick")
    sent2 = mid(x0, cond, a0, sent[0], first, second)
    wide = prep(x0, cond, a0, sent2[0], first, second)
    first2, second2 = swap(*sent2, "depth")
    v, w, sums, blocks = chain(wide, first2, second2, cov_blocks[0, 0], size_x, size_z, n_dev)
    every = lax.all_to_all(sums, BOTH, 0, 0, tiled=True)
    forward, gradient = combine(every, x0, a0, v, w)
    every_block = lax.all_gather(gradient, "depth", axis=0, tiled=False)
    out = covariance(cov_rows[0, 0], cov_cols[0, 0], every_block, gradient, blocks)
    return (forward, out.reshape(size_x, size_z, size_y))


def solution(mesh):
    return jax.shard_map(
        local,
        mesh=mesh,
        in_specs=(
            P("brick", "depth", None),
            P(None, "brick", "depth", None),
            P(None, "brick", "depth", None),
            P("brick", "depth", None),
            P("brick", "depth", None, None),
            P("brick", "depth", None),
            P("brick", "depth", None, None),
            P("brick", "depth", None, None, None),
            P("brick", "depth", None),
            P("brick", "depth", None),
        ),
        out_specs=(P(None, "brick", "depth", None), P("brick", "depth", None)),
        check_vma=False,
    )
```

time: 90.3 us -> 74.3 us (0.82)
  other arithmetic: 10.1 us -> 0 us
  Pallas kernels: 30.6 us -> 23.8 us
  blocking collectives: 26.6 us -> 21.8 us
  local copies, waits for them, and re-layouts: 5.48 us -> 8.86 us
  starting transfers between devices: 7.18 us -> 10.1 us
    unnamed x35 -> x24, local copies, waits for them, and re-layouts: 1.98 us -> 8.86 us
    another operation x15 -> x0, other arithmetic: 4.29 us -> none
    all_to_all x1, blocking collectives: 20.1 us -> 16 us  [local(): every = lax.all_to_all(sums, BOTH, 0, 0, tiled=True)]
    pallas_call x1, Pallas kernels: 20.9 us -> 17.8 us  [chain(): pl.pallas_call(functools.partial(chain_kernel, size_x, size_z), out_shape...]
    ppermute x4, starting transfers between devices: 7.18 us -> 10.1 us  [swap(): return (lax.ppermute(first, axis, one), lax.ppermute(second, axis, two))]
    concatenate x2 -> x0, other arithmetic: 2.28 us -> none  [widen(): out.append(jnp.concatenate([before, a, after], axis=dim))]
    another operation x16 -> x0, local copies, waits for them, and re-layouts: 2.05 us -> none  [local(): jnp.stack(list(c) + [d[j] * g[k] for j in range(3) for k in range(4)], ax...]
    pallas_call x1 -> x4, Pallas kernels: 6.48 us -> 4.48 us  [the longest x1 3.5 us: covariance(): pl.pallas_call(covariance_kernel, out_shape=jax.ShapeDtypeStruct((size_x...]
  transfers between devices with their start and end apart: 4 -> 4, of which waited for: 2 -> 2; matrix products, arithmetic and copies ran while one was open for 1% -> 0% of each run, Pallas kernels for 0% -> 1%
where the time goes in v4:
time: 74.3 us; the launch traced here: 74 us
  Pallas kernels  23.8 us (32%)
  blocking collectives  21.8 us (29%)
  starting transfers between devices  10.1 us (14%)
  local copies, waits for them, and re-layouts  8.86 us (12%)
  waiting for transfers between devices  8.76 us (12%)
    pallas_call x1, Pallas kernels, chain(): pl.pallas_call(functools.partial(chain_kernel, size_x, size_z), out_shape...  17.8 us
    all_to_all x1, blocking collectives, local(): every = lax.all_to_all(sums, BOTH, 0, 0, tiled=True)  16 us
    ppermute x4, starting transfers between devices, swap(): return (lax.ppermute(first, axis, one), lax.ppermute(second, axis, two))  10.1 us
    unnamed x24, local copies, waits for them, and re-layouts  8.86 us
    ppermute x4, waiting for transfers between devices, swap(): return (lax.ppermute(first, axis, one), lax.ppermute(second, axis, two))  8.76 us
    all_gather x1, blocking collectives, local(): every_block = lax.all_gather(gradient, 'depth', axis=0, tiled=False)  5.76 us
    pallas_call x1, Pallas kernels, covariance(): pl.pallas_call(covariance_kernel, out_shape=jax.ShapeDtypeStruct((size_x...  3.5 us
    pallas_call x1, Pallas kernels, combine(): pl.pallas_call(combine_kernel, out_shape=(jax.ShapeDtypeStruct(x0.shape,...  1.51 us
  transfers between devices with their start and end apart: 4, of which 2 were waited for; matrix products, arithmetic and copies ran while one was open for 0% of the time, Pallas kernels for 1%

profile of v4, /device:TPU:0, one launch (start us, length us, event | category | flops | bytes accessed | tf_op | source)
XLA Modules:
  0.0 74.0 jit_solution(14568705464928703911)
XLA Ops:
  0.6 0.0 copy-start.1
  0.6 0.9 %copy-done.1 = f32[2,8,16,256]{3,2,1,0:T(8,128)S(1)} copy-done((f32[2,8,16,256]{3,2,1,0:T(8,128)S(1)}, f32[2,8,16,256]{3,2,1,0:T(8,128)}, u32[]{:S(2)}) %copy-start.1) | copy-done | bytes 262168
  1.6 0.0 copy-start.3
  1.6 0.9 %copy-done.3 = f32[2,8,16,256]{3,2,1,0:T(8,128)S(1)} copy-done((f32[2,8,16,256]{3,2,1,0:T(8,128)S(1)}, f32[2,8,16,256]{3,2,1,0:T(8,128)}, u32[]{:S(2)}) %copy-start.3) | copy-done | bytes 262168
  2.5 0.0 copy-start.5
  2.5 0.9 %copy-done.5 = f32[8,16,256]{2,1,0:T(8,128)S(1)} copy-done((f32[8,16,256]{2,1,0:T(8,128)S(1)}, f32[8,16,256]{2,1,0:T(8,128)}, u32[]{:S(2)}) %copy-start.5) | copy-done | bytes 131096
  3.4 0.0 copy-start.6
  3.4 0.7 copy-done.6
  4.1 0.0 copy-start.7
  4.1 0.7 copy-done.7
  4.8 0.0 copy-start.8
  4.8 0.7 copy-done.8
  5.5 0.0 copy-start.9
  5.5 0.7 copy-done.9
  6.1 0.1 pack.1
  6.2 0.7 collective-permute-start.1
  6.9 5.8 %collective-permute-start = (bf16[26,16,256]{2,1,0:T(8,128)(2,1)S(1)}, bf16[26,16,256]{2,1,0:T(8,128)(2,1)S(1)}, u32[]{:S(2)}, u32[]{:S(2)}) collective-permute-start(bf16[26,16,256]{2,1,0:T(8,128)(2,1)S(1)} %get-tuple-element.17.sent), channel_id=1, source_target_pairs={{0,4},{4,0},{8,12},{12,8},{16,20},{20,16},{24,28},{28,24},{1,5},{5... | collective-permute-start | bytes 638984 | tf_op jit(solution)/shard_map/ppermute | solution.py:44
  12.7 0.0 collective-permute-done.1.second
  12.7 8.4 %collective-permute-done.first = bf16[26,16,256]{2,1,0:T(8,128)(2,1)S(1)} collective-permute-done((bf16[26,16,256]{2,1,0:T(8,128)(2,1)S(1)}, bf16[26,16,256]{2,1,0:T(8,128)(2,1)S(1)}, u32[]{:S(2)}, u32[]{:S(2)}) %collective-permute-start) | collective-permute-done | bytes 213024 | tf_op jit(solution)/shard_map/ppermute | solution.py:44
  21.0 0.1 mid.1
  21.2 0.7 collective-permute-start.3
  21.9 2.9 %collective-permute-start.2 = (bf16[34,16,256]{2,1,0:T(8,128)(2,1)S(1)}, bf16[34,16,256]{2,1,0:T(8,128)(2,1)S(1)}, u32[]{:S(2)}, u32[]{:S(2)}) collective-permute-start(bf16[34,16,256]{2,1,0:T(8,128)(2,1)S(1)} %get-tuple-element.19.sent2), channel_id=1, source_target_pairs={{0,1},{1,0},{2,3},{3,2},{4,5},{5,4},{6,7},{7,6},{8,9},{9,8},{10,11... | collective-permute-start | bytes 835592 | tf_op jit(solution)/shard_map/ppermute | solution.py:44
  24.8 0.8 %prep.1 = (f32[2,20,32,256]{3,2,1,0:T(8,128)S(1)}, f32[18,32,256]{2,1,0:T(8,128)S(1)}, f32[2,16,32,256]{3,2,1,0:T(8,128)S(1)}, f32[2,18,32,256]{3,2,1,0:T(8,128)S(1)}, f32[3,14,32,256]{3,2,1,0:T(8,128)S(1)}) custom-call(f32[2,8,16,256]{3,2,1,0:T(8,128)S(1)} %copy-done.1, f32[8,16,256]{2,1,0:T(8,128)S(1)} %copy-done.5, f32[2,8,16,256]{3,2,1,0:T(8,128)S(1)} %copy-done.3, ...), custom_call_target="tpu_custom_call" | custom-call | tf_op jit(solution)/shard_map/prep/pallas_call | solution.py:234
  25.6 0.0 collective-permute-done.3.second
  25.6 0.4 collective-permute-done.2.first
  26.0 0.0 copy-start
  26.0 3.4 %copy-done = bf16[1,1,16,512,512]{4,3,2,1,0:T(8,128)(2,1)S(1)} copy-done((bf16[1,1,16,512,512]{4,3,2,1,0:T(8,128)(2,1)S(1)}, bf16[1,1,16,512,512]{4,3,2,1,0:T(8,128)(2,1)}, u32[]{:S(2)}) %copy-start) | copy-done | bytes 8388632
  29.3 0.0 copy-start.2
  29.3 0.0 copy-start.4
  29.3 17.8 %chain.1 = (f32[2,20,32,256]{3,2,1,0:T(8,128)S(1)}, f32[18,32,256]{2,1,0:T(8,128)S(1)}, f32[2,16,32,256]{3,2,1,0:T(8,128)S(1)}, f32[2,18,32,256]{3,2,1,0:T(8,128...) custom-call(f32[2,20,32,256]{3,2,1,0:T(8,128)S(1)} %get-tuple-elemen, ...), custom_call_target="tpu_custom_call", output_to_operand_aliasing={{0}: (0, {}), {1}: (1, {}), {2}: (2, {}), {3}: (3, {}), {4}... | custom-call | tf_op jit(solution)/shard_map/chain/pallas_call | solution.py:458
  47.2 16.0 %all_to_all.5.every = f32[32,1,256]{2,1,0:T(1,128)S(1)} all-to-all(f32[32,1,256]{2,1,0:T(1,128)S(1)} %get-tuple-element.26), channel_id=1, replica_groups=mesh['brick'=8,'depth'=4] {'brick','depth'}, dimensions={0} | all-to-all | bytes 65536 | tf_op jit(solution)/shard_map/all_to_all | solution.py:605
  63.2 0.0 copy-done.2
  63.2 0.0 copy-done.4
  63.2 0.0 copy-start.10
  63.2 0.0 copy-start.11
  63.2 1.5 %combine.1 = (f32[2,8,16,256]{3,2,1,0:T(8,128)}, bf16[8,16,256]{2,1,0:T(8,128)(2,1)S(1)}) custom-call(f32[32,1,256]{2,1,0:T(1,128)S(1)} %all_to_all.5.every, f32[2,8,16,256]{3,2,1,0:T(8,128)S(1)} %copy-done.2, f32[2,8,16,256]{3,2,1,0:T(8,128)S(1)} %copy-done.4, f32[3,2,8,16,256]{4,3,2,1,0:T(8,128)S(1)} %get-tuple-element.27.v, ...), custom_call_target="tpu_custom_call" | custom-call | tf_op jit(solution)/shard_map/combine/pallas_call | solution.py:541
  64.7 5.8 %all-gather = bf16[32,16,256]{2,1,0:T(8,128)(2,1)S(1)} all-gather(bf16[8,16,256]{2,1,0:T(8,128)(2,1)S(1)} %get-tuple-element.30.own), channel_id=2, replica_groups=mesh['brick'=8,'depth'=4] {'depth'}, dimensions={0}, use_global_device_ids=true | all-gather | bytes 327680 | tf_op jit(solution)/shard_map/all_gather | solution.py:607
  70.5 0.0 copy-done.10
  70.5 0.0 copy-done.11
  70.5 3.5 %covariance.1 = f32[128,256]{1,0:T(8,128)} custom-call(s32[16]{0:T(128)S(1)} %bitcast.15, s32[16]{0:T(128)S(1)} %bitcast.16, bf16[4,8,16,256]{3,2,1,0:T(8,128)(2,1)S(1)} %bitcast.10, bf16[8,16,256]{2,1,0:T(8,128)(2,1)S(1)} %get-tuple-element.30.own, bf16[16,512,512]{2,1,0:T(8,128)(2,1)S(1)} %get-tuple-element.31.blocks), custom_call_target="tpu_custom_call" | custom-call | tf_op jit(solution)/shard_map/covariance/pallas_call | solution.py:572
Async XLA Ops:
  0.6 1.0 %copy-start.1 = (f32[2,8,16,256]{3,2,1,0:T(8,128)S(1)}, f32[2,8,16,256]{3,2,1,0:T(8,128)}, u32[]{:S(2)}) copy-start(f32[2,8,16,256]{3,2,1,0:T(8,128)} %x0.7) | copy-start | bytes 786436
  1.6 0.9 %copy-start.3 = (f32[2,8,16,256]{3,2,1,0:T(8,128)S(1)}, f32[2,8,16,256]{3,2,1,0:T(8,128)}, u32[]{:S(2)}) copy-start(f32[2,8,16,256]{3,2,1,0:T(8,128)} %a0.7) | copy-start | bytes 786436
  2.5 0.9 %copy-start.5 = (f32[8,16,256]{2,1,0:T(8,128)S(1)}, f32[8,16,256]{2,1,0:T(8,128)}, u32[]{:S(2)}) copy-start(f32[8,16,256]{2,1,0:T(8,128)} %cond.5) | copy-start | bytes 393220
  3.4 0.7 copy-start.6
  4.1 0.7 copy-start.7
  4.8 0.7 copy-start.8
  5.5 0.7 copy-start.9
  6.2 6.5 %collective-permute-start.1 = (bf16[26,16,256]{2,1,0:T(8,128)(2,1)S(1)}, bf16[26,16,256]{2,1,0:T(8,128)(2,1)S(1)}, u32[]{:S(2)}, u32[]{:S(2)}) collective-permute-start(bf16[26,16,256]{2,1,0:T(8,128)(2,1)S(1)} %get-tuple-element.18), channel_id=1, source_target_pairs={{4,8},{8,4},{12,16},{16,12},{20,24},{24,20},{5,9},{9,5},{13,17},{1... | collective-permute-start | bytes 638984 | tf_op jit(solution)/shard_map/ppermute | solution.py:44
  6.9 14.2 %collective-permute-start = (bf16[26,16,256]{2,1,0:T(8,128)(2,1)S(1)}, bf16[26,16,256]{2,1,0:T(8,128)(2,1)S(1)}, u32[]{:S(2)}, u32[]{:S(2)}) collective-permute-start(bf16[26,16,256]{2,1,0:T(8,128)(2,1)S(1)} %get-tuple-element.17.sent), channel_id=1, source_target_pairs={{0,4},{4,0},{8,12},{12,8},{16,20},{20,16},{24,28},{28,24},{1,5},{5... | collective-permute-start | bytes 638984 | tf_op jit(solution)/shard_map/ppermute | solution.py:44
  21.2 4.4 %collective-permute-start.3 = (bf16[34,16,256]{2,1,0:T(8,128)(2,1)S(1)}, bf16[34,16,256]{2,1,0:T(8,128)(2,1)S(1)}, u32[]{:S(2)}, u32[]{:S(2)}) collective-permute-start(bf16[34,16,256]{2,1,0:T(8,128)(2,1)S(1)} %get-tuple-element.25), channel_id=1, source_target_pairs={{1,2},{2,1},{5,6},{6,5},{9,10},{10,9},{13,14},{14,13},{17,18},{18,... | collective-permute-start | bytes 835592 | tf_op jit(solution)/shard_map/ppermute | solution.py:44
  21.9 4.1 %collective-permute-start.2 = (bf16[34,16,256]{2,1,0:T(8,128)(2,1)S(1)}, bf16[34,16,256]{2,1,0:T(8,128)(2,1)S(1)}, u32[]{:S(2)}, u32[]{:S(2)}) collective-permute-start(bf16[34,16,256]{2,1,0:T(8,128)(2,1)S(1)} %get-tuple-element.19.sent2), channel_id=1, source_target_pairs={{0,1},{1,0},{2,3},{3,2},{4,5},{5,4},{6,7},{7,6},{8,9},{9,8},{10,11... | collective-permute-start | bytes 835592 | tf_op jit(solution)/shard_map/ppermute | solution.py:44
  26.0 3.4 %copy-start = (bf16[1,1,16,512,512]{4,3,2,1,0:T(8,128)(2,1)S(1)}, bf16[1,1,16,512,512]{4,3,2,1,0:T(8,128)(2,1)}, u32[]{:S(2)}) copy-start(bf16[1,1,16,512,512]{4,3,2,1,0:T(8,128)(2,1)} %param.17) | copy-start | bytes 25165828
  29.3 33.8 %copy-start.2 = (f32[2,8,16,256]{3,2,1,0:T(8,128)S(1)}, f32[2,8,16,256]{3,2,1,0:T(8,128)}, u32[]{:S(2)}) copy-start(f32[2,8,16,256]{3,2,1,0:T(8,128)} %x0.7) | copy-start | bytes 786436
  29.3 33.8 %copy-start.4 = (f32[2,8,16,256]{3,2,1,0:T(8,128)S(1)}, f32[2,8,16,256]{3,2,1,0:T(8,128)}, u32[]{:S(2)}) copy-start(f32[2,8,16,256]{3,2,1,0:T(8,128)} %a0.7) | copy-start | bytes 786436
  63.2 7.3 %copy-start.10 = (s32[1,1,16]{2,1,0:T(1,128)S(1)}, s32[1,1,16]{2,1,0:T(1,128)}, u32[]{:S(2)}) copy-start(s32[1,1,16]{2,1,0:T(1,128)} %param.18) | copy-start | bytes 196
  63.2 7.3 %copy-start.11 = (s32[1,1,16]{2,1,0:T(1,128)S(1)}, s32[1,1,16]{2,1,0:T(1,128)}, u32[]{:S(2)}) copy-start(s32[1,1,16]{2,1,0:T(1,128)} %param.19) | copy-start | bytes 196

commit v5 on v4

--- a/solution.py
+++ b/solution.py
@@ -19,13 +19,17 @@
 SLOTS = 32
 VMEM = pl.BlockSpec(memory_space=pltpu.VMEM)
 SMEM = pl.BlockSpec(memory_space=pltpu.SMEM)
-ANY = pl.BlockSpec(memory_space=pl.ANY)
+HBM = pl.BlockSpec(memory_space=pltpu.HBM)
 NT = (((1,), (1,)), ((), ()))
 PARAMS = pltpu.CompilerParams(vmem_limit_bytes=28 * 1024 * 1024)
 
 
 def held(a):
     return pltpu.with_memory_space_constraint(a, pltpu.VMEM)
+
+
+def in_hbm(a):
+    return pltpu.with_memory_space_constraint(a, pltpu.HBM)
 
 
 def is_odd(axis):
@@ -48,7 +52,18 @@
 LP = LA + 2 * HA
 
 
-def pack_kernel(x0, cond, a0, src_cell, src_amp, rec_cell, observed, first, second, table):
+def pack_kernel(*refs):
+    ins, (first, second), kept, pieces = refs[:7], refs[7:9], refs[9:12], refs[12:16]
+    table, sems = refs[16:]
+    copies = [
+        pltpu.make_async_copy(a, b, sems.at[i]) for i, (a, b) in enumerate(zip(ins, kept + pieces))
+    ]
+    for copy in copies:
+        copy.start()
+    for copy in copies:
+        copy.wait()
+    x0, cond, a0 = kept
+    src_cell, src_amp, rec_cell, observed = pieces
     size_x, _, size_y = cond.shape
     odd = is_odd("brick")
 
@@ -78,17 +93,20 @@
         out[LP] = points
 
 
-def pack(x0, cond, a0, src_cell, src_amp, rec_cell, observed):
+def pack(*ins):
+    x0, cond, a0 = ins[:3]
     shape = (LP + 1,) + cond.shape[1:]
     return pl.pallas_call(
         pack_kernel,
-        out_shape=(jax.ShapeDtypeStruct(shape, jnp.bfloat16),) * 2,
-        in_specs=[VMEM] * 7,
-        out_specs=(VMEM, VMEM),
-        scratch_shapes=[pltpu.VMEM(cond.shape[1:], jnp.float32)],
+        out_shape=(jax.ShapeDtypeStruct(shape, jnp.bfloat16),) * 2
+        + tuple(pltpu.VMEM(a.shape, a.dtype) for a in ins[:3]),
+        in_specs=[HBM] * 7,
+        out_specs=(VMEM,) * 5,
+        scratch_shapes=[pltpu.VMEM(a.shape, a.dtype) for a in ins[3:]]
+        + [pltpu.VMEM(cond.shape[1:], jnp.float32), pltpu.SemaphoreType.DMA((7,))],
         compiler_params=PARAMS,
         name="pack",
-    )(x0, cond, a0, src_cell, src_amp, rec_cell, observed)
+    )(*[in_hbm(a) for a in ins])
 
 
 def joined_rows(x0, cond, a0, first, second):
@@ -326,32 +344,37 @@
         c = ref[idx + (i,)]
         return damp * c - (ref[idx + (i - 1,)] + ref[idx + (i + 1,)] + beside_z_y(c))
 
-    def loop(n, body):
+    def loop(n, body, unroll):
+        while n % unroll:
+            unroll -= 1
+
         def step(i, carry):
-            body(i)
+            for j in range(unroll):
+                body(i * unroll + j)
             return carry
-        lax.fori_loop(0, n, step, 0)
+
+        lax.fori_loop(0, n // unroll, step, 0)
 
     def first(i):
         m = mask(i, HC)
         for f, s in enumerate(LAPLACE_SHIFTS):
             v0[f, i] = m * (src[f, i] - apply(x0, (f,), i + 1, s * cond[i] + THETA))
 
-    loop(size_x + 2 * HC, first)
+    loop(size_x + 2 * HC, first, 18)
 
     def second(i):
         m = mask(i, 4)
         for f, s in enumerate(LAPLACE_SHIFTS):
             v1[f, i] = m * apply(v0, (f,), i + 1, s * cond[i + 1])
 
-    loop(size_x + 8, second)
+    loop(size_x + 8, second, 18)
 
     def third(i):
         m = mask(i, 3)
         for f, s in enumerate(LAPLACE_SHIFTS):
             v2[f, i] = m * apply(v1, (f,), i + 1, s * cond[i + 2])
 
-    loop(size_x + 6, third)
+    loop(size_x + 6, third, 18)
 
     def start(i):
         m = mask(i, HU)
@@ -362,7 +385,7 @@
             u[2, f, i] = many * v1[f, i + 1]
             u[3, f, i] = many * v2[f, i]
 
-    loop(size_x + 2 * HU, start)
+    loop(size_x + 2 * HU, start, 18)
 
     def level(src_ref, dst_ref, halo):
         def body(i):
@@ -371,7 +394,7 @@
                 damp = s * cond[i + HC - halo]
                 for k in range(4):
                     dst_ref[k, f, i] = m * apply(src_ref, (k, f), i + 1, damp)
-        loop(size_x + 2 * halo, body)
+        loop(size_x + 2 * halo, body, 6)
 
     level(u, w1, 2)
     level(w1, w2, 1)
@@ -382,7 +405,7 @@
             for k in range(4):
                 w3[k, f, i] = apply(w2, (k, f), i + 1, damp)[own]
 
-    loop(size_x, last)
+    loop(size_x, last, 4)
 
     def tiles(a):
         total = None
@@ -393,6 +416,15 @@
         return total
 
     zero = jnp.zeros((8, 128), jnp.float32)
+
+    def over_rows(body, carry, unroll=2):
+        def step(i, carry):
+            for j in range(unroll):
+                carry = body(i * unroll + j, carry)
+            return carry
+
+        return lax.fori_loop(0, size_x // unroll, step, carry)
+
     for f, s in enumerate(LAPLACE_SHIFTS):
         def forward_sums(i, carry, f=f, s=s):
             p0 = v0[f, i + 5, own]
@@ -404,7 +436,7 @@
             v_out[2, f, i] = p2
             made = (p0 * p0, p0 * p1, p1 * p1, p1 * p2, p2 * p2, p2 * p3)
             return tuple(c + tiles(a) for c, a in zip(carry, made))
-        done = lax.fori_loop(0, size_x, forward_sums, (zero,) * 6)
+        done = over_rows(forward_sums, (zero,) * 6)
         for j in range(6):
             acc[j * SLOTS + 2 * len(PAIRS) + f] = done[j]
 
@@ -420,7 +452,7 @@
                     for k in range(4):
                         w_out[j // 2, k, f, i] = a[k]
                 return tuple(c + tiles(a[k] * b[l]) for c, (k, l) in zip(carry, PAIRS))
-            done = lax.fori_loop(0, size_x, pair_sums, (zero,) * len(PAIRS))
+            done = over_rows(pair_sums, (zero,) * len(PAIRS))
             for n in range(len(PAIRS)):
                 acc[j * SLOTS + 2 * n + f] = done[n]
 
@@ -430,7 +462,8 @@
     by_lane = jnp.sum(acc[...], axis=1)
     ones = jnp.ones((8, 128), jnp.float32)
     out = lax.dot_general(ones, by_lane, NT, precision=lax.Precision.HIGHEST, preferred_element_type=jnp.float32)
-    sums_out[...] = jnp.broadcast_to(out[0:1][None], sums_out.shape)
+    out = jnp.concatenate([out[0:1, :128], out[0:1, 128:]], axis=0)
+    sums_out[...] = jnp.broadcast_to(out[None], sums_out.shape)
     prefetch.wait()
 
 
@@ -441,7 +474,7 @@
     outs = tuple(pltpu.VMEM(a.shape, f32) for a in wide) + (
         pltpu.VMEM((3, 2, size_x, size_z, size_y), f32),
         pltpu.VMEM((3, 4, 2, size_x, size_z, size_y), f32),
-        jax.ShapeDtypeStruct((n_dev, 1, 256), f32),
+        jax.ShapeDtypeStruct((n_dev, 2, 128), f32),
         pltpu.VMEM(blocks.shape, blocks.dtype),
     )
     scratch = [
@@ -458,13 +491,13 @@
     return pl.pallas_call(
         functools.partial(chain_kernel, size_x, size_z),
         out_shape=outs,
-        in_specs=[VMEM] * 7 + [ANY],
+        in_specs=[VMEM] * 7 + [HBM],
         out_specs=(VMEM,) * 9,
         scratch_shapes=scratch,
         input_output_aliases={i: i for i in range(5)},
         compiler_params=PARAMS,
         name="chain",
-    )(*[held(a) for a in wide], first, second, blocks)[5:]
+    )(*[held(a) for a in wide], first, second, in_hbm(blocks))[5:]
 
 
 def coefficients(mu):
@@ -492,7 +525,10 @@
 
 def combine_kernel(every, x0, a0, v, w, forward, gradient):
     total = jnp.sum(every[...], axis=0)
-    rows = jnp.concatenate([total[:, j * SLOTS : (j + 1) * SLOTS] for j in range(6)], axis=0)
+    per = 128 // SLOTS
+    rows = jnp.concatenate(
+        [total[j // per : j // per + 1, j % per * SLOTS : (j % per + 1) * SLOTS] for j in range(6)], axis=0
+    )
     rows = jnp.concatenate([rows, jnp.zeros((2, SLOTS), jnp.float32)], axis=0)
     rows = jnp.concatenate([rows, jnp.zeros((8, 128 - SLOTS), jnp.float32)], axis=1)
     n_pair = 2 * len(PAIRS)
@@ -551,33 +587,49 @@
     )(every, x0, a0, held(v), held(w))
 
 
-def covariance_kernel(rows, cols, every, own, blocks, out, wide):
+def covariance_kernel(cols, rows, every, own, blocks, out, wide):
     n_dev, size_x, size_z, width = every.shape
     n_rows = size_x * size_z
-    per = blocks.shape[-1] // width
+    n_blocks, size, _ = blocks.shape
+    per = size // width
     for d in range(n_dev):
         wide[d * n_rows : (d + 1) * n_rows, :] = every[d].reshape(n_rows, width).astype(jnp.float32)
-    out[...] = own[...].reshape(n_rows, width).astype(jnp.float32)
-    for k in range(blocks.shape[0]):
-        picked = jnp.concatenate([wide[pl.ds(cols[k] * per + i, 1), :] for i in range(per)], axis=1)
-        picked = jnp.broadcast_to(picked, (16, picked.shape[1])).astype(jnp.bfloat16)
-        term = lax.dot_general(picked, blocks[k], NT, preferred_element_type=jnp.float32)[0:1]
-        for i in range(per):
-            at = pl.ds(rows[k] * per + i, 1)
-            out[at, :] = out[at, :] + term[:, i * width : (i + 1) * width]
-
-
-def covariance(rows, cols, every, own, blocks):
+    picked = jnp.concatenate(
+        [
+            jnp.concatenate([wide[pl.ds(cols[k] * per + i, 1), :] for i in range(per)], axis=1)
+            for k in range(n_blocks)
+        ],
+        axis=0,
+    ).astype(jnp.bfloat16)
+    which = lax.broadcasted_iota(jnp.int32, (n_blocks, size), 0)
+    terms = jnp.zeros((n_blocks, size), jnp.float32)
+    for k in range(n_blocks):
+        product = lax.dot_general(picked, blocks[k], NT, preferred_element_type=jnp.float32)
+        terms = jnp.where(which == k, product, terms)
+    total = own[...].reshape(n_rows, width).astype(jnp.float32)
+    at = lax.broadcasted_iota(jnp.int32, (n_rows, n_blocks), 0)
+    for i in range(per):
+        hit = jnp.where(at == rows[...] * per + i, 1.0, 0.0)
+        total = total + jnp.dot(
+            hit,
+            terms[:, i * width : (i + 1) * width],
+            precision=lax.Precision.HIGHEST,
+            preferred_element_type=jnp.float32,
+        )
+    out[...] = total
+
+
+def covariance(cols, rows, every, own, blocks):
     n_dev, size_x, size_z, width = every.shape
     return pl.pallas_call(
         covariance_kernel,
         out_shape=jax.ShapeDtypeStruct((size_x * size_z, width), jnp.float32),
-        in_specs=[SMEM, SMEM, VMEM, VMEM, VMEM],
+        in_specs=[SMEM, VMEM, VMEM, VMEM, VMEM],
         out_specs=VMEM,
         scratch_shapes=[pltpu.VMEM((n_dev * size_x * size_z, width), jnp.float32)],
         compiler_params=PARAMS,
         name="covariance",
-    )(rows, cols, every, own, held(blocks))
+    )(cols, rows, every, own, held(blocks))
 
 
 def local(
@@ -594,9 +646,10 @@
 ):
     size_x, size_z, size_y = conductivity.shape
     n_dev = lax.axis_size("brick") * lax.axis_size("depth")
-    fields = (initial_field, conductivity, adjoint_initial)
-    x0, cond, a0 = fields
-    sent = pack(x0, cond, a0, src_cell[0], src_amp[0, 0], rec_cell[0], observed[0, 0])
+    *sent, x0, cond, a0 = pack(
+        initial_field, conductivity, adjoint_initial, src_cell[0], src_amp[0, 0], rec_cell[0], observed[0, 0]
+    )
+    x0, cond, a0 = held(x0), held(cond), held(a0)
     first, second = swap(*sent, "brick")
     sent2 = mid(x0, cond, a0, sent[0], first, second)
     wide = prep(x0, cond, a0, sent2[0], first, second)
@@ -605,7 +658,7 @@
     every = lax.all_to_all(sums, BOTH, 0, 0, tiled=True)
     forward, gradient = combine(every, x0, a0, v, w)
     every_block = lax.all_gather(gradient, "depth", axis=0, tiled=False)
-    out = covariance(cov_rows[0, 0], cov_cols[0, 0], every_block, gradient, blocks)
+    out = covariance(cov_cols[0, 0], cov_rows[0], every_block, gradient, blocks)
     return (forward, out.reshape(size_x, size_z, size_y))
 
 

time: 74.3 us -> 59.6 us (0.80)
  local copies, waits for them, and re-layouts: 8.86 us -> 0.01 us
  Pallas kernels: 23.8 us -> 18.1 us
    unnamed x24 -> x4, local copies, waits for them, and re-layouts: 8.86 us -> 0.01 us
    pallas_call x1, Pallas kernels: 17.8 us -> 10.4 us  [chain(): pl.pallas_call(functools.partial(chain_kernel, size_x, size_z), out_shape...]
    pallas_call x1, Pallas kernels: 0.06 us -> 1.22 us  [pack(): pl.pallas_call(pack_kernel, out_shape=(jax.ShapeDtypeStruct(shape, jnp.bf...]
where the time goes in v5:
time: 59.6 us; the launch traced here: 59.4 us
  blocking collectives  21.8 us (37%)
  Pallas kernels  18.1 us (30%)
  starting transfers between devices  10.1 us (17%)
  waiting for transfers between devices  8.76 us (15%)
  between operations  0.69 us (1%)
    all_to_all x1, blocking collectives, local(): every = lax.all_to_all(sums, BOTH, 0, 0, tiled=True)  16 us
    pallas_call x1, Pallas kernels, chain(): pl.pallas_call(functools.partial(chain_kernel, size_x, size_z), out_shape...  10.4 us
    ppermute x4, starting transfers between devices, swap(): return (lax.ppermute(first, axis, one), lax.ppermute(second, axis, two))  10.1 us
    ppermute x4, waiting for transfers between devices, swap(): return (lax.ppermute(first, axis, one), lax.ppermute(second, axis, two))  8.76 us
    all_gather x1, blocking collectives, local(): every_block = lax.all_gather(gradient, 'depth', axis=0, tiled=False)  5.76 us
    pallas_call x1, Pallas kernels, covariance(): pl.pallas_call(covariance_kernel, out_shape=jax.ShapeDtypeStruct((size_x...  4.03 us
    pallas_call x1, Pallas kernels, combine(): pl.pallas_call(combine_kernel, out_shape=(jax.ShapeDtypeStruct(x0.shape,...  1.5 us
    pallas_call x1, Pallas kernels, pack(): pl.pallas_call(pack_kernel, out_shape=(jax.ShapeDtypeStruct(shape, jnp.bf...  1.22 us
  transfers between devices with their start and end apart: 4, of which 2 were waited for; matrix products, arithmetic and copies ran while one was open for 0% of the time, Pallas kernels for 1%

profile of v5, /device:TPU:0, one launch (start us, length us, event | category | flops | bytes accessed | tf_op | source)
XLA Modules:
  0.0 59.4 jit_solution(6692433884399716242)
XLA Ops:
  0.6 1.2 %pack.1 = (bf16[26,16,256]{2,1,0:T(8,128)(2,1)S(1)}, bf16[26,16,256]{2,1,0:T(8,128)(2,1)S(1)}, f32[2,8,16,256]{3,2,1,0:T(8,128)S(1)}, f32[8,16,256]{2,1,0:T(8,128)S(1)}, f32[2,8,16,256]{3,2,1,0:T(8,128)S(1)}) custom-call(f32[2,8,16,256]{3,2,1,0:T(8,128)} %refs_0_.1, f32[8,16,256]{2,1,0:T(8,128)} %refs_1_.1, f32[2,8,16,256]{3,2,1,0:T(8,128)} %refs_2_.1, ...), custom_call_target="tpu_custom_call" | custom-call | tf_op jit(solution)/shard_map/pack/pallas_call | solution.py:99
  1.9 0.7 %collective-permute-start.1 = (bf16[26,16,256]{2,1,0:T(8,128)(2,1)S(1)}, bf16[26,16,256]{2,1,0:T(8,128)(2,1)S(1)}, u32[]{:S(2)}, u32[]{:S(2)}) collective-permute-start(bf16[26,16,256]{2,1,0:T(8,128)(2,1)S(1)} %get-tuple-element.24), channel_id=1, source_target_pairs={{4,8},{8,4},{12,16},{16,12},{20,24},{24,20},{5,9},{9,5},{13,17},{1... | collective-permute-start | bytes 638984 | tf_op jit(solution)/shard_map/ppermute | solution.py:48
  2.5 5.8 %collective-permute-start = (bf16[26,16,256]{2,1,0:T(8,128)(2,1)S(1)}, bf16[26,16,256]{2,1,0:T(8,128)(2,1)S(1)}, u32[]{:S(2)}, u32[]{:S(2)}) collective-permute-start(bf16[26,16,256]{2,1,0:T(8,128)(2,1)S(1)} %get-tuple-element.23.sent), channel_id=1, source_target_pairs={{0,4},{4,0},{8,12},{12,8},{16,20},{20,16},{24,28},{28,24},{1,5},{5... | collective-permute-start | bytes 638984 | tf_op jit(solution)/shard_map/ppermute | solution.py:48
  8.4 0.0 collective-permute-done.1.second
  8.4 8.4 %collective-permute-done.first = bf16[26,16,256]{2,1,0:T(8,128)(2,1)S(1)} collective-permute-done((bf16[26,16,256]{2,1,0:T(8,128)(2,1)S(1)}, bf16[26,16,256]{2,1,0:T(8,128)(2,1)S(1)}, u32[]{:S(2)}, u32[]{:S(2)}) %collective-permute-start) | collective-permute-done | bytes 213024 | tf_op jit(solution)/shard_map/ppermute | solution.py:48
  16.7 0.1 mid.1
  16.9 0.7 %collective-permute-start.3 = (bf16[34,16,256]{2,1,0:T(8,128)(2,1)S(1)}, bf16[34,16,256]{2,1,0:T(8,128)(2,1)S(1)}, u32[]{:S(2)}, u32[]{:S(2)}) collective-permute-start(bf16[34,16,256]{2,1,0:T(8,128)(2,1)S(1)} %get-tuple-element.31), channel_id=1, source_target_pairs={{1,2},{2,1},{5,6},{6,5},{9,10},{10,9},{13,14},{14,13},{17,18},{18,... | collective-permute-start | bytes 835592 | tf_op jit(solution)/shard_map/ppermute | solution.py:48
  17.6 2.9 %collective-permute-start.2 = (bf16[34,16,256]{2,1,0:T(8,128)(2,1)S(1)}, bf16[34,16,256]{2,1,0:T(8,128)(2,1)S(1)}, u32[]{:S(2)}, u32[]{:S(2)}) collective-permute-start(bf16[34,16,256]{2,1,0:T(8,128)(2,1)S(1)} %get-tuple-element.25.sent2), channel_id=1, source_target_pairs={{0,1},{1,0},{2,3},{3,2},{4,5},{5,4},{6,7},{7,6},{8,9},{9,8},{10,11... | collective-permute-start | bytes 835592 | tf_op jit(solution)/shard_map/ppermute | solution.py:48
  20.5 0.8 %prep.1 = (f32[2,20,32,256]{3,2,1,0:T(8,128)S(1)}, f32[18,32,256]{2,1,0:T(8,128)S(1)}, f32[2,16,32,256]{3,2,1,0:T(8,128)S(1)}, f32[2,18,32,256]{3,2,1,0:T(8,128)S(1)}, f32[3,14,32,256]{3,2,1,0:T(8,128)S(1)}) custom-call(f32[2,8,16,256]{3,2,1,0:T(8,128)S(1)} %get-tuple-element.20.x0, f32[8,16,256]{2,1,0:T(8,128)S(1)} %get-tuple-element.21.cond, ...), custom_call_target="tpu_custom_call" | custom-call | tf_op jit(solution)/shard_map/prep/pallas_call | solution.py:252
  21.2 0.0 collective-permute-done.3.second
  21.3 0.4 collective-permute-done.2.first
  21.6 10.4 %chain.1 = (f32[2,20,32,256]{3,2,1,0:T(8,128)S(1)}, f32[18,32,256]{2,1,0:T(8,128)S(1)}, f32[2,16,32,256]{3,2,1,0:T(8,128)S(1)}, f32[2,18,32,256]{3,2,1,0:T(8,128...) custom-call(f32[2,20,32,256]{3,2,1,0:T(8,128)S(1)} %get-tuple-elemen, ...), custom_call_target="tpu_custom_call", output_to_operand_aliasing={{0}: (0, {}), {1}: (1, {}), {2}: (2, {}), {3}: (3, {}), {4}... | custom-call | tf_op jit(solution)/shard_map/chain/pallas_call | solution.py:491
  32.0 16.0 %all_to_all.5.every = f32[32,2,128]{2,1,0:T(2,128)S(1)} all-to-all(f32[32,2,128]{2,1,0:T(2,128)S(1)} %get-tuple-element.32), channel_id=1, replica_groups=mesh['brick'=8,'depth'=4] {'brick','depth'}, dimensions={0} | all-to-all | bytes 65536 | tf_op jit(solution)/shard_map/all_to_all | solution.py:658
  48.1 0.0 copy-start
  48.1 0.0 copy-start.1
  48.1 1.5 %combine.1 = (f32[2,8,16,256]{3,2,1,0:T(8,128)}, bf16[8,16,256]{2,1,0:T(8,128)(2,1)S(1)}) custom-call(f32[32,2,128]{2,1,0:T(2,128)S(1)} %all_to_all.5.every, f32[2,8,16,256]{3,2,1,0:T(8,128)S(1)} %get-tuple-element.20.x0, f32[2,8,16,256]{3,2,1,0:T(8,128)S(1)} %get-tuple-element.22.a0, f32[3,2,8,16,256]{4,3,2,1,0:T(8,128)S(1)} %get-tuple-element.33.v, ...), custom_call_target="tpu_custom_call" | custom-call | tf_op jit(solution)/shard_map/combine/pallas_call | solution.py:577
  49.6 5.8 %all-gather = bf16[32,16,256]{2,1,0:T(8,128)(2,1)S(1)} all-gather(bf16[8,16,256]{2,1,0:T(8,128)(2,1)S(1)} %get-tuple-element.36.own), channel_id=2, replica_groups=mesh['brick'=8,'depth'=4] {'depth'}, dimensions={0}, use_global_device_ids=true | all-gather | bytes 327680 | tf_op jit(solution)/shard_map/all_gather | solution.py:660
  55.3 0.0 copy-done
  55.3 0.0 copy-done.1
  55.3 4.0 %covariance.1 = f32[128,256]{1,0:T(8,128)} custom-call(s32[16]{0:T(128)S(1)} %bitcast.10, s32[1,16]{1,0:T(1,128)S(1)} %bitcast.11, bf16[4,8,16,256]{3,2,1,0:T(8,128)(2,1)S(1)} %bitcast.9, bf16[8,16,256]{2,1,0:T(8,128)(2,1)S(1)} %get-tuple-element.36.own, bf16[16,512,512]{2,1,0:T(8,128)(2,1)S(1)} %get-tuple-element.37.blocks), custom_call_target="tpu_custom_call" | custom-call | tf_op jit(solution)/shard_map/covariance/pallas_call | solution.py:624
Async XLA Ops:
  1.9 6.5 %collective-permute-start.1 = (bf16[26,16,256]{2,1,0:T(8,128)(2,1)S(1)}, bf16[26,16,256]{2,1,0:T(8,128)(2,1)S(1)}, u32[]{:S(2)}, u32[]{:S(2)}) collective-permute-start(bf16[26,16,256]{2,1,0:T(8,128)(2,1)S(1)} %get-tuple-element.24), channel_id=1, source_target_pairs={{4,8},{8,4},{12,16},{16,12},{20,24},{24,20},{5,9},{9,5},{13,17},{1... | collective-permute-start | bytes 638984 | tf_op jit(solution)/shard_map/ppermute | solution.py:48
  2.5 14.2 %collective-permute-start = (bf16[26,16,256]{2,1,0:T(8,128)(2,1)S(1)}, bf16[26,16,256]{2,1,0:T(8,128)(2,1)S(1)}, u32[]{:S(2)}, u32[]{:S(2)}) collective-permute-start(bf16[26,16,256]{2,1,0:T(8,128)(2,1)S(1)} %get-tuple-element.23.sent), channel_id=1, source_target_pairs={{0,4},{4,0},{8,12},{12,8},{16,20},{20,16},{24,28},{28,24},{1,5},{5... | collective-permute-start | bytes 638984 | tf_op jit(solution)/shard_map/ppermute | solution.py:48
  16.9 4.4 %collective-permute-start.3 = (bf16[34,16,256]{2,1,0:T(8,128)(2,1)S(1)}, bf16[34,16,256]{2,1,0:T(8,128)(2,1)S(1)}, u32[]{:S(2)}, u32[]{:S(2)}) collective-permute-start(bf16[34,16,256]{2,1,0:T(8,128)(2,1)S(1)} %get-tuple-element.31), channel_id=1, source_target_pairs={{1,2},{2,1},{5,6},{6,5},{9,10},{10,9},{13,14},{14,13},{17,18},{18,... | collective-permute-start | bytes 835592 | tf_op jit(solution)/shard_map/ppermute | solution.py:48
  17.6 4.1 %collective-permute-start.2 = (bf16[34,16,256]{2,1,0:T(8,128)(2,1)S(1)}, bf16[34,16,256]{2,1,0:T(8,128)(2,1)S(1)}, u32[]{:S(2)}, u32[]{:S(2)}) collective-permute-start(bf16[34,16,256]{2,1,0:T(8,128)(2,1)S(1)} %get-tuple-element.25.sent2), channel_id=1, source_target_pairs={{0,1},{1,0},{2,3},{3,2},{4,5},{5,4},{6,7},{7,6},{8,9},{9,8},{10,11... | collective-permute-start | bytes 835592 | tf_op jit(solution)/shard_map/ppermute | solution.py:48
  48.1 7.3 %copy-start = (s32[1,1,16]{2,1,0:T(1,128)S(1)}, s32[1,1,16]{2,1,0:T(1,128)}, u32[]{:S(2)}) copy-start(s32[1,1,16]{2,1,0:T(1,128)} %param.19) | copy-start | bytes 196
  48.1 7.3 %copy-start.1 = (s32[1,1,16]{2,1,0:T(1,128)S(1)}, s32[1,1,16]{2,1,0:T(1,128)}, u32[]{:S(2)}) copy-start(s32[1,1,16]{2,1,0:T(1,128)} %param.18) | copy-start | bytes 196

commit v6 on v5

--- a/solution.py
+++ b/solution.py
@@ -133,7 +133,7 @@
     return fields, reader(lambda i: cond[i], LC, HC), adjoints, low, high
 
 
-def mid_kernel(x0, cond, a0, sent, first, second, out_first, out_second):
+def mid_kernel(x0, cond, a0, sent, first, second, _, out_first, out_second):
     size_x, size_z, size_y = cond.shape
     fields, conds, adjoints, low, high = joined_rows(x0, cond, a0, first, second)
     odd = is_odd("depth")
@@ -167,17 +167,17 @@
     return (size_x + 2 * HX - 2) + (size_x + 2 * HC - 2) // 2 + (size_x + 2 * HA - 2) // 2 + 1
 
 
-def mid(x0, cond, a0, sent, first, second):
+def mid(x0, cond, a0, sent, first, second, ready):
     size_x, size_z, size_y = cond.shape
     shape = (depth_layers(size_x), size_z, size_y)
     return pl.pallas_call(
         mid_kernel,
         out_shape=(jax.ShapeDtypeStruct(shape, jnp.bfloat16),) * 2,
-        in_specs=[VMEM] * 6,
+        in_specs=[VMEM] * 7,
         out_specs=(VMEM, VMEM),
         compiler_params=PARAMS,
         name="mid",
-    )(x0, cond, a0, sent, first, second)
+    )(x0, cond, a0, sent, first, second, held(ready))
 
 
 def place(t, q, weights, halo, dst, lists, size_x, size_z, size_y):
@@ -274,11 +274,9 @@
     return total + jnp.concatenate([ya, yb], axis=1)
 
 
-def chain_kernel(size_x, size_z, x0_in, cond_in, a0_in, src_in, rec_in, first, second, blocks,
-                 x0, cond, a0, src, rec, v_out, w_out, sums_out, blocks_out,
-                 v0, v1, v2, u, w1, w2, w3, acc, sem):
-    prefetch = pltpu.make_async_copy(blocks, blocks_out, sem)
-    prefetch.start()
+def chain_kernel(size_x, size_z, x0_in, cond_in, a0_in, src_in, rec_in, first, second,
+                 x0, cond, a0, src, rec, v_out, w_out, sums_out,
+                 v0, v1, v2, u, w1, w2, w3, acc):
     rows_z = x0.shape[-2]
     size_y = x0.shape[-1]
     own = slice(ZP, ZP + size_z)
@@ -347,6 +345,10 @@
     def loop(n, body, unroll):
         while n % unroll:
             unroll -= 1
+        if n == unroll:
+            for j in range(n):
+                body(j)
+            return
 
         def step(i, carry):
             for j in range(unroll):
@@ -417,7 +419,7 @@
 
     zero = jnp.zeros((8, 128), jnp.float32)
 
-    def over_rows(body, carry, unroll=2):
+    def over_rows(body, carry, unroll=8):
         def step(i, carry):
             for j in range(unroll):
                 carry = body(i * unroll + j, carry)
@@ -464,10 +466,9 @@
     out = lax.dot_general(ones, by_lane, NT, precision=lax.Precision.HIGHEST, preferred_element_type=jnp.float32)
     out = jnp.concatenate([out[0:1, :128], out[0:1, 128:]], axis=0)
     sums_out[...] = jnp.broadcast_to(out[None], sums_out.shape)
-    prefetch.wait()
-
-
-def chain(wide, first, second, blocks, size_x, size_z, n_dev):
+
+
+def chain(wide, first, second, size_x, size_z, n_dev):
     size_y = wide[0].shape[-1]
     f32 = jnp.float32
     slab = (size_z + 2 * ZP, size_y)
@@ -475,7 +476,6 @@
         pltpu.VMEM((3, 2, size_x, size_z, size_y), f32),
         pltpu.VMEM((3, 4, 2, size_x, size_z, size_y), f32),
         jax.ShapeDtypeStruct((n_dev, 2, 128), f32),
-        pltpu.VMEM(blocks.shape, blocks.dtype),
     )
     scratch = [
         pltpu.VMEM((2, size_x + 2 * HC) + slab, f32),
@@ -486,18 +486,17 @@
         pltpu.VMEM((4, 2, size_x + 2) + slab, f32),
         pltpu.VMEM((4, 2, size_x, size_z, size_y), f32),
         pltpu.VMEM((256, 8, 128), f32),
-        pltpu.SemaphoreType.DMA,
     ]
     return pl.pallas_call(
         functools.partial(chain_kernel, size_x, size_z),
         out_shape=outs,
-        in_specs=[VMEM] * 7 + [HBM],
-        out_specs=(VMEM,) * 9,
+        in_specs=[VMEM] * 7,
+        out_specs=(VMEM,) * 8,
         scratch_shapes=scratch,
         input_output_aliases={i: i for i in range(5)},
         compiler_params=PARAMS,
         name="chain",
-    )(*[held(a) for a in wide], first, second, in_hbm(blocks))[5:]
+    )(*[held(a) for a in wide], first, second)[5:]
 
 
 def coefficients(mu):
@@ -587,36 +586,61 @@
     )(every, x0, a0, held(v), held(w))
 
 
-def covariance_kernel(cols, rows, every, own, blocks, out, wide):
+def turn_kernel(blocks, out, buf, sems):
+    n = buf.shape[0]
+    copies = [pltpu.make_async_copy(blocks.at[k], buf.at[k], sems.at[k]) for k in range(n)]
+    for copy in copies:
+        copy.start()
+    for k, copy in enumerate(copies):
+        copy.wait()
+        out[k] = buf[k].T
+
+
+def turn(blocks):
+    return pl.pallas_call(
+        turn_kernel,
+        out_shape=pltpu.VMEM(blocks.shape, blocks.dtype),
+        in_specs=[HBM],
+        out_specs=VMEM,
+        scratch_shapes=[
+            pltpu.VMEM(blocks.shape, blocks.dtype),
+            pltpu.SemaphoreType.DMA((blocks.shape[0],)),
+        ],
+        compiler_params=PARAMS,
+        name="turn",
+    )(in_hbm(blocks))
+
+
+def covariance_kernel(cols, rows, every, own, blocks, out):
     n_dev, size_x, size_z, width = every.shape
     n_rows = size_x * size_z
     n_blocks, size, _ = blocks.shape
     per = size // width
-    for d in range(n_dev):
-        wide[d * n_rows : (d + 1) * n_rows, :] = every[d].reshape(n_rows, width).astype(jnp.float32)
-    picked = jnp.concatenate(
-        [
-            jnp.concatenate([wide[pl.ds(cols[k] * per + i, 1), :] for i in range(per)], axis=1)
-            for k in range(n_blocks)
-        ],
-        axis=0,
-    ).astype(jnp.bfloat16)
+    table = every[...].reshape(n_dev * n_rows, width)
+    at = lax.broadcasted_iota(jnp.int32, (n_dev * n_rows, n_blocks), 0)
+    hits = jnp.concatenate([jnp.where(at == cols[...] * per + i, 1.0, 0.0) for i in range(per)], axis=1)
+    picked = lax.dot_general(
+        hits.astype(jnp.bfloat16), table, (((0,), (0,)), ((), ())), preferred_element_type=jnp.float32
+    )
+    picked = jnp.concatenate([picked[i * n_blocks : (i + 1) * n_blocks] for i in range(per)], axis=1)
+    picked = picked.astype(jnp.bfloat16)
     which = lax.broadcasted_iota(jnp.int32, (n_blocks, size), 0)
     terms = jnp.zeros((n_blocks, size), jnp.float32)
     for k in range(n_blocks):
-        product = lax.dot_general(picked, blocks[k], NT, preferred_element_type=jnp.float32)
-        terms = jnp.where(which == k, product, terms)
-    total = own[...].reshape(n_rows, width).astype(jnp.float32)
+        terms = jnp.where(which == k, jnp.dot(picked, blocks[k], preferred_element_type=jnp.float32), terms)
+    one = terms.astype(jnp.bfloat16)
+    rest = terms - one.astype(jnp.float32)
+    two = rest.astype(jnp.bfloat16)
+    three = (rest - two.astype(jnp.float32)).astype(jnp.bfloat16)
+    right = jnp.concatenate(
+        [p[:, i * width : (i + 1) * width] for p in (one, two, three) for i in range(per)], axis=0
+    )
     at = lax.broadcasted_iota(jnp.int32, (n_rows, n_blocks), 0)
-    for i in range(per):
-        hit = jnp.where(at == rows[...] * per + i, 1.0, 0.0)
-        total = total + jnp.dot(
-            hit,
-            terms[:, i * width : (i + 1) * width],
-            precision=lax.Precision.HIGHEST,
-            preferred_element_type=jnp.float32,
-        )
-    out[...] = total
+    hits = [jnp.where(at == rows[...] * per + i, 1.0, 0.0) for i in range(per)]
+    left = jnp.concatenate(hits * 3, axis=1).astype(jnp.bfloat16)
+    out[...] = own[...].reshape(n_rows, width).astype(jnp.float32) + jnp.dot(
+        left, right, preferred_element_type=jnp.float32
+    )
 
 
 def covariance(cols, rows, every, own, blocks):
@@ -624,9 +648,8 @@
     return pl.pallas_call(
         covariance_kernel,
         out_shape=jax.ShapeDtypeStruct((size_x * size_z, width), jnp.float32),
-        in_specs=[SMEM, VMEM, VMEM, VMEM, VMEM],
+        in_specs=[VMEM] * 5,
         out_specs=VMEM,
-        scratch_shapes=[pltpu.VMEM((n_dev * size_x * size_z, width), jnp.float32)],
         compiler_params=PARAMS,
         name="covariance",
     )(cols, rows, every, own, held(blocks))
@@ -651,14 +674,15 @@
     )
     x0, cond, a0 = held(x0), held(cond), held(a0)
     first, second = swap(*sent, "brick")
-    sent2 = mid(x0, cond, a0, sent[0], first, second)
+    blocks = turn(cov_blocks[0, 0])
+    sent2 = mid(x0, cond, a0, sent[0], first, second, blocks)
     wide = prep(x0, cond, a0, sent2[0], first, second)
     first2, second2 = swap(*sent2, "depth")
-    v, w, sums, blocks = chain(wide, first2, second2, cov_blocks[0, 0], size_x, size_z, n_dev)
+    v, w, sums = chain(wide, first2, second2, size_x, size_z, n_dev)
     every = lax.all_to_all(sums, BOTH, 0, 0, tiled=True)
     forward, gradient = combine(every, x0, a0, v, w)
     every_block = lax.all_gather(gradient, "depth", axis=0, tiled=False)
-    out = covariance(cov_cols[0, 0], cov_rows[0], every_block, gradient, blocks)
+    out = covariance(cov_cols[0], cov_rows[0], every_block, gradient, blocks)
     return (forward, out.reshape(size_x, size_z, size_y))
 
 

time: 59.6 us -> 57 us (0.956)
  waiting for transfers between devices: 8.76 us -> 4.51 us
  Pallas kernels: 18.1 us -> 19.7 us
    ppermute x4, waiting for transfers between devices: 8.76 us -> 4.51 us  [swap(): return (lax.ppermute(first, axis, one), lax.ppermute(second, axis, two))]
    pallas_call x0 -> x1, Pallas kernels: none -> 4.23 us  [turn(): pl.pallas_call(turn_kernel, out_shape=pltpu.VMEM(blocks.shape, blocks.dty...]
    pallas_call x1, Pallas kernels: 4.03 us -> 2.27 us  [covariance(): pl.pallas_call(covariance_kernel, out_shape=jax.ShapeDtypeStruct((size_x...]
    pallas_call x1, Pallas kernels: 10.4 us -> 9.59 us  [chain(): pl.pallas_call(functools.partial(chain_kernel, size_x, size_z), out_shape...]
  transfers between devices with their start and end apart: 4 -> 4, of which waited for: 2 -> 2; matrix products, arithmetic and copies ran while one was open for 0% -> 0% of each run, Pallas kernels for 1% -> 9%
where the time goes in v6:
time: 57 us; the launch traced here: 56.8 us
  blocking collectives  21.8 us (38%)
  Pallas kernels  19.7 us (35%)
  starting transfers between devices  10.1 us (18%)
  waiting for transfers between devices  4.51 us (8%)
  between operations  0.7 us (1%)
    all_to_all x1, blocking collectives, local(): every = lax.all_to_all(sums, BOTH, 0, 0, tiled=True)  16 us
    ppermute x4, starting transfers between devices, swap(): return (lax.ppermute(first, axis, one), lax.ppermute(second, axis, two))  10.1 us
    pallas_call x1, Pallas kernels, chain(): pl.pallas_call(functools.partial(chain_kernel, size_x, size_z), out_shape...  9.59 us
    all_gather x1, blocking collectives, local(): every_block = lax.all_gather(gradient, 'depth', axis=0, tiled=False)  5.76 us
    ppermute x4, waiting for transfers between devices, swap(): return (lax.ppermute(first, axis, one), lax.ppermute(second, axis, two))  4.51 us
    pallas_call x1, Pallas kernels, turn(): pl.pallas_call(turn_kernel, out_shape=pltpu.VMEM(blocks.shape, blocks.dty...  4.23 us
    pallas_call x1, Pallas kernels, covariance(): pl.pallas_call(covariance_kernel, out_shape=jax.ShapeDtypeStruct((size_x...  2.27 us
    pallas_call x1, Pallas kernels, combine(): pl.pallas_call(combine_kernel, out_shape=(jax.ShapeDtypeStruct(x0.shape,...  1.5 us
  transfers between devices with their start and end apart: 4, of which 2 were waited for; matrix products, arithmetic and copies ran while one was open for 0% of the time, Pallas kernels for 9%

profile of v6, /device:TPU:0, one launch (start us, length us, event | category | flops | bytes accessed | tf_op | source)
XLA Modules:
  0.0 56.8 jit_solution(9482444959442448137)
XLA Ops:
  0.6 1.2 %pack.1 = (bf16[26,16,256]{2,1,0:T(8,128)(2,1)S(1)}, bf16[26,16,256]{2,1,0:T(8,128)(2,1)S(1)}, f32[2,8,16,256]{3,2,1,0:T(8,128)S(1)}, f32[8,16,256]{2,1,0:T(8,128)S(1)}, f32[2,8,16,256]{3,2,1,0:T(8,128)S(1)}) custom-call(f32[2,8,16,256]{3,2,1,0:T(8,128)} %refs_0_.1, f32[8,16,256]{2,1,0:T(8,128)} %refs_1_.1, f32[2,8,16,256]{3,2,1,0:T(8,128)} %refs_2_.1, ...), custom_call_target="tpu_custom_call" | custom-call | tf_op jit(solution)/shard_map/pack/pallas_call | solution.py:99
  1.9 0.7 %collective-permute-start.1 = (bf16[26,16,256]{2,1,0:T(8,128)(2,1)S(1)}, bf16[26,16,256]{2,1,0:T(8,128)(2,1)S(1)}, u32[]{:S(2)}, u32[]{:S(2)}) collective-permute-start(bf16[26,16,256]{2,1,0:T(8,128)(2,1)S(1)} %get-tuple-element.23), channel_id=1, source_target_pairs={{4,8},{8,4},{12,16},{16,12},{20,24},{24,20},{5,9},{9,5},{13,17},{1... | collective-permute-start | bytes 638984 | tf_op jit(solution)/shard_map/ppermute | solution.py:48
  2.5 5.8 %collective-permute-start = (bf16[26,16,256]{2,1,0:T(8,128)(2,1)S(1)}, bf16[26,16,256]{2,1,0:T(8,128)(2,1)S(1)}, u32[]{:S(2)}, u32[]{:S(2)}) collective-permute-start(bf16[26,16,256]{2,1,0:T(8,128)(2,1)S(1)} %get-tuple-element.22.sent), channel_id=1, source_target_pairs={{0,4},{4,0},{8,12},{12,8},{16,20},{20,16},{24,28},{28,24},{1,5},{5... | collective-permute-start | bytes 638984 | tf_op jit(solution)/shard_map/ppermute | solution.py:48
  8.4 4.2 %turn.1._.blocks = bf16[16,512,512]{2,1,0:T(8,128)(2,1)S(1)} custom-call(bf16[16,512,512]{2,1,0:T(8,128)(2,1)} %bitcast.12), custom_call_target="tpu_custom_call" | custom-call | tf_op jit(solution)/shard_map/turn/pallas_call | solution.py:600
  12.6 0.0 collective-permute-done.1.second
  12.6 4.1 %collective-permute-done.first = bf16[26,16,256]{2,1,0:T(8,128)(2,1)S(1)} collective-permute-done((bf16[26,16,256]{2,1,0:T(8,128)(2,1)S(1)}, bf16[26,16,256]{2,1,0:T(8,128)(2,1)S(1)}, u32[]{:S(2)}, u32[]{:S(2)}) %collective-permute-start) | collective-permute-done | bytes 213024 | tf_op jit(solution)/shard_map/ppermute | solution.py:48
  16.7 0.1 mid.1
  16.9 0.7 %collective-permute-start.3 = (bf16[34,16,256]{2,1,0:T(8,128)(2,1)S(1)}, bf16[34,16,256]{2,1,0:T(8,128)(2,1)S(1)}, u32[]{:S(2)}, u32[]{:S(2)}) collective-permute-start(bf16[34,16,256]{2,1,0:T(8,128)(2,1)S(1)} %get-tuple-element.30), channel_id=1, source_target_pairs={{1,2},{2,1},{5,6},{6,5},{9,10},{10,9},{13,14},{14,13},{17,18},{18,... | collective-permute-start | bytes 835592 | tf_op jit(solution)/shard_map/ppermute | solution.py:48
  17.6 2.9 %collective-permute-start.2 = (bf16[34,16,256]{2,1,0:T(8,128)(2,1)S(1)}, bf16[34,16,256]{2,1,0:T(8,128)(2,1)S(1)}, u32[]{:S(2)}, u32[]{:S(2)}) collective-permute-start(bf16[34,16,256]{2,1,0:T(8,128)(2,1)S(1)} %get-tuple-element.24.sent2), channel_id=1, source_target_pairs={{0,1},{1,0},{2,3},{3,2},{4,5},{5,4},{6,7},{7,6},{8,9},{9,8},{10,11... | collective-permute-start | bytes 835592 | tf_op jit(solution)/shard_map/ppermute | solution.py:48
  20.5 0.8 %prep.1 = (f32[2,20,32,256]{3,2,1,0:T(8,128)S(1)}, f32[18,32,256]{2,1,0:T(8,128)S(1)}, f32[2,16,32,256]{3,2,1,0:T(8,128)S(1)}, f32[2,18,32,256]{3,2,1,0:T(8,128)S(1)}, f32[3,14,32,256]{3,2,1,0:T(8,128)S(1)}) custom-call(f32[2,8,16,256]{3,2,1,0:T(8,128)S(1)} %get-tuple-element.19.x0, f32[8,16,256]{2,1,0:T(8,128)S(1)} %get-tuple-element.20.cond, ...), custom_call_target="tpu_custom_call" | custom-call | tf_op jit(solution)/shard_map/prep/pallas_call | solution.py:252
  21.2 0.0 collective-permute-done.3.second
  21.3 0.4 collective-permute-done.2.first
  21.6 9.6 %chain.1 = (f32[2,20,32,256]{3,2,1,0:T(8,128)S(1)}, f32[18,32,256]{2,1,0:T(8,128)S(1)}, f32[2,16,32,256]{3,2,1,0:T(8,128)S(1)}, f32[2,18,32,256]{3,2,1,0:T(8,128...) custom-call(f32[2,20,32,256]{3,2,1,0:T(8,128)S(1)} %get-tuple-elemen, ...), custom_call_target="tpu_custom_call", output_to_operand_aliasing={{0}: (0, {}), {1}: (1, {}), {2}: (2, {}), {3}: (3, {}), {4}... | custom-call | tf_op jit(solution)/shard_map/chain/pallas_call | solution.py:490
  31.2 16.0 %all_to_all.5.every = f32[32,2,128]{2,1,0:T(2,128)S(1)} all-to-all(f32[32,2,128]{2,1,0:T(2,128)S(1)} %get-tuple-element.31), channel_id=1, replica_groups=mesh['brick'=8,'depth'=4] {'brick','depth'}, dimensions={0} | all-to-all | bytes 65536 | tf_op jit(solution)/shard_map/all_to_all | solution.py:682
  47.3 0.0 copy-start
  47.3 0.0 copy-start.1
  47.3 1.5 %combine.1 = (f32[2,8,16,256]{3,2,1,0:T(8,128)}, bf16[8,16,256]{2,1,0:T(8,128)(2,1)S(1)}) custom-call(f32[32,2,128]{2,1,0:T(2,128)S(1)} %all_to_all.5.every, f32[2,8,16,256]{3,2,1,0:T(8,128)S(1)} %get-tuple-element.19.x0, f32[2,8,16,256]{3,2,1,0:T(8,128)S(1)} %get-tuple-element.21.a0, f32[3,2,8,16,256]{4,3,2,1,0:T(8,128)S(1)} %get-tuple-element.32.v, ...), custom_call_target="tpu_custom_call" | custom-call | tf_op jit(solution)/shard_map/combine/pallas_call | solution.py:576
  48.8 5.8 %all-gather = bf16[32,16,256]{2,1,0:T(8,128)(2,1)S(1)} all-gather(bf16[8,16,256]{2,1,0:T(8,128)(2,1)S(1)} %get-tuple-element.35.own), channel_id=2, replica_groups=mesh['brick'=8,'depth'=4] {'depth'}, dimensions={0}, use_global_device_ids=true | all-gather | bytes 327680 | tf_op jit(solution)/shard_map/all_gather | solution.py:684
  54.5 0.0 copy-done
  54.5 0.0 copy-done.1
  54.5 2.3 %covariance.1 = f32[128,256]{1,0:T(8,128)} custom-call(s32[1,16]{1,0:T(1,128)S(1)} %bitcast.10, s32[1,16]{1,0:T(1,128)S(1)} %bitcast.11, bf16[4,8,16,256]{3,2,1,0:T(8,128)(2,1)S(1)} %bitcast.9, bf16[8,16,256]{2,1,0:T(8,128)(2,1)S(1)} %get-tuple-element.35.own, bf16[16,512,512]{2,1,0:T(8,128)(2,1)S(1)} %turn.1._.blocks), custom_call_target="tpu_custom_call" | custom-call | tf_op jit(solution)/shard_map/covariance/pallas_call | solution.py:648
Async XLA Ops:
  1.9 10.7 %collective-permute-start.1 = (bf16[26,16,256]{2,1,0:T(8,128)(2,1)S(1)}, bf16[26,16,256]{2,1,0:T(8,128)(2,1)S(1)}, u32[]{:S(2)}, u32[]{:S(2)}) collective-permute-start(bf16[26,16,256]{2,1,0:T(8,128)(2,1)S(1)} %get-tuple-element.23), channel_id=1, source_target_pairs={{4,8},{8,4},{12,16},{16,12},{20,24},{24,20},{5,9},{9,5},{13,17},{1... | collective-permute-start | bytes 638984 | tf_op jit(solution)/shard_map/ppermute | solution.py:48
  2.5 14.2 %collective-permute-start = (bf16[26,16,256]{2,1,0:T(8,128)(2,1)S(1)}, bf16[26,16,256]{2,1,0:T(8,128)(2,1)S(1)}, u32[]{:S(2)}, u32[]{:S(2)}) collective-permute-start(bf16[26,16,256]{2,1,0:T(8,128)(2,1)S(1)} %get-tuple-element.22.sent), channel_id=1, source_target_pairs={{0,4},{4,0},{8,12},{12,8},{16,20},{20,16},{24,28},{28,24},{1,5},{5... | collective-permute-start | bytes 638984 | tf_op jit(solution)/shard_map/ppermute | solution.py:48
  16.9 4.4 %collective-permute-start.3 = (bf16[34,16,256]{2,1,0:T(8,128)(2,1)S(1)}, bf16[34,16,256]{2,1,0:T(8,128)(2,1)S(1)}, u32[]{:S(2)}, u32[]{:S(2)}) collective-permute-start(bf16[34,16,256]{2,1,0:T(8,128)(2,1)S(1)} %get-tuple-element.30), channel_id=1, source_target_pairs={{1,2},{2,1},{5,6},{6,5},{9,10},{10,9},{13,14},{14,13},{17,18},{18,... | collective-permute-start | bytes 835592 | tf_op jit(solution)/shard_map/ppermute | solution.py:48
  17.6 4.1 %collective-permute-start.2 = (bf16[34,16,256]{2,1,0:T(8,128)(2,1)S(1)}, bf16[34,16,256]{2,1,0:T(8,128)(2,1)S(1)}, u32[]{:S(2)}, u32[]{:S(2)}) collective-permute-start(bf16[34,16,256]{2,1,0:T(8,128)(2,1)S(1)} %get-tuple-element.24.sent2), channel_id=1, source_target_pairs={{0,1},{1,0},{2,3},{3,2},{4,5},{5,4},{6,7},{7,6},{8,9},{9,8},{10,11... | collective-permute-start | bytes 835592 | tf_op jit(solution)/shard_map/ppermute | solution.py:48
  47.3 7.3 %copy-start = (s32[1,1,16]{2,1,0:T(1,128)S(1)}, s32[1,1,16]{2,1,0:T(1,128)}, u32[]{:S(2)}) copy-start(s32[1,1,16]{2,1,0:T(1,128)} %param.19) | copy-start | bytes 196
  47.3 7.3 %copy-start.1 = (s32[1,1,16]{2,1,0:T(1,128)S(1)}, s32[1,1,16]{2,1,0:T(1,128)}, u32[]{:S(2)}) copy-start(s32[1,1,16]{2,1,0:T(1,128)} %param.18) | copy-start | bytes 196

commit v7 on v6

--- a/solution.py
+++ b/solution.py
@@ -53,8 +53,8 @@
 
 
 def pack_kernel(*refs):
-    ins, (first, second), kept, pieces = refs[:7], refs[7:9], refs[9:12], refs[12:16]
-    table, sems = refs[16:]
+    ins, (first, second), sides, kept, pieces = refs[:7], refs[7:9], refs[9:11], refs[11:14], refs[14:18]
+    table, sems = refs[18:]
     copies = [
         pltpu.make_async_copy(a, b, sems.at[i]) for i, (a, b) in enumerate(zip(ins, kept + pieces))
     ]
@@ -64,7 +64,7 @@
         copy.wait()
     x0, cond, a0 = kept
     src_cell, src_amp, rec_cell, observed = pieces
-    size_x, _, size_y = cond.shape
+    size_x, size_z, size_y = cond.shape
     odd = is_odd("brick")
 
     def split(v):
@@ -91,6 +91,93 @@
         for i in range(HC):
             out[LC + i] = cond[jnp.where(low, i, size_x - HC + i)].astype(jnp.bfloat16)
         out[LP] = points
+    put = depth_writer(*sides, size_z)
+    fill_depth(
+        put,
+        [[(lambda i, f=f: x0[f, i]) for f in range(2)], lambda i: cond[i], [(lambda i, f=f: a0[f, i]) for f in range(2)]],
+        [list(range(size_x))] * 3,
+        size_z,
+    )
+
+
+def depth_writer(out_first, out_second, size_z):
+    odd = is_odd("depth")
+
+    def put(at, down, up):
+        down = jnp.concatenate(down, axis=0)
+        up = jnp.concatenate(up, axis=0)
+        out_first[at] = jnp.where(odd, down, up).astype(jnp.bfloat16)
+        out_second[at] = jnp.where(odd, up, down).astype(jnp.bfloat16)
+
+    return put
+
+
+def fill_depth(put, readers, chosen, size_z):
+    fields, conds, adjoints = readers
+    at = 0
+    for i in chosen[0]:
+        rows = [r(i) for r in fields]
+        put(at, [r[:ZP] for r in rows], [r[size_z - ZP :] for r in rows])
+        at += 1
+    for i, j in zip(chosen[1][::2], chosen[1][1::2]):
+        rows = [conds(i), conds(j)]
+        put(at, [r[:ZP] for r in rows], [r[size_z - ZP :] for r in rows])
+        at += 1
+    for i, j in zip(chosen[2][::2], chosen[2][1::2]):
+        rows = [r(n) for n in (i, j) for r in adjoints]
+        put(at, [r[:HA] for r in rows], [r[size_z - HA :] for r in rows])
+        at += 1
+    return at
+
+
+def empty_depth(x0, cond, a0, chosen, low, high, top):
+    gap = jnp.zeros((ZP - HA, x0.shape[-1]), jnp.float32)
+    at = 0
+    for i in chosen[0]:
+        a, b = low(at), high(at)
+        for f in range(2):
+            x0[f, i, 0:ZP] = a[f * ZP : (f + 1) * ZP]
+            x0[f, i, top : top + ZP] = b[f * ZP : (f + 1) * ZP]
+        at += 1
+    for pair in zip(chosen[1][::2], chosen[1][1::2]):
+        a, b = low(at), high(at)
+        for n, i in enumerate(pair):
+            cond[i, 0:ZP] = a[n * ZP : (n + 1) * ZP]
+            cond[i, top : top + ZP] = b[n * ZP : (n + 1) * ZP]
+        at += 1
+    for pair in zip(chosen[2][::2], chosen[2][1::2]):
+        a, b = low(at), high(at)
+        for n, i in enumerate(pair):
+            for f in range(2):
+                part = slice((2 * n + f) * HA, (2 * n + f + 1) * HA)
+                a0[f, i, 0:ZP] = jnp.concatenate([gap, a[part]], axis=0)
+                a0[f, i, top : top + ZP] = jnp.concatenate([b[part], gap], axis=0)
+        at += 1
+    return at
+
+
+def own_rows(size_x):
+    return [list(range(h, h + size_x)) for h in (HX, HC, HA)]
+
+
+def corner_rows(size_x):
+    return [list(range(1, h)) + list(range(h + size_x, size_x + 2 * h - 1)) for h in (HX, HC, HA)]
+
+
+def tiles_of(chosen):
+    return len(chosen[0]) + len(chosen[1]) // 2 + len(chosen[2]) // 2
+
+
+def sides_of(axis, first, second):
+    odd = is_odd(axis)
+
+    def low(at):
+        return jnp.where(odd, first[at].astype(jnp.float32), second[at].astype(jnp.float32))
+
+    def high(at):
+        return jnp.where(odd, second[at].astype(jnp.float32), first[at].astype(jnp.float32))
+
+    return low, high
 
 
 def pack(*ins):
@@ -99,9 +186,10 @@
     return pl.pallas_call(
         pack_kernel,
         out_shape=(jax.ShapeDtypeStruct(shape, jnp.bfloat16),) * 2
+        + (jax.ShapeDtypeStruct((tiles_of(own_rows(cond.shape[0])),) + shape[1:], jnp.bfloat16),) * 2
         + tuple(pltpu.VMEM(a.shape, a.dtype) for a in ins[:3]),
         in_specs=[HBM] * 7,
-        out_specs=(VMEM,) * 5,
+        out_specs=(VMEM,) * 7,
         scratch_shapes=[pltpu.VMEM(a.shape, a.dtype) for a in ins[3:]]
         + [pltpu.VMEM(cond.shape[1:], jnp.float32), pltpu.SemaphoreType.DMA((7,))],
         compiler_params=PARAMS,
@@ -111,13 +199,7 @@
 
 def joined_rows(x0, cond, a0, first, second):
     size_x = cond.shape[0]
-    odd = is_odd("brick")
-
-    def low(at):
-        return jnp.where(odd, first[at].astype(jnp.float32), second[at].astype(jnp.float32))
-
-    def high(at):
-        return jnp.where(odd, second[at].astype(jnp.float32), first[at].astype(jnp.float32))
+    low, high = sides_of("brick", first, second)
 
     def reader(own, base, halo):
         def row(i):
@@ -133,51 +215,30 @@
     return fields, reader(lambda i: cond[i], LC, HC), adjoints, low, high
 
 
-def mid_kernel(x0, cond, a0, sent, first, second, _, out_first, out_second):
+def mid_kernel(x0, cond, a0, sent, first, second, *refs):
+    out_first, out_second = refs[-2:]
     size_x, size_z, size_y = cond.shape
     fields, conds, adjoints, low, high = joined_rows(x0, cond, a0, first, second)
-    odd = is_odd("depth")
     n = size_y // 4
     points = low(LP) + pltpu.roll(sent[LP].astype(jnp.float32), n, 1) + pltpu.roll(high(LP), 2 * n, 1)
-
-    def put(at, down, up):
-        down = jnp.concatenate(down, axis=0)
-        up = jnp.concatenate(up, axis=0)
-        out_first[at] = jnp.where(odd, down, up).astype(jnp.bfloat16)
-        out_second[at] = jnp.where(odd, up, down).astype(jnp.bfloat16)
-
-    at = 0
-    for i in range(1, size_x + 2 * HX - 1):
-        rows = [r(i) for r in fields]
-        put(at, [r[:ZP] for r in rows], [r[size_z - ZP :] for r in rows])
-        at += 1
-    for i in range(1, size_x + 2 * HC - 1, 2):
-        rows = [conds(i), conds(i + 1)]
-        put(at, [r[:ZP] for r in rows], [r[size_z - ZP :] for r in rows])
-        at += 1
-    for i in range(1, size_x + 2 * HA - 1, 2):
-        rows = [r(j) for j in (i, i + 1) for r in adjoints]
-        put(at, [r[:HA] for r in rows], [r[size_z - HA :] for r in rows])
-        at += 1
+    at = fill_depth(
+        depth_writer(out_first, out_second, size_z), [fields, conds, adjoints], corner_rows(size_x), size_z
+    )
     out_first[at] = points.astype(jnp.bfloat16)
     out_second[at] = points.astype(jnp.bfloat16)
 
 
-def depth_layers(size_x):
-    return (size_x + 2 * HX - 2) + (size_x + 2 * HC - 2) // 2 + (size_x + 2 * HA - 2) // 2 + 1
-
-
-def mid(x0, cond, a0, sent, first, second, ready):
+def mid(x0, cond, a0, sent, first, second, *ready):
     size_x, size_z, size_y = cond.shape
-    shape = (depth_layers(size_x), size_z, size_y)
+    shape = (tiles_of(corner_rows(size_x)) + 1, size_z, size_y)
     return pl.pallas_call(
         mid_kernel,
         out_shape=(jax.ShapeDtypeStruct(shape, jnp.bfloat16),) * 2,
-        in_specs=[VMEM] * 7,
+        in_specs=[VMEM] * (6 + len(ready)),
         out_specs=(VMEM, VMEM),
         compiler_params=PARAMS,
         name="mid",
-    )(x0, cond, a0, sent, first, second, held(ready))
+    )(x0, cond, a0, sent, first, second, *[held(a) for a in ready])
 
 
 def place(t, q, weights, halo, dst, lists, size_x, size_z, size_y):
@@ -206,21 +267,22 @@
     target = jnp.where(ok, target, -1)
     hit = lax.broadcasted_iota(jnp.int32, (nx * depth, n_list), 0) == target
     right = (lax.broadcasted_iota(jnp.int32, (size_y, n_list), 0) == lo).astype(jnp.float32).astype(jnp.bfloat16)
-    for at_out, parts in weights:
-        total = None
-        for p in parts:
-            amount = 1.0 if p is None else lists[p : p + 1]
-            left = jnp.where(hit, amount, 0.0).astype(jnp.bfloat16)
-            d = lax.dot_general(left, right, NT, preferred_element_type=jnp.float32)
-            total = d if total is None else total + d
-        dst[at_out, :, z0 : z0 + depth, :] = total.reshape(nx, depth, size_y)
+    terms = [(n, p) for n, parts in weights for p in parts]
+    left = jnp.concatenate([jnp.where(hit, 1.0 if p is None else lists[p : p + 1], 0.0) for _, p in terms], axis=0)
+    placed = lax.dot_general(left.astype(jnp.bfloat16), right, NT, preferred_element_type=jnp.float32)
+    totals = {}
+    for i, (n, _) in enumerate(terms):
+        part = placed[i * nx * depth : (i + 1) * nx * depth]
+        totals[n] = totals[n] + part if n in totals else part
+    for n, total in totals.items():
+        dst[n, :, z0 : z0 + depth, :] = total.reshape(nx, depth, size_y)
 
 
 SRC_WEIGHTS = ((0, (2, 4, 6)), (1, (3, 5, 7)))
 REC_WEIGHTS = ((0, (10, 12, 14)), (1, (11, 13, 15)), (2, (None,)))
 
 
-def prep_kernel(x0, cond, a0, sent2, first, second, x0_w, cond_w, a0_w, src, rec):
+def prep_kernel(x0, cond, a0, sent2, first, second, side_first, side_second, x0_w, cond_w, a0_w, src, rec):
     size_x, size_z, size_y = cond.shape
     fields, conds, adjoints, _, _ = joined_rows(x0, cond, a0, first, second)
     own = slice(ZP, ZP + size_z)
@@ -231,6 +293,7 @@
             a0_w[f, i, own] = adjoints[f](i)
     for i in range(size_x + 2 * HC):
         cond_w[i, own] = conds(i)
+    empty_depth(x0_w, cond_w, a0_w, own_rows(size_x), *sides_of("depth", side_first, side_second), ZP + size_z)
     lists = sent2[sent2.shape[0] - 1].astype(jnp.float32)
     place(1, 0, SRC_WEIGHTS, HC, src, lists, size_x, size_z, size_y)
     place(1, 8, REC_WEIGHTS, HU, rec, lists, size_x, size_z, size_y)
@@ -247,16 +310,16 @@
     )
 
 
-def prep(x0, cond, a0, sent2, first, second):
+def prep(x0, cond, a0, sent2, first, second, side_first, side_second):
     shapes = wide_shapes(*cond.shape)
     return pl.pallas_call(
         prep_kernel,
         out_shape=tuple(pltpu.VMEM(s, jnp.float32) for s in shapes),
-        in_specs=[VMEM] * 6,
+        in_specs=[VMEM] * 8,
         out_specs=(VMEM,) * 5,
         compiler_params=PARAMS,
         name="prep",
-    )(x0, cond, a0, sent2, first, second)
+    )(x0, cond, a0, sent2, first, second, side_first, side_second)
 
 
 def beside_z_y(c):
@@ -275,44 +338,15 @@
 
 
 def chain_kernel(size_x, size_z, x0_in, cond_in, a0_in, src_in, rec_in, first, second,
-                 x0, cond, a0, src, rec, v_out, w_out, sums_out,
-                 v0, v1, v2, u, w1, w2, w3, acc):
+                 x0, cond, a0, src, rec, v0, v1, v2, u, w1, w2, sums_out, w3, acc):
     rows_z = x0.shape[-2]
     size_y = x0.shape[-1]
     own = slice(ZP, ZP + size_z)
     top = ZP + size_z
 
-    odd = is_odd("depth")
-
-    def low(at):
-        return jnp.where(odd, first[at].astype(jnp.float32), second[at].astype(jnp.float32))
-
-    def high(at):
-        return jnp.where(odd, second[at].astype(jnp.float32), first[at].astype(jnp.float32))
-
+    low, high = sides_of("depth", first, second)
     blank = jnp.zeros((ZP, size_y), jnp.float32)
-    gap = jnp.zeros((ZP - HA, size_y), jnp.float32)
-    at = 0
-    for i in range(1, size_x + 2 * HX - 1):
-        a, b = low(at), high(at)
-        for f in range(2):
-            x0[f, i, 0:ZP] = a[f * ZP : (f + 1) * ZP]
-            x0[f, i, top : top + ZP] = b[f * ZP : (f + 1) * ZP]
-        at += 1
-    for i in range(1, size_x + 2 * HC - 1, 2):
-        a, b = low(at), high(at)
-        for j in range(2):
-            cond[i + j, 0:ZP] = a[j * ZP : (j + 1) * ZP]
-            cond[i + j, top : top + ZP] = b[j * ZP : (j + 1) * ZP]
-        at += 1
-    for i in range(1, size_x + 2 * HA - 1, 2):
-        a, b = low(at), high(at)
-        for j in range(2):
-            for f in range(2):
-                part = slice((2 * j + f) * HA, (2 * j + f + 1) * HA)
-                a0[f, i + j, 0:ZP] = jnp.concatenate([gap, a[part]], axis=0)
-                a0[f, i + j, top : top + ZP] = jnp.concatenate([b[part], gap], axis=0)
-        at += 1
+    at = empty_depth(x0, cond, a0, corner_rows(size_x), low, high, top)
     for ref, lead in ((x0, 2), (cond, 0), (a0, 2)):
         n = ref.shape[-3]
         for i in (0, n - 1):
@@ -332,71 +366,58 @@
 
     low_x, high_x = edge("brick")
     low_z, high_z = edge("depth")
-    row = lax.broadcasted_iota(jnp.int32, (rows_z, size_y), 0)
-    in_z = jnp.where(row < ZP, low_z, jnp.where(row >= ZP + size_z, high_z, 1.0))
-
-    def mask(i, halo):
-        return in_z * jnp.where(i < halo, low_x, jnp.where(i >= halo + size_x, high_x, 1.0))
+    def inside(value, i, halo):
+        in_x = low_x if i < halo else high_x if i >= halo + size_x else None
+        parts = [value[:ZP] * low_z, value[own], value[top:] * high_z]
+        if in_x is not None:
+            parts = [p * in_x for p in parts]
+        return jnp.concatenate(parts, axis=0)
 
     def apply(ref, idx, i, damp):
         c = ref[idx + (i,)]
         return damp * c - (ref[idx + (i - 1,)] + ref[idx + (i + 1,)] + beside_z_y(c))
 
-    def loop(n, body, unroll):
-        while n % unroll:
-            unroll -= 1
-        if n == unroll:
-            for j in range(n):
-                body(j)
-            return
-
-        def step(i, carry):
-            for j in range(unroll):
-                body(i * unroll + j)
-            return carry
-
-        lax.fori_loop(0, n // unroll, step, 0)
+    def loop(n, body):
+        for i in range(n):
+            body(i)
 
     def first(i):
-        m = mask(i, HC)
         for f, s in enumerate(LAPLACE_SHIFTS):
-            v0[f, i] = m * (src[f, i] - apply(x0, (f,), i + 1, s * cond[i] + THETA))
-
-    loop(size_x + 2 * HC, first, 18)
+            v0[f, i] = inside(src[f, i] - apply(x0, (f,), i + 1, s * cond[i] + THETA), i, HC)
+
+    loop(size_x + 2 * HC, first)
 
     def second(i):
-        m = mask(i, 4)
         for f, s in enumerate(LAPLACE_SHIFTS):
-            v1[f, i] = m * apply(v0, (f,), i + 1, s * cond[i + 1])
-
-    loop(size_x + 8, second, 18)
+            v1[f, i] = inside(apply(v0, (f,), i + 1, s * cond[i + 1]), i, 4)
+
+    loop(size_x + 8, second)
 
     def third(i):
-        m = mask(i, 3)
         for f, s in enumerate(LAPLACE_SHIFTS):
-            v2[f, i] = m * apply(v1, (f,), i + 1, s * cond[i + 2])
-
-    loop(size_x + 6, third, 18)
+            v2[f, i] = inside(apply(v1, (f,), i + 1, s * cond[i + 2]), i, 3)
+
+    loop(size_x + 6, third)
 
     def start(i):
-        m = mask(i, HU)
         many = rec[2, i]
         for f, s in enumerate(LAPLACE_SHIFTS):
-            u[0, f, i] = m * (many * x0[f, i + 3] - rec[f, i] - apply(a0, (f,), i + 1, s * cond[i + 2] + THETA))
+            u[0, f, i] = inside(
+                many * x0[f, i + 3] - rec[f, i] - apply(a0, (f,), i + 1, s * cond[i + 2] + THETA), i, HU
+            )
             u[1, f, i] = many * v0[f, i + 2]
             u[2, f, i] = many * v1[f, i + 1]
             u[3, f, i] = many * v2[f, i]
 
-    loop(size_x + 2 * HU, start, 18)
+    loop(size_x + 2 * HU, start)
 
     def level(src_ref, dst_ref, halo):
         def body(i):
-            m = mask(i, halo)
             for f, s in enumerate(LAPLACE_SHIFTS):
                 damp = s * cond[i + HC - halo]
                 for k in range(4):
-                    dst_ref[k, f, i] = m * apply(src_ref, (k, f), i + 1, damp)
-        loop(size_x + 2 * halo, body, 6)
+                    dst_ref[k, f, i] = inside(apply(src_ref, (k, f), i + 1, damp), i, halo)
+        loop(size_x + 2 * halo, body)
 
     level(u, w1, 2)
     level(w1, w2, 1)
@@ -407,7 +428,7 @@
             for k in range(4):
                 w3[k, f, i] = apply(w2, (k, f), i + 1, damp)[own]
 
-    loop(size_x, last, 4)
+    loop(size_x, last)
 
     def tiles(a):
         total = None
@@ -433,9 +454,6 @@
             p1 = v1[f, i + 4, own]
             p2 = v2[f, i + 3, own]
             p3 = apply(v2, (f,), i + 3, s * cond[i + 5])[own]
-            v_out[0, f, i] = p0
-            v_out[1, f, i] = p1
-            v_out[2, f, i] = p2
             made = (p0 * p0, p0 * p1, p1 * p1, p1 * p2, p2 * p2, p2 * p3)
             return tuple(c + tiles(a) for c, a in zip(carry, made))
         done = over_rows(forward_sums, (zero,) * 6)
@@ -443,20 +461,19 @@
             acc[j * SLOTS + 2 * len(PAIRS) + f] = done[j]
 
     levels = ((u, 3, own), (w1, 2, own), (w2, 1, own), (w3, 0, slice(0, size_z)))
-    for j in range(6):
-        ra, oa, za = levels[j // 2]
-        rb, ob, zb = levels[j - j // 2]
+    for j in range(3):
+        ra, oa, za = levels[j]
+        rb, ob, zb = levels[j + 1]
         for f in range(2):
-            def pair_sums(i, carry, f=f, j=j):
+            def pair_sums(i, carry, f=f):
                 a = [ra[k, f, i + oa, za] for k in range(4)]
-                b = a if j % 2 == 0 else [rb[k, f, i + ob, zb] for k in range(4)]
-                if j % 2 == 0:
-                    for k in range(4):
-                        w_out[j // 2, k, f, i] = a[k]
-                return tuple(c + tiles(a[k] * b[l]) for c, (k, l) in zip(carry, PAIRS))
-            done = over_rows(pair_sums, (zero,) * len(PAIRS))
+                b = [rb[k, f, i + ob, zb] for k in range(4)]
+                made = [a[k] * a[l] for k, l in PAIRS] + [a[k] * b[l] for k, l in PAIRS]
+                return tuple(c + tiles(m) for c, m in zip(carry, made))
+            done = over_rows(pair_sums, (zero,) * (2 * len(PAIRS)), 2)
             for n in range(len(PAIRS)):
-                acc[j * SLOTS + 2 * n + f] = done[n]
+                acc[2 * j * SLOTS + 2 * n + f] = done[n]
+                acc[(2 * j + 1) * SLOTS + 2 * n + f] = done[len(PAIRS) + n]
 
     for j in range(acc.shape[0] // SLOTS):
         for n in range(0 if j >= 6 else 2 * len(PAIRS) + 2, SLOTS):
@@ -473,17 +490,15 @@
     f32 = jnp.float32
     slab = (size_z + 2 * ZP, size_y)
     outs = tuple(pltpu.VMEM(a.shape, f32) for a in wide) + (
-        pltpu.VMEM((3, 2, size_x, size_z, size_y), f32),
-        pltpu.VMEM((3, 4, 2, size_x, size_z, size_y), f32),
-        jax.ShapeDtypeStruct((n_dev, 2, 128), f32),
-    )
-    scratch = [
         pltpu.VMEM((2, size_x + 2 * HC) + slab, f32),
         pltpu.VMEM((2, size_x + 8) + slab, f32),
         pltpu.VMEM((2, size_x + 6) + slab, f32),
         pltpu.VMEM((4, 2, size_x + 6) + slab, f32),
         pltpu.VMEM((4, 2, size_x + 4) + slab, f32),
         pltpu.VMEM((4, 2, size_x + 2) + slab, f32),
+        jax.ShapeDtypeStruct((n_dev, 2, 128), f32),
+    )
+    scratch = [
         pltpu.VMEM((4, 2, size_x, size_z, size_y), f32),
         pltpu.VMEM((256, 8, 128), f32),
     ]
@@ -491,7 +506,7 @@
         functools.partial(chain_kernel, size_x, size_z),
         out_shape=outs,
         in_specs=[VMEM] * 7,
-        out_specs=(VMEM,) * 8,
+        out_specs=(VMEM,) * len(outs),
         scratch_shapes=scratch,
         input_output_aliases={i: i for i in range(5)},
         compiler_params=PARAMS,
@@ -522,7 +537,7 @@
     return c0, c1, c2
 
 
-def combine_kernel(every, x0, a0, v, w, forward, gradient):
+def combine_kernel(every, x0, a0, v0, v1, v2, u, w1, w2, forward, gradient):
     total = jnp.sum(every[...], axis=0)
     per = 128 // SLOTS
     rows = jnp.concatenate(
@@ -549,7 +564,10 @@
         weight = jnp.where(pair == n, product, weight)
     nu = gather_lanes(rows * weight, at < n_pair)
     d = coefficients([nu[j : j + 1] for j in range(6)])
-    size_x = x0.shape[1]
+    size_x, size_z = x0.shape[1:3]
+    own = slice(ZP, ZP + size_z)
+    v = ((v0, 5), (v1, 4), (v2, 3))
+    w = ((u, 3), (w1, 2), (w2, 1))
     scale = []
     for f in range(2):
         up = [c[k][:, f : f + 1] for k in range(3)]
@@ -561,29 +579,29 @@
             up, down = scale[f]
             field = x0[f, i]
             for k in range(3):
-                field = field + up[k] * v[k, f, i]
+                field = field + up[k] * v[k][0][f, i + v[k][1], own]
             other = a0[f, i]
             for j in range(3):
                 for k in range(4):
-                    other = other + down[j][k] * w[j, k, f, i]
+                    other = other + down[j][k] * w[j][0][k, f, i + w[j][1], own]
             forward[f, i] = field
             part = s * field * other
             total = part if total is None else total + part
         gradient[i] = (-total).astype(gradient.dtype)
 
 
-def combine(every, x0, a0, v, w):
+def combine(every, x0, a0, *made):
     return pl.pallas_call(
         combine_kernel,
         out_shape=(
             jax.ShapeDtypeStruct(x0.shape, jnp.float32),
             jax.ShapeDtypeStruct(x0.shape[1:], jnp.bfloat16),
         ),
-        in_specs=[VMEM] * 5,
+        in_specs=[VMEM] * (3 + len(made)),
         out_specs=(VMEM, VMEM),
         compiler_params=PARAMS,
         name="combine",
-    )(every, x0, a0, held(v), held(w))
+    )(every, x0, a0, *[held(a) for a in made])
 
 
 def turn_kernel(blocks, out, buf, sems):
@@ -669,18 +687,19 @@
 ):
     size_x, size_z, size_y = conductivity.shape
     n_dev = lax.axis_size("brick") * lax.axis_size("depth")
-    *sent, x0, cond, a0 = pack(
+    *sent, side_low, side_high, x0, cond, a0 = pack(
         initial_field, conductivity, adjoint_initial, src_cell[0], src_amp[0, 0], rec_cell[0], observed[0, 0]
     )
     x0, cond, a0 = held(x0), held(cond), held(a0)
     first, second = swap(*sent, "brick")
+    sides = swap(side_low, side_high, "depth")
     blocks = turn(cov_blocks[0, 0])
-    sent2 = mid(x0, cond, a0, sent[0], first, second, blocks)
-    wide = prep(x0, cond, a0, sent2[0], first, second)
+    sent2 = mid(x0, cond, a0, sent[0], first, second, blocks, *sides)
+    wide = prep(x0, cond, a0, sent2[0], first, second, *sides)
     first2, second2 = swap(*sent2, "depth")
-    v, w, sums = chain(wide, first2, second2, size_x, size_z, n_dev)
+    *made, sums = chain(wide, first2, second2, size_x, size_z, n_dev)
     every = lax.all_to_all(sums, BOTH, 0, 0, tiled=True)
-    forward, gradient = combine(every, x0, a0, v, w)
+    forward, gradient = combine(every, x0, a0, *made)
     every_block = lax.all_gather(gradient, "depth", axis=0, tiled=False)
     out = covariance(cov_cols[0], cov_rows[0], every_block, gradient, blocks)
     return (forward, out.reshape(size_x, size_z, size_y))

time: 57 us -> 55 us (0.965)
  blocking collectives: 21.8 us -> 20.6 us
  waiting for transfers between devices: 4.51 us -> 3.59 us
  starting transfers between devices: 10.1 us -> 10.7 us
    all_to_all x1, blocking collectives: 16 us -> 14.8 us  [local(): every = lax.all_to_all(sums, BOTH, 0, 0, tiled=True)]
    ppermute x4 -> x6, waiting for transfers between devices: 4.51 us -> 3.59 us  [swap(): return (lax.ppermute(first, axis, one), lax.ppermute(second, axis, two))]
    ppermute x4 -> x6, starting transfers between devices: 10.1 us -> 10.7 us  [swap(): return (lax.ppermute(first, axis, one), lax.ppermute(second, axis, two))]
  transfers between devices with their start and end apart: 4 -> 6, of which waited for: 2 -> 2; matrix products, arithmetic and copies ran while one was open for 0% -> 0% of each run, Pallas kernels for 9% -> 9%
where the time goes in v7:
time: 55 us; the launch traced here: 54.8 us
  blocking collectives  20.6 us (37%)
  Pallas kernels  19.2 us (35%)
  starting transfers between devices  10.7 us (19%)
  waiting for transfers between devices  3.59 us (7%)
  between operations  0.73 us (1%)
    all_to_all x1, blocking collectives, local(): every = lax.all_to_all(sums, BOTH, 0, 0, tiled=True)  14.8 us
    ppermute x6, starting transfers between devices, swap(): return (lax.ppermute(first, axis, one), lax.ppermute(second, axis, two))  10.7 us
    pallas_call x1, Pallas kernels, chain(): pl.pallas_call(functools.partial(chain_kernel, size_x, size_z), out_shape...  9.02 us
    all_gather x1, blocking collectives, local(): every_block = lax.all_gather(gradient, 'depth', axis=0, tiled=False)  5.76 us
    pallas_call x1, Pallas kernels, turn(): pl.pallas_call(turn_kernel, out_shape=pltpu.VMEM(blocks.shape, blocks.dty...  4.23 us
    ppermute x6, waiting for transfers between devices, swap(): return (lax.ppermute(first, axis, one), lax.ppermute(second, axis, two))  3.59 us
    pallas_call x1, Pallas kernels, covariance(): pl.pallas_call(covariance_kernel, out_shape=jax.ShapeDtypeStruct((size_x...  2.27 us
    pallas_call x1, Pallas kernels, combine(): pl.pallas_call(combine_kernel, out_shape=(jax.ShapeDtypeStruct(x0.shape,...  1.5 us
  transfers between devices with their start and end apart: 6, of which 2 were waited for; matrix products, arithmetic and copies ran while one was open for 0% of the time, Pallas kernels for 9%

profile of v7, /device:TPU:0, one launch (start us, length us, event | category | flops | bytes accessed | tf_op | source)
XLA Modules:
  0.0 54.8 jit_solution(15164063404719698827)
XLA Ops:
  0.6 1.3 %pack.1 = (bf16[26,16,256]{2,1,0:T(8,128)(2,1)S(1)}, bf16[26,16,256]{2,1,0:T(8,128)(2,1)S(1)}, bf16[16,16,256]{2,1,0:T(8,128)(2,1)S(1)}, bf16[16,16,256]{2,1,0:T...) custom-call(f32[2,8,16,256]{3,2,1,0:T(8,128)} %refs_0_.1, ...), custom_call_target="tpu_custom_call" | custom-call | tf_op jit(solution)/shard_map/pack/pallas_call | solution.py:186
  1.9 0.7 %collective-permute-start.1 = (bf16[26,16,256]{2,1,0:T(8,128)(2,1)S(1)}, bf16[26,16,256]{2,1,0:T(8,128)(2,1)S(1)}, u32[]{:S(2)}, u32[]{:S(2)}) collective-permute-start(bf16[26,16,256]{2,1,0:T(8,128)(2,1)S(1)} %get-tuple-element.29), channel_id=1, source_target_pairs={{4,8},{8,4},{12,16},{16,12},{20,24},{24,20},{5,9},{9,5},{13,17},{1... | collective-permute-start | bytes 638984 | tf_op jit(solution)/shard_map/ppermute | solution.py:48
  2.6 5.8 %collective-permute-start = (bf16[26,16,256]{2,1,0:T(8,128)(2,1)S(1)}, bf16[26,16,256]{2,1,0:T(8,128)(2,1)S(1)}, u32[]{:S(2)}, u32[]{:S(2)}) collective-permute-start(bf16[26,16,256]{2,1,0:T(8,128)(2,1)S(1)} %get-tuple-element.28.sent), channel_id=1, source_target_pairs={{0,4},{4,0},{8,12},{12,8},{16,20},{20,16},{24,28},{28,24},{1,5},{5... | collective-permute-start | bytes 638984 | tf_op jit(solution)/shard_map/ppermute | solution.py:48
  8.4 0.0 collective-permute-start.2
  8.4 0.7 %collective-permute-start.3 = (bf16[16,16,256]{2,1,0:T(8,128)(2,1)S(1)}, bf16[16,16,256]{2,1,0:T(8,128)(2,1)S(1)}, u32[]{:S(2)}, u32[]{:S(2)}) collective-permute-start(bf16[16,16,256]{2,1,0:T(8,128)(2,1)S(1)} %get-tuple-element.31), channel_id=1, source_target_pairs={{1,2},{2,1},{5,6},{6,5},{9,10},{10,9},{13,14},{14,13},{17,18},{18,... | collective-permute-start | bytes 393224 | tf_op jit(solution)/shard_map/ppermute | solution.py:48
  9.1 4.2 %turn.1.refs_0_.blocks = bf16[16,512,512]{2,1,0:T(8,128)(2,1)S(1)} custom-call(bf16[16,512,512]{2,1,0:T(8,128)(2,1)} %bitcast.12), custom_call_target="tpu_custom_call" | custom-call | tf_op jit(solution)/shard_map/turn/pallas_call | solution.py:618
  13.3 0.0 collective-permute-done.2.refs_1_.side_first
  13.3 0.0 collective-permute-done.3.refs_2_.side_second
  13.3 0.0 collective-permute-done.1.second
  13.3 3.4 %collective-permute-done.first = bf16[26,16,256]{2,1,0:T(8,128)(2,1)S(1)} collective-permute-done((bf16[26,16,256]{2,1,0:T(8,128)(2,1)S(1)}, bf16[26,16,256]{2,1,0:T(8,128)(2,1)S(1)}, u32[]{:S(2)}, u32[]{:S(2)}) %collective-permute-start) | collective-permute-done | bytes 213024 | tf_op jit(solution)/shard_map/ppermute | solution.py:48
  16.8 0.1 mid.1
  16.9 0.7 %collective-permute-start.5 = (bf16[18,16,256]{2,1,0:T(8,128)(2,1)S(1)}, bf16[18,16,256]{2,1,0:T(8,128)(2,1)S(1)}, u32[]{:S(2)}, u32[]{:S(2)}) collective-permute-start(bf16[18,16,256]{2,1,0:T(8,128)(2,1)S(1)} %get-tuple-element.38), channel_id=1, source_target_pairs={{1,2},{2,1},{5,6},{6,5},{9,10},{10,9},{13,14},{14,13},{17,18},{18,... | collective-permute-start | bytes 442376 | tf_op jit(solution)/shard_map/ppermute | solution.py:48
  17.6 2.9 %collective-permute-start.4 = (bf16[18,16,256]{2,1,0:T(8,128)(2,1)S(1)}, bf16[18,16,256]{2,1,0:T(8,128)(2,1)S(1)}, u32[]{:S(2)}, u32[]{:S(2)}) collective-permute-start(bf16[18,16,256]{2,1,0:T(8,128)(2,1)S(1)} %get-tuple-element.32.sent2), channel_id=1, source_target_pairs={{0,1},{1,0},{2,3},{3,2},{4,5},{5,4},{6,7},{7,6},{8,9},{9,8},{10,11... | collective-permute-start | bytes 442376 | tf_op jit(solution)/shard_map/ppermute | solution.py:48
  20.5 0.8 %prep.1 = (f32[2,20,32,256]{3,2,1,0:T(8,128)S(1)}, f32[18,32,256]{2,1,0:T(8,128)S(1)}, f32[2,16,32,256]{3,2,1,0:T(8,128)S(1)}, f32[2,18,32,256]{3,2,1,0:T(8,128)S(1)}, f32[3,14,32,256]{3,2,1,0:T(8,128)S(1)}) custom-call(f32[2,8,16,256]{3,2,1,0:T(8,128)S(1)} %get-tuple-element.25.x0, f32[8,16,256]{2,1,0:T(8,128)S(1)} %get-tuple-element.26.cond, ...), custom_call_target="tpu_custom_call" | custom-call | tf_op jit(solution)/shard_map/prep/pallas_call | solution.py:315
  21.3 0.0 collective-permute-done.5.second
  21.3 0.2 collective-permute-done.4.first
  21.5 9.0 %chain.1 = (f32[2,20,32,256]{3,2,1,0:T(8,128)S(1)}, f32[18,32,256]{2,1,0:T(8,128)S(1)}, f32[2,16,32,256]{3,2,1,0:T(8,128)S(1)}, f32[2,18,32,256]{3,2,1,0:T(8,128...) custom-call(f32[2,20,32,256]{3,2,1,0:T(8,128)S(1)} %get-tuple-elemen, ...), custom_call_target="tpu_custom_call", output_to_operand_aliasing={{0}: (0, {}), {1}: (1, {}), {2}: (2, {}), {3}: (3, {}), {4}... | custom-call | tf_op jit(solution)/shard_map/chain/pallas_call | solution.py:505
  30.5 14.8 %all_to_all.5.every = f32[32,2,128]{2,1,0:T(2,128)S(1)} all-to-all(f32[32,2,128]{2,1,0:T(2,128)S(1)} %get-tuple-element.39), channel_id=1, replica_groups=mesh['brick'=8,'depth'=4] {'brick','depth'}, dimensions={0} | all-to-all | bytes 65536 | tf_op jit(solution)/shard_map/all_to_all | solution.py:701
  45.3 0.0 copy-start
  45.3 0.0 copy-start.1
  45.3 1.5 %combine.1 = (f32[2,8,16,256]{3,2,1,0:T(8,128)}, bf16[8,16,256]{2,1,0:T(8,128)(2,1)S(1)}) custom-call(f32[32,2,128]{2,1,0:T(2,128)S(1)} %all_to_all.5.every, f32[2,8,16,256]{3,2,1,0:T(8,128)S(1)} %get-tuple-element.25.x0, f32[2,8,16,256]{3,2,1,0:T(8,128)S(1)} %get-tuple-element.27.a0, f32[2,18,32,256]{3,2,1,0:T(8,128)S(1)} %get-tuple-element.40.v0, ...), custom_call_target="tpu_custom_call" | custom-call | tf_op jit(solution)/shard_map/combine/pallas_call | solution.py:594
  46.8 5.8 %all-gather = bf16[32,16,256]{2,1,0:T(8,128)(2,1)S(1)} all-gather(bf16[8,16,256]{2,1,0:T(8,128)(2,1)S(1)} %get-tuple-element.47.own), channel_id=2, replica_groups=mesh['brick'=8,'depth'=4] {'depth'}, dimensions={0}, use_global_device_ids=true | all-gather | bytes 327680 | tf_op jit(solution)/shard_map/all_gather | solution.py:703
  52.6 0.0 copy-done
  52.6 0.0 copy-done.1
  52.6 2.3 %covariance.1 = f32[128,256]{1,0:T(8,128)} custom-call(s32[1,16]{1,0:T(1,128)S(1)} %bitcast.10, s32[1,16]{1,0:T(1,128)S(1)} %bitcast.11, bf16[4,8,16,256]{3,2,1,0:T(8,128)(2,1)S(1)} %bitcast.9, bf16[8,16,256]{2,1,0:T(8,128)(2,1)S(1)} %get-tuple-element.47.own, bf16[16,512,512]{2,1,0:T(8,128)(2,1)S(1)} %turn.1.refs_0_.blocks), custom_call_target="tpu_custom_call" | custom-call | tf_op jit(solution)/shard_map/covariance/pallas_call | solution.py:666
Async XLA Ops:
  1.9 11.4 %collective-permute-start.1 = (bf16[26,16,256]{2,1,0:T(8,128)(2,1)S(1)}, bf16[26,16,256]{2,1,0:T(8,128)(2,1)S(1)}, u32[]{:S(2)}, u32[]{:S(2)}) collective-permute-start(bf16[26,16,256]{2,1,0:T(8,128)(2,1)S(1)} %get-tuple-element.29), channel_id=1, source_target_pairs={{4,8},{8,4},{12,16},{16,12},{20,24},{24,20},{5,9},{9,5},{13,17},{1... | collective-permute-start | bytes 638984 | tf_op jit(solution)/shard_map/ppermute | solution.py:48
  2.6 14.2 %collective-permute-start = (bf16[26,16,256]{2,1,0:T(8,128)(2,1)S(1)}, bf16[26,16,256]{2,1,0:T(8,128)(2,1)S(1)}, u32[]{:S(2)}, u32[]{:S(2)}) collective-permute-start(bf16[26,16,256]{2,1,0:T(8,128)(2,1)S(1)} %get-tuple-element.28.sent), channel_id=1, source_target_pairs={{0,4},{4,0},{8,12},{12,8},{16,20},{20,16},{24,28},{28,24},{1,5},{5... | collective-permute-start | bytes 638984 | tf_op jit(solution)/shard_map/ppermute | solution.py:48
  8.4 4.9 %collective-permute-start.2 = (bf16[16,16,256]{2,1,0:T(8,128)(2,1)S(1)}, bf16[16,16,256]{2,1,0:T(8,128)(2,1)S(1)}, u32[]{:S(2)}, u32[]{:S(2)}) collective-permute-start(bf16[16,16,256]{2,1,0:T(8,128)(2,1)S(1)} %get-tuple-element.30), channel_id=1, source_target_pairs={{0,1},{1,0},{2,3},{3,2},{4,5},{5,4},{6,7},{7,6},{8,9},{9,8},{10,11... | collective-permute-start | bytes 393224 | tf_op jit(solution)/shard_map/ppermute | solution.py:48
  8.4 4.9 %collective-permute-start.3 = (bf16[16,16,256]{2,1,0:T(8,128)(2,1)S(1)}, bf16[16,16,256]{2,1,0:T(8,128)(2,1)S(1)}, u32[]{:S(2)}, u32[]{:S(2)}) collective-permute-start(bf16[16,16,256]{2,1,0:T(8,128)(2,1)S(1)} %get-tuple-element.31), channel_id=1, source_target_pairs={{1,2},{2,1},{5,6},{6,5},{9,10},{10,9},{13,14},{14,13},{17,18},{18,... | collective-permute-start | bytes 393224 | tf_op jit(solution)/shard_map/ppermute | solution.py:48
  16.9 4.4 %collective-permute-start.5 = (bf16[18,16,256]{2,1,0:T(8,128)(2,1)S(1)}, bf16[18,16,256]{2,1,0:T(8,128)(2,1)S(1)}, u32[]{:S(2)}, u32[]{:S(2)}) collective-permute-start(bf16[18,16,256]{2,1,0:T(8,128)(2,1)S(1)} %get-tuple-element.38), channel_id=1, source_target_pairs={{1,2},{2,1},{5,6},{6,5},{9,10},{10,9},{13,14},{14,13},{17,18},{18,... | collective-permute-start | bytes 442376 | tf_op jit(solution)/shard_map/ppermute | solution.py:48
  17.6 3.9 %collective-permute-start.4 = (bf16[18,16,256]{2,1,0:T(8,128)(2,1)S(1)}, bf16[18,16,256]{2,1,0:T(8,128)(2,1)S(1)}, u32[]{:S(2)}, u32[]{:S(2)}) collective-permute-start(bf16[18,16,256]{2,1,0:T(8,128)(2,1)S(1)} %get-tuple-element.32.sent2), channel_id=1, source_target_pairs={{0,1},{1,0},{2,3},{3,2},{4,5},{5,4},{6,7},{7,6},{8,9},{9,8},{10,11... | collective-permute-start | bytes 442376 | tf_op jit(solution)/shard_map/ppermute | solution.py:48
  45.3 7.3 %copy-start = (s32[1,1,16]{2,1,0:T(1,128)S(1)}, s32[1,1,16]{2,1,0:T(1,128)}, u32[]{:S(2)}) copy-start(s32[1,1,16]{2,1,0:T(1,128)} %param.19) | copy-start | bytes 196
  45.3 7.3 %copy-start.1 = (s32[1,1,16]{2,1,0:T(1,128)S(1)}, s32[1,1,16]{2,1,0:T(1,128)}, u32[]{:S(2)}) copy-start(s32[1,1,16]{2,1,0:T(1,128)} %param.18) | copy-start | bytes 196

commit v8 on v7

--- a/solution.py
+++ b/solution.py
@@ -131,18 +131,17 @@
 
 
 def empty_depth(x0, cond, a0, chosen, low, high, top):
-    gap = jnp.zeros((ZP - HA, x0.shape[-1]), jnp.float32)
     at = 0
     for i in chosen[0]:
         a, b = low(at), high(at)
         for f in range(2):
-            x0[f, i, 0:ZP] = a[f * ZP : (f + 1) * ZP]
+            x0[f, i, top + ZP : top + 2 * ZP] = a[f * ZP : (f + 1) * ZP]
             x0[f, i, top : top + ZP] = b[f * ZP : (f + 1) * ZP]
         at += 1
     for pair in zip(chosen[1][::2], chosen[1][1::2]):
         a, b = low(at), high(at)
         for n, i in enumerate(pair):
-            cond[i, 0:ZP] = a[n * ZP : (n + 1) * ZP]
+            cond[i, top + ZP : top + 2 * ZP] = a[n * ZP : (n + 1) * ZP]
             cond[i, top : top + ZP] = b[n * ZP : (n + 1) * ZP]
         at += 1
     for pair in zip(chosen[2][::2], chosen[2][1::2]):
@@ -150,8 +149,7 @@
         for n, i in enumerate(pair):
             for f in range(2):
                 part = slice((2 * n + f) * HA, (2 * n + f + 1) * HA)
-                a0[f, i, 0:ZP] = jnp.concatenate([gap, a[part]], axis=0)
-                a0[f, i, top : top + ZP] = jnp.concatenate([b[part], gap], axis=0)
+                a0[f, i, top : top + 2 * HA] = jnp.concatenate([b[part], a[part]], axis=0)
         at += 1
     return at
 
@@ -254,14 +252,14 @@
     row_x = x.astype(jnp.int32) + halo + size_x * dx
     ok = (hi >= 0.0) & (row_x >= 0) & (row_x < nx)
     if t == 1:
-        depth, z0 = size_z, ZP
+        depth, z0 = size_z, 0
         target = row_x * size_z + z
     elif t == 0:
-        depth, z0 = ZP, 0
+        depth, z0 = ZP, size_z + ZP
         target = row_x * ZP + z - (size_z - ZP)
         ok = ok & (z >= size_z - ZP)
     else:
-        depth, z0 = ZP, ZP + size_z
+        depth, z0 = ZP, size_z
         target = row_x * ZP + z
         ok = ok & (z < ZP)
     target = jnp.where(ok, target, -1)
@@ -285,7 +283,7 @@
 def prep_kernel(x0, cond, a0, sent2, first, second, side_first, side_second, x0_w, cond_w, a0_w, src, rec):
     size_x, size_z, size_y = cond.shape
     fields, conds, adjoints, _, _ = joined_rows(x0, cond, a0, first, second)
-    own = slice(ZP, ZP + size_z)
+    own = slice(0, size_z)
     for f in range(2):
         for i in range(size_x + 2 * HX):
             x0_w[f, i, own] = fields[f](i)
@@ -293,7 +291,7 @@
             a0_w[f, i, own] = adjoints[f](i)
     for i in range(size_x + 2 * HC):
         cond_w[i, own] = conds(i)
-    empty_depth(x0_w, cond_w, a0_w, own_rows(size_x), *sides_of("depth", side_first, side_second), ZP + size_z)
+    empty_depth(x0_w, cond_w, a0_w, own_rows(size_x), *sides_of("depth", side_first, side_second), size_z)
     lists = sent2[sent2.shape[0] - 1].astype(jnp.float32)
     place(1, 0, SRC_WEIGHTS, HC, src, lists, size_x, size_z, size_y)
     place(1, 8, REC_WEIGHTS, HU, rec, lists, size_x, size_z, size_y)
@@ -304,7 +302,7 @@
     return (
         (2, size_x + 2 * HX) + slab,
         (size_x + 2 * HC,) + slab,
-        (2, size_x + 2 * HA) + slab,
+        (2, size_x + 2 * HA) + (size_z + 2 * HA, size_y),
         (2, size_x + 2 * HC) + slab,
         (3, size_x + 2 * HU) + slab,
     )
@@ -338,24 +336,22 @@
 
 
 def chain_kernel(size_x, size_z, x0_in, cond_in, a0_in, src_in, rec_in, first, second,
-                 x0, cond, a0, src, rec, v0, v1, v2, u, w1, w2, sums_out, w3, acc):
+                 x0, cond, a0, src, rec, v0, v1, v2, u, w1, w2, sums_out, w3, acc, cond_n):
     rows_z = x0.shape[-2]
     size_y = x0.shape[-1]
-    own = slice(ZP, ZP + size_z)
-    top = ZP + size_z
+    own = slice(0, size_z)
+    top = size_z
 
     low, high = sides_of("depth", first, second)
-    blank = jnp.zeros((ZP, size_y), jnp.float32)
     at = empty_depth(x0, cond, a0, corner_rows(size_x), low, high, top)
-    for ref, lead in ((x0, 2), (cond, 0), (a0, 2)):
-        n = ref.shape[-3]
-        for i in (0, n - 1):
-            for z in (slice(0, ZP), slice(top, top + ZP)):
-                if lead:
-                    for f in range(lead):
-                        ref[f, i, z] = blank
-                else:
-                    ref[i, z] = blank
+    for ref in (x0, cond, a0):
+        blank = jnp.zeros((ref.shape[-2] - top, size_y), jnp.float32)
+        for i in (0, ref.shape[-3] - 1):
+            if len(ref.shape) == 3:
+                ref[i, top:] = blank
+            else:
+                for f in range(2):
+                    ref[f, i, top:] = blank
     for t, lists in ((0, low(at)), (2, high(at))):
         place(t, 0, SRC_WEIGHTS, HC, src, lists, size_x, size_z, size_y)
         place(t, 8, REC_WEIGHTS, HU, rec, lists, size_x, size_z, size_y)
@@ -366,9 +362,18 @@
 
     low_x, high_x = edge("brick")
     low_z, high_z = edge("depth")
+    upper = lax.broadcasted_iota(jnp.int32, (2 * HA, size_y), 0) < HA
+    both_z = jnp.where(upper, high_z, low_z)
+
+    def narrow(value):
+        return jnp.concatenate([value[own], jnp.where(upper, value[top : top + ZP], value[top + ZP :])], axis=0)
+
     def inside(value, i, halo):
         in_x = low_x if i < halo else high_x if i >= halo + size_x else None
-        parts = [value[:ZP] * low_z, value[own], value[top:] * high_z]
+        if value.shape[0] == rows_z:
+            parts = [value[own], value[top : top + ZP] * high_z, value[top + ZP :] * low_z]
+        else:
+            parts = [value[own], value[top:] * both_z]
         if in_x is not None:
             parts = [p * in_x for p in parts]
         return jnp.concatenate(parts, axis=0)
@@ -381,6 +386,11 @@
         for i in range(n):
             body(i)
 
+    def thin(i):
+        cond_n[i] = narrow(cond[i])
+
+    loop(size_x + 2 * HC, thin)
+
     def first(i):
         for f, s in enumerate(LAPLACE_SHIFTS):
             v0[f, i] = inside(src[f, i] - apply(x0, (f,), i + 1, s * cond[i] + THETA), i, HC)
@@ -389,23 +399,25 @@
 
     def second(i):
         for f, s in enumerate(LAPLACE_SHIFTS):
-            v1[f, i] = inside(apply(v0, (f,), i + 1, s * cond[i + 1]), i, 4)
+            v1[f, i] = inside(narrow(apply(v0, (f,), i + 1, s * cond[i + 1])), i, 4)
 
     loop(size_x + 8, second)
 
     def third(i):
         for f, s in enumerate(LAPLACE_SHIFTS):
-            v2[f, i] = inside(apply(v1, (f,), i + 1, s * cond[i + 2]), i, 3)
+            v2[f, i] = inside(apply(v1, (f,), i + 1, s * cond_n[i + 2]), i, 3)
 
     loop(size_x + 6, third)
 
     def start(i):
-        many = rec[2, i]
+        many = narrow(rec[2, i])
         for f, s in enumerate(LAPLACE_SHIFTS):
             u[0, f, i] = inside(
-                many * x0[f, i + 3] - rec[f, i] - apply(a0, (f,), i + 1, s * cond[i + 2] + THETA), i, HU
+                many * narrow(x0[f, i + 3]) - narrow(rec[f, i]) - apply(a0, (f,), i + 1, s * cond_n[i + 2] + THETA),
+                i,
+                HU,
             )
-            u[1, f, i] = many * v0[f, i + 2]
+            u[1, f, i] = many * narrow(v0[f, i + 2])
             u[2, f, i] = many * v1[f, i + 1]
             u[3, f, i] = many * v2[f, i]
 
@@ -414,7 +426,7 @@
     def level(src_ref, dst_ref, halo):
         def body(i):
             for f, s in enumerate(LAPLACE_SHIFTS):
-                damp = s * cond[i + HC - halo]
+                damp = s * cond_n[i + HC - halo]
                 for k in range(4):
                     dst_ref[k, f, i] = inside(apply(src_ref, (k, f), i + 1, damp), i, halo)
         loop(size_x + 2 * halo, body)
@@ -424,7 +436,7 @@
 
     def last(i):
         for f, s in enumerate(LAPLACE_SHIFTS):
-            damp = s * cond[i + HC]
+            damp = s * cond_n[i + HC]
             for k in range(4):
                 w3[k, f, i] = apply(w2, (k, f), i + 1, damp)[own]
 
@@ -453,7 +465,7 @@
             p0 = v0[f, i + 5, own]
             p1 = v1[f, i + 4, own]
             p2 = v2[f, i + 3, own]
-            p3 = apply(v2, (f,), i + 3, s * cond[i + 5])[own]
+            p3 = apply(v2, (f,), i + 3, s * cond_n[i + 5])[own]
             made = (p0 * p0, p0 * p1, p1 * p1, p1 * p2, p2 * p2, p2 * p3)
             return tuple(c + tiles(a) for c, a in zip(carry, made))
         done = over_rows(forward_sums, (zero,) * 6)
@@ -489,18 +501,20 @@
     size_y = wide[0].shape[-1]
     f32 = jnp.float32
     slab = (size_z + 2 * ZP, size_y)
+    thin = (size_z + 2 * HA, size_y)
     outs = tuple(pltpu.VMEM(a.shape, f32) for a in wide) + (
         pltpu.VMEM((2, size_x + 2 * HC) + slab, f32),
-        pltpu.VMEM((2, size_x + 8) + slab, f32),
-        pltpu.VMEM((2, size_x + 6) + slab, f32),
-        pltpu.VMEM((4, 2, size_x + 6) + slab, f32),
-        pltpu.VMEM((4, 2, size_x + 4) + slab, f32),
-        pltpu.VMEM((4, 2, size_x + 2) + slab, f32),
+        pltpu.VMEM((2, size_x + 8) + thin, f32),
+        pltpu.VMEM((2, size_x + 6) + thin, f32),
+        pltpu.VMEM((4, 2, size_x + 6) + thin, f32),
+        pltpu.VMEM((4, 2, size_x + 4) + thin, f32),
+        pltpu.VMEM((4, 2, size_x + 2) + thin, f32),
         jax.ShapeDtypeStruct((n_dev, 2, 128), f32),
     )
     scratch = [
         pltpu.VMEM((4, 2, size_x, size_z, size_y), f32),
         pltpu.VMEM((256, 8, 128), f32),
+        pltpu.VMEM((size_x + 2 * HC,) + thin, f32),
     ]
     return pl.pallas_call(
         functools.partial(chain_kernel, size_x, size_z),
@@ -565,7 +579,7 @@
     nu = gather_lanes(rows * weight, at < n_pair)
     d = coefficients([nu[j : j + 1] for j in range(6)])
     size_x, size_z = x0.shape[1:3]
-    own = slice(ZP, ZP + size_z)
+    own = slice(0, size_z)
     v = ((v0, 5), (v1, 4), (v2, 3))
     w = ((u, 3), (w1, 2), (w2, 1))
     scale = []

time: 55 us -> 53.6 us (0.975)
  Pallas kernels: 19.2 us -> 17.8 us
    pallas_call x1, Pallas kernels: 9.02 us -> 7.63 us  [chain(): pl.pallas_call(functools.partial(chain_kernel, size_x, size_z), out_shape...]
where the time goes in v8:
time: 53.6 us; the launch traced here: 53.4 us
  blocking collectives  20.6 us (38%)
  Pallas kernels  17.8 us (33%)
  starting transfers between devices  10.7 us (20%)
  waiting for transfers between devices  3.6 us (7%)
  between operations  0.73 us (1%)
    all_to_all x1, blocking collectives, local(): every = lax.all_to_all(sums, BOTH, 0, 0, tiled=True)  14.8 us
    ppermute x6, starting transfers between devices, swap(): return (lax.ppermute(first, axis, one), lax.ppermute(second, axis, two))  10.7 us
    pallas_call x1, Pallas kernels, chain(): pl.pallas_call(functools.partial(chain_kernel, size_x, size_z), out_shape...  7.63 us
    all_gather x1, blocking collectives, local(): every_block = lax.all_gather(gradient, 'depth', axis=0, tiled=False)  5.76 us
    pallas_call x1, Pallas kernels, turn(): pl.pallas_call(turn_kernel, out_shape=pltpu.VMEM(blocks.shape, blocks.dty...  4.23 us
    ppermute x6, waiting for transfers between devices, swap(): return (lax.ppermute(first, axis, one), lax.ppermute(second, axis, two))  3.6 us
    pallas_call x1, Pallas kernels, covariance(): pl.pallas_call(covariance_kernel, out_shape=jax.ShapeDtypeStruct((size_x...  2.27 us
    pallas_call x1, Pallas kernels, combine(): pl.pallas_call(combine_kernel, out_shape=(jax.ShapeDtypeStruct(x0.shape,...  1.5 us
  transfers between devices with their start and end apart: 6, of which 2 were waited for; matrix products, arithmetic and copies ran while one was open for 0% of the time, Pallas kernels for 9%

profile of v8, /device:TPU:0, one launch (start us, length us, event | category | flops | bytes accessed | tf_op | source)
XLA Modules:
  0.0 53.4 jit_solution(16157399188899998446)
XLA Ops:
  0.6 1.3 %pack.1 = (bf16[26,16,256]{2,1,0:T(8,128)(2,1)S(1)}, bf16[26,16,256]{2,1,0:T(8,128)(2,1)S(1)}, bf16[16,16,256]{2,1,0:T(8,128)(2,1)S(1)}, bf16[16,16,256]{2,1,0:T...) custom-call(f32[2,8,16,256]{3,2,1,0:T(8,128)} %refs_0_.1, ...), custom_call_target="tpu_custom_call" | custom-call | tf_op jit(solution)/shard_map/pack/pallas_call | solution.py:184
  1.9 0.7 %collective-permute-start.1 = (bf16[26,16,256]{2,1,0:T(8,128)(2,1)S(1)}, bf16[26,16,256]{2,1,0:T(8,128)(2,1)S(1)}, u32[]{:S(2)}, u32[]{:S(2)}) collective-permute-start(bf16[26,16,256]{2,1,0:T(8,128)(2,1)S(1)} %get-tuple-element.29), channel_id=1, source_target_pairs={{4,8},{8,4},{12,16},{16,12},{20,24},{24,20},{5,9},{9,5},{13,17},{1... | collective-permute-start | bytes 638984 | tf_op jit(solution)/shard_map/ppermute | solution.py:48
  2.6 5.8 %collective-permute-start = (bf16[26,16,256]{2,1,0:T(8,128)(2,1)S(1)}, bf16[26,16,256]{2,1,0:T(8,128)(2,1)S(1)}, u32[]{:S(2)}, u32[]{:S(2)}) collective-permute-start(bf16[26,16,256]{2,1,0:T(8,128)(2,1)S(1)} %get-tuple-element.28.sent), channel_id=1, source_target_pairs={{0,4},{4,0},{8,12},{12,8},{16,20},{20,16},{24,28},{28,24},{1,5},{5... | collective-permute-start | bytes 638984 | tf_op jit(solution)/shard_map/ppermute | solution.py:48
  8.4 0.0 collective-permute-start.2
  8.4 0.7 %collective-permute-start.3 = (bf16[16,16,256]{2,1,0:T(8,128)(2,1)S(1)}, bf16[16,16,256]{2,1,0:T(8,128)(2,1)S(1)}, u32[]{:S(2)}, u32[]{:S(2)}) collective-permute-start(bf16[16,16,256]{2,1,0:T(8,128)(2,1)S(1)} %get-tuple-element.31), channel_id=1, source_target_pairs={{1,2},{2,1},{5,6},{6,5},{9,10},{10,9},{13,14},{14,13},{17,18},{18,... | collective-permute-start | bytes 393224 | tf_op jit(solution)/shard_map/ppermute | solution.py:48
  9.1 4.2 %turn.1.refs_0_.blocks = bf16[16,512,512]{2,1,0:T(8,128)(2,1)S(1)} custom-call(bf16[16,512,512]{2,1,0:T(8,128)(2,1)} %bitcast.12), custom_call_target="tpu_custom_call" | custom-call | tf_op jit(solution)/shard_map/turn/pallas_call | solution.py:632
  13.3 0.0 collective-permute-done.2.refs_1_.side_first
  13.3 0.0 collective-permute-done.3.refs_2_.side_second
  13.3 0.0 collective-permute-done.1.second
  13.3 3.4 %collective-permute-done.first = bf16[26,16,256]{2,1,0:T(8,128)(2,1)S(1)} collective-permute-done((bf16[26,16,256]{2,1,0:T(8,128)(2,1)S(1)}, bf16[26,16,256]{2,1,0:T(8,128)(2,1)S(1)}, u32[]{:S(2)}, u32[]{:S(2)}) %collective-permute-start) | collective-permute-done | bytes 213024 | tf_op jit(solution)/shard_map/ppermute | solution.py:48
  16.8 0.1 mid.1
  16.9 0.7 %collective-permute-start.5 = (bf16[18,16,256]{2,1,0:T(8,128)(2,1)S(1)}, bf16[18,16,256]{2,1,0:T(8,128)(2,1)S(1)}, u32[]{:S(2)}, u32[]{:S(2)}) collective-permute-start(bf16[18,16,256]{2,1,0:T(8,128)(2,1)S(1)} %get-tuple-element.38), channel_id=1, source_target_pairs={{1,2},{2,1},{5,6},{6,5},{9,10},{10,9},{13,14},{14,13},{17,18},{18,... | collective-permute-start | bytes 442376 | tf_op jit(solution)/shard_map/ppermute | solution.py:48
  17.6 2.9 %collective-permute-start.4 = (bf16[18,16,256]{2,1,0:T(8,128)(2,1)S(1)}, bf16[18,16,256]{2,1,0:T(8,128)(2,1)S(1)}, u32[]{:S(2)}, u32[]{:S(2)}) collective-permute-start(bf16[18,16,256]{2,1,0:T(8,128)(2,1)S(1)} %get-tuple-element.32.sent2), channel_id=1, source_target_pairs={{0,1},{1,0},{2,3},{3,2},{4,5},{5,4},{6,7},{7,6},{8,9},{9,8},{10,11... | collective-permute-start | bytes 442376 | tf_op jit(solution)/shard_map/ppermute | solution.py:48
  20.5 0.8 %prep.1 = (f32[2,20,32,256]{3,2,1,0:T(8,128)S(1)}, f32[18,32,256]{2,1,0:T(8,128)S(1)}, f32[2,16,24,256]{3,2,1,0:T(8,128)S(1)}, f32[2,18,32,256]{3,2,1,0:T(8,128)S(1)}, f32[3,14,32,256]{3,2,1,0:T(8,128)S(1)}) custom-call(f32[2,8,16,256]{3,2,1,0:T(8,128)S(1)} %get-tuple-element.25.x0, f32[8,16,256]{2,1,0:T(8,128)S(1)} %get-tuple-element.26.cond, ...), custom_call_target="tpu_custom_call" | custom-call | tf_op jit(solution)/shard_map/prep/pallas_call | solution.py:313
  21.3 0.0 collective-permute-done.5.second
  21.3 0.2 collective-permute-done.4.first
  21.5 7.6 %chain.1 = (f32[2,20,32,256]{3,2,1,0:T(8,128)S(1)}, f32[18,32,256]{2,1,0:T(8,128)S(1)}, f32[2,16,24,256]{3,2,1,0:T(8,128)S(1)}, f32[2,18,32,256]{3,2,1,0:T(8,128...) custom-call(f32[2,20,32,256]{3,2,1,0:T(8,128)S(1)} %get-tuple-elemen, ...), custom_call_target="tpu_custom_call", output_to_operand_aliasing={{0}: (0, {}), {1}: (1, {}), {2}: (2, {}), {3}: (3, {}), {4}... | custom-call | tf_op jit(solution)/shard_map/chain/pallas_call | solution.py:519
  29.1 14.8 %all_to_all.5.every = f32[32,2,128]{2,1,0:T(2,128)S(1)} all-to-all(f32[32,2,128]{2,1,0:T(2,128)S(1)} %get-tuple-element.39), channel_id=1, replica_groups=mesh['brick'=8,'depth'=4] {'brick','depth'}, dimensions={0} | all-to-all | bytes 65536 | tf_op jit(solution)/shard_map/all_to_all | solution.py:715
  43.9 0.0 copy-start
  43.9 0.0 copy-start.1
  43.9 1.5 %combine.1 = (f32[2,8,16,256]{3,2,1,0:T(8,128)}, bf16[8,16,256]{2,1,0:T(8,128)(2,1)S(1)}) custom-call(f32[32,2,128]{2,1,0:T(2,128)S(1)} %all_to_all.5.every, f32[2,8,16,256]{3,2,1,0:T(8,128)S(1)} %get-tuple-element.25.x0, f32[2,8,16,256]{3,2,1,0:T(8,128)S(1)} %get-tuple-element.27.a0, f32[2,18,32,256]{3,2,1,0:T(8,128)S(1)} %get-tuple-element.40.v0, ...), custom_call_target="tpu_custom_call" | custom-call | tf_op jit(solution)/shard_map/combine/pallas_call | solution.py:608
  45.4 5.8 %all-gather = bf16[32,16,256]{2,1,0:T(8,128)(2,1)S(1)} all-gather(bf16[8,16,256]{2,1,0:T(8,128)(2,1)S(1)} %get-tuple-element.47.own), channel_id=2, replica_groups=mesh['brick'=8,'depth'=4] {'depth'}, dimensions={0}, use_global_device_ids=true | all-gather | bytes 327680 | tf_op jit(solution)/shard_map/all_gather | solution.py:717
  51.2 0.0 copy-done
  51.2 0.0 copy-done.1
  51.2 2.3 %covariance.1 = f32[128,256]{1,0:T(8,128)} custom-call(s32[1,16]{1,0:T(1,128)S(1)} %bitcast.10, s32[1,16]{1,0:T(1,128)S(1)} %bitcast.11, bf16[4,8,16,256]{3,2,1,0:T(8,128)(2,1)S(1)} %bitcast.9, bf16[8,16,256]{2,1,0:T(8,128)(2,1)S(1)} %get-tuple-element.47.own, bf16[16,512,512]{2,1,0:T(8,128)(2,1)S(1)} %turn.1.refs_0_.blocks), custom_call_target="tpu_custom_call" | custom-call | tf_op jit(solution)/shard_map/covariance/pallas_call | solution.py:680
Async XLA Ops:
  1.9 11.4 %collective-permute-start.1 = (bf16[26,16,256]{2,1,0:T(8,128)(2,1)S(1)}, bf16[26,16,256]{2,1,0:T(8,128)(2,1)S(1)}, u32[]{:S(2)}, u32[]{:S(2)}) collective-permute-start(bf16[26,16,256]{2,1,0:T(8,128)(2,1)S(1)} %get-tuple-element.29), channel_id=1, source_target_pairs={{4,8},{8,4},{12,16},{16,12},{20,24},{24,20},{5,9},{9,5},{13,17},{1... | collective-permute-start | bytes 638984 | tf_op jit(solution)/shard_map/ppermute | solution.py:48
  2.6 14.2 %collective-permute-start = (bf16[26,16,256]{2,1,0:T(8,128)(2,1)S(1)}, bf16[26,16,256]{2,1,0:T(8,128)(2,1)S(1)}, u32[]{:S(2)}, u32[]{:S(2)}) collective-permute-start(bf16[26,16,256]{2,1,0:T(8,128)(2,1)S(1)} %get-tuple-element.28.sent), channel_id=1, source_target_pairs={{0,4},{4,0},{8,12},{12,8},{16,20},{20,16},{24,28},{28,24},{1,5},{5... | collective-permute-start | bytes 638984 | tf_op jit(solution)/shard_map/ppermute | solution.py:48
  8.4 4.9 %collective-permute-start.2 = (bf16[16,16,256]{2,1,0:T(8,128)(2,1)S(1)}, bf16[16,16,256]{2,1,0:T(8,128)(2,1)S(1)}, u32[]{:S(2)}, u32[]{:S(2)}) collective-permute-start(bf16[16,16,256]{2,1,0:T(8,128)(2,1)S(1)} %get-tuple-element.30), channel_id=1, source_target_pairs={{0,1},{1,0},{2,3},{3,2},{4,5},{5,4},{6,7},{7,6},{8,9},{9,8},{10,11... | collective-permute-start | bytes 393224 | tf_op jit(solution)/shard_map/ppermute | solution.py:48
  8.4 4.9 %collective-permute-start.3 = (bf16[16,16,256]{2,1,0:T(8,128)(2,1)S(1)}, bf16[16,16,256]{2,1,0:T(8,128)(2,1)S(1)}, u32[]{:S(2)}, u32[]{:S(2)}) collective-permute-start(bf16[16,16,256]{2,1,0:T(8,128)(2,1)S(1)} %get-tuple-element.31), channel_id=1, source_target_pairs={{1,2},{2,1},{5,6},{6,5},{9,10},{10,9},{13,14},{14,13},{17,18},{18,... | collective-permute-start | bytes 393224 | tf_op jit(solution)/shard_map/ppermute | solution.py:48
  16.9 4.4 %collective-permute-start.5 = (bf16[18,16,256]{2,1,0:T(8,128)(2,1)S(1)}, bf16[18,16,256]{2,1,0:T(8,128)(2,1)S(1)}, u32[]{:S(2)}, u32[]{:S(2)}) collective-permute-start(bf16[18,16,256]{2,1,0:T(8,128)(2,1)S(1)} %get-tuple-element.38), channel_id=1, source_target_pairs={{1,2},{2,1},{5,6},{6,5},{9,10},{10,9},{13,14},{14,13},{17,18},{18,... | collective-permute-start | bytes 442376 | tf_op jit(solution)/shard_map/ppermute | solution.py:48
  17.6 3.9 %collective-permute-start.4 = (bf16[18,16,256]{2,1,0:T(8,128)(2,1)S(1)}, bf16[18,16,256]{2,1,0:T(8,128)(2,1)S(1)}, u32[]{:S(2)}, u32[]{:S(2)}) collective-permute-start(bf16[18,16,256]{2,1,0:T(8,128)(2,1)S(1)} %get-tuple-element.32.sent2), channel_id=1, source_target_pairs={{0,1},{1,0},{2,3},{3,2},{4,5},{5,4},{6,7},{7,6},{8,9},{9,8},{10,11... | collective-permute-start | bytes 442376 | tf_op jit(solution)/shard_map/ppermute | solution.py:48
  43.9 7.3 %copy-start = (s32[1,1,16]{2,1,0:T(1,128)S(1)}, s32[1,1,16]{2,1,0:T(1,128)}, u32[]{:S(2)}) copy-start(s32[1,1,16]{2,1,0:T(1,128)} %param.19) | copy-start | bytes 196
  43.9 7.3 %copy-start.1 = (s32[1,1,16]{2,1,0:T(1,128)S(1)}, s32[1,1,16]{2,1,0:T(1,128)}, u32[]{:S(2)}) copy-start(s32[1,1,16]{2,1,0:T(1,128)} %param.18) | copy-start | bytes 196

commit v9 on v8

--- a/solution.py
+++ b/solution.py
@@ -560,15 +560,16 @@
     rows = jnp.concatenate([rows, jnp.zeros((2, SLOTS), jnp.float32)], axis=0)
     rows = jnp.concatenate([rows, jnp.zeros((8, 128 - SLOTS), jnp.float32)], axis=1)
     n_pair = 2 * len(PAIRS)
-    at = lax.broadcasted_iota(jnp.int32, (128, 128), 0)
-    to = lax.broadcasted_iota(jnp.int32, (128, 128), 1)
-    same = (at & 1) == (to & 1)
-
-    def gather_lanes(values, chosen):
-        table = jnp.where(same & chosen, 1.0, 0.0)
-        return jnp.dot(values, table, precision=lax.Precision.HIGHEST, preferred_element_type=jnp.float32)
-
-    mu = gather_lanes(rows, (at >= n_pair) & (at < n_pair + 2))
+    lane = lax.broadcasted_iota(jnp.int32, (8, 128), 1)
+    even = (lane & 1) == 0
+
+    def by_parity(values, chosen):
+        values = jnp.where(chosen, values, 0.0)
+        first = jnp.sum(jnp.where(even, values, 0.0), axis=1, keepdims=True)
+        second = jnp.sum(jnp.where(even, 0.0, values), axis=1, keepdims=True)
+        return jnp.where(even, first, second)
+
+    mu = by_parity(rows, (lane >= n_pair) & (lane < n_pair + 2))
     c = coefficients([mu[j : j + 1] for j in range(6)])
     basis = (jnp.ones_like(c[0]),) + c
     pair = lax.broadcasted_iota(jnp.int32, (1, 128), 1) // 2
@@ -576,7 +577,7 @@
     for n, (k, l) in enumerate(PAIRS):
         product = basis[k] * basis[l] * (1.0 if k == l else 2.0)
         weight = jnp.where(pair == n, product, weight)
-    nu = gather_lanes(rows * weight, at < n_pair)
+    nu = by_parity(rows * weight, lane < n_pair)
     d = coefficients([nu[j : j + 1] for j in range(6)])
     size_x, size_z = x0.shape[1:3]
     own = slice(0, size_z)

time: 53.6 us -> 53.5 us (level)
  transfers between devices with their start and end apart: 6 -> 6, of which waited for: 2 -> 2; matrix products, arithmetic and copies ran while one was open for 0% -> 0% of each run, Pallas kernels for 9% -> 10%
where the time goes in v9:
time: 53.5 us; the launch traced here: 53.3 us
  blocking collectives  20.6 us (39%)
  Pallas kernels  17.7 us (33%)
  starting transfers between devices  10.7 us (20%)
  waiting for transfers between devices  3.6 us (7%)
  between operations  0.73 us (1%)
    all_to_all x1, blocking collectives, local(): every = lax.all_to_all(sums, BOTH, 0, 0, tiled=True)  14.8 us
    ppermute x6, starting transfers between devices, swap(): return (lax.ppermute(first, axis, one), lax.ppermute(second, axis, two))  10.7 us
    pallas_call x1, Pallas kernels, chain(): pl.pallas_call(functools.partial(chain_kernel, size_x, size_z), out_shape...  7.63 us
    all_gather x1, blocking collectives, local(): every_block = lax.all_gather(gradient, 'depth', axis=0, tiled=False)  5.76 us
    pallas_call x1, Pallas kernels, turn(): pl.pallas_call(turn_kernel, out_shape=pltpu.VMEM(blocks.shape, blocks.dty...  4.23 us
    ppermute x6, waiting for transfers between devices, swap(): return (lax.ppermute(first, axis, one), lax.ppermute(second, axis, two))  3.6 us
    pallas_call x1, Pallas kernels, covariance(): pl.pallas_call(covariance_kernel, out_shape=jax.ShapeDtypeStruct((size_x...  2.27 us
    pallas_call x1, Pallas kernels, combine(): pl.pallas_call(combine_kernel, out_shape=(jax.ShapeDtypeStruct(x0.shape,...  1.36 us
  transfers between devices with their start and end apart: 6, of which 2 were waited for; matrix products, arithmetic and copies ran while one was open for 0% of the time, Pallas kernels for 10%

profile of v9, /device:TPU:0, one launch (start us, length us, event | category | flops | bytes accessed | tf_op | source)
XLA Modules:
  0.0 53.3 jit_solution(12477306219718812013)
XLA Ops:
  0.6 1.3 %pack.1 = (bf16[26,16,256]{2,1,0:T(8,128)(2,1)S(1)}, bf16[26,16,256]{2,1,0:T(8,128)(2,1)S(1)}, bf16[16,16,256]{2,1,0:T(8,128)(2,1)S(1)}, bf16[16,16,256]{2,1,0:T...) custom-call(f32[2,8,16,256]{3,2,1,0:T(8,128)} %refs_0_.1, ...), custom_call_target="tpu_custom_call" | custom-call | tf_op jit(solution)/shard_map/pack/pallas_call | solution.py:184
  1.9 0.7 %collective-permute-start.1 = (bf16[26,16,256]{2,1,0:T(8,128)(2,1)S(1)}, bf16[26,16,256]{2,1,0:T(8,128)(2,1)S(1)}, u32[]{:S(2)}, u32[]{:S(2)}) collective-permute-start(bf16[26,16,256]{2,1,0:T(8,128)(2,1)S(1)} %get-tuple-element.29), channel_id=1, source_target_pairs={{4,8},{8,4},{12,16},{16,12},{20,24},{24,20},{5,9},{9,5},{13,17},{1... | collective-permute-start | bytes 638984 | tf_op jit(solution)/shard_map/ppermute | solution.py:48
  2.6 5.8 %collective-permute-start = (bf16[26,16,256]{2,1,0:T(8,128)(2,1)S(1)}, bf16[26,16,256]{2,1,0:T(8,128)(2,1)S(1)}, u32[]{:S(2)}, u32[]{:S(2)}) collective-permute-start(bf16[26,16,256]{2,1,0:T(8,128)(2,1)S(1)} %get-tuple-element.28.sent), channel_id=1, source_target_pairs={{0,4},{4,0},{8,12},{12,8},{16,20},{20,16},{24,28},{28,24},{1,5},{5... | collective-permute-start | bytes 638984 | tf_op jit(solution)/shard_map/ppermute | solution.py:48
  8.4 0.0 collective-permute-start.2
  8.4 0.7 %collective-permute-start.3 = (bf16[16,16,256]{2,1,0:T(8,128)(2,1)S(1)}, bf16[16,16,256]{2,1,0:T(8,128)(2,1)S(1)}, u32[]{:S(2)}, u32[]{:S(2)}) collective-permute-start(bf16[16,16,256]{2,1,0:T(8,128)(2,1)S(1)} %get-tuple-element.31), channel_id=1, source_target_pairs={{1,2},{2,1},{5,6},{6,5},{9,10},{10,9},{13,14},{14,13},{17,18},{18,... | collective-permute-start | bytes 393224 | tf_op jit(solution)/shard_map/ppermute | solution.py:48
  9.1 4.2 %turn.1.refs_0_.blocks = bf16[16,512,512]{2,1,0:T(8,128)(2,1)S(1)} custom-call(bf16[16,512,512]{2,1,0:T(8,128)(2,1)} %bitcast.12), custom_call_target="tpu_custom_call" | custom-call | tf_op jit(solution)/shard_map/turn/pallas_call | solution.py:633
  13.3 0.0 collective-permute-done.2.refs_1_.side_first
  13.3 0.0 collective-permute-done.3.refs_2_.side_second
  13.3 0.0 collective-permute-done.1.second
  13.3 3.4 %collective-permute-done.first = bf16[26,16,256]{2,1,0:T(8,128)(2,1)S(1)} collective-permute-done((bf16[26,16,256]{2,1,0:T(8,128)(2,1)S(1)}, bf16[26,16,256]{2,1,0:T(8,128)(2,1)S(1)}, u32[]{:S(2)}, u32[]{:S(2)}) %collective-permute-start) | collective-permute-done | bytes 213024 | tf_op jit(solution)/shard_map/ppermute | solution.py:48
  16.8 0.1 mid.1
  16.9 0.7 %collective-permute-start.5 = (bf16[18,16,256]{2,1,0:T(8,128)(2,1)S(1)}, bf16[18,16,256]{2,1,0:T(8,128)(2,1)S(1)}, u32[]{:S(2)}, u32[]{:S(2)}) collective-permute-start(bf16[18,16,256]{2,1,0:T(8,128)(2,1)S(1)} %get-tuple-element.38), channel_id=1, source_target_pairs={{1,2},{2,1},{5,6},{6,5},{9,10},{10,9},{13,14},{14,13},{17,18},{18,... | collective-permute-start | bytes 442376 | tf_op jit(solution)/shard_map/ppermute | solution.py:48
  17.6 2.9 %collective-permute-start.4 = (bf16[18,16,256]{2,1,0:T(8,128)(2,1)S(1)}, bf16[18,16,256]{2,1,0:T(8,128)(2,1)S(1)}, u32[]{:S(2)}, u32[]{:S(2)}) collective-permute-start(bf16[18,16,256]{2,1,0:T(8,128)(2,1)S(1)} %get-tuple-element.32.sent2), channel_id=1, source_target_pairs={{0,1},{1,0},{2,3},{3,2},{4,5},{5,4},{6,7},{7,6},{8,9},{9,8},{10,11... | collective-permute-start | bytes 442376 | tf_op jit(solution)/shard_map/ppermute | solution.py:48
  20.5 0.8 %prep.1 = (f32[2,20,32,256]{3,2,1,0:T(8,128)S(1)}, f32[18,32,256]{2,1,0:T(8,128)S(1)}, f32[2,16,24,256]{3,2,1,0:T(8,128)S(1)}, f32[2,18,32,256]{3,2,1,0:T(8,128)S(1)}, f32[3,14,32,256]{3,2,1,0:T(8,128)S(1)}) custom-call(f32[2,8,16,256]{3,2,1,0:T(8,128)S(1)} %get-tuple-element.25.x0, f32[8,16,256]{2,1,0:T(8,128)S(1)} %get-tuple-element.26.cond, ...), custom_call_target="tpu_custom_call" | custom-call | tf_op jit(solution)/shard_map/prep/pallas_call | solution.py:313
  21.3 0.0 collective-permute-done.5.second
  21.3 0.2 collective-permute-done.4.first
  21.5 7.6 %chain.1 = (f32[2,20,32,256]{3,2,1,0:T(8,128)S(1)}, f32[18,32,256]{2,1,0:T(8,128)S(1)}, f32[2,16,24,256]{3,2,1,0:T(8,128)S(1)}, f32[2,18,32,256]{3,2,1,0:T(8,128...) custom-call(f32[2,20,32,256]{3,2,1,0:T(8,128)S(1)} %get-tuple-elemen, ...), custom_call_target="tpu_custom_call", output_to_operand_aliasing={{0}: (0, {}), {1}: (1, {}), {2}: (2, {}), {3}: (3, {}), {4}... | custom-call | tf_op jit(solution)/shard_map/chain/pallas_call | solution.py:519
  29.1 14.8 %all_to_all.5.every = f32[32,2,128]{2,1,0:T(2,128)S(1)} all-to-all(f32[32,2,128]{2,1,0:T(2,128)S(1)} %get-tuple-element.39), channel_id=1, replica_groups=mesh['brick'=8,'depth'=4] {'brick','depth'}, dimensions={0} | all-to-all | bytes 65536 | tf_op jit(solution)/shard_map/all_to_all | solution.py:716
  43.9 0.0 copy-start
  43.9 0.0 copy-start.1
  43.9 1.4 %combine.1 = (f32[2,8,16,256]{3,2,1,0:T(8,128)}, bf16[8,16,256]{2,1,0:T(8,128)(2,1)S(1)}) custom-call(f32[32,2,128]{2,1,0:T(2,128)S(1)} %all_to_all.5.every, f32[2,8,16,256]{3,2,1,0:T(8,128)S(1)} %get-tuple-element.25.x0, f32[2,8,16,256]{3,2,1,0:T(8,128)S(1)} %get-tuple-element.27.a0, f32[2,18,32,256]{3,2,1,0:T(8,128)S(1)} %get-tuple-element.40.v0, ...), custom_call_target="tpu_custom_call" | custom-call | tf_op jit(solution)/shard_map/combine/pallas_call | solution.py:609
  45.3 5.8 %all-gather = bf16[32,16,256]{2,1,0:T(8,128)(2,1)S(1)} all-gather(bf16[8,16,256]{2,1,0:T(8,128)(2,1)S(1)} %get-tuple-element.47.own), channel_id=2, replica_groups=mesh['brick'=8,'depth'=4] {'depth'}, dimensions={0}, use_global_device_ids=true | all-gather | bytes 327680 | tf_op jit(solution)/shard_map/all_gather | solution.py:718
  51.0 0.0 copy-done
  51.0 0.0 copy-done.1
  51.0 2.3 %covariance.1 = f32[128,256]{1,0:T(8,128)} custom-call(s32[1,16]{1,0:T(1,128)S(1)} %bitcast.10, s32[1,16]{1,0:T(1,128)S(1)} %bitcast.11, bf16[4,8,16,256]{3,2,1,0:T(8,128)(2,1)S(1)} %bitcast.9, bf16[8,16,256]{2,1,0:T(8,128)(2,1)S(1)} %get-tuple-element.47.own, bf16[16,512,512]{2,1,0:T(8,128)(2,1)S(1)} %turn.1.refs_0_.blocks), custom_call_target="tpu_custom_call" | custom-call | tf_op jit(solution)/shard_map/covariance/pallas_call | solution.py:681
Async XLA Ops:
  1.9 11.4 %collective-permute-start.1 = (bf16[26,16,256]{2,1,0:T(8,128)(2,1)S(1)}, bf16[26,16,256]{2,1,0:T(8,128)(2,1)S(1)}, u32[]{:S(2)}, u32[]{:S(2)}) collective-permute-start(bf16[26,16,256]{2,1,0:T(8,128)(2,1)S(1)} %get-tuple-element.29), channel_id=1, source_target_pairs={{4,8},{8,4},{12,16},{16,12},{20,24},{24,20},{5,9},{9,5},{13,17},{1... | collective-permute-start | bytes 638984 | tf_op jit(solution)/shard_map/ppermute | solution.py:48
  2.6 14.2 %collective-permute-start = (bf16[26,16,256]{2,1,0:T(8,128)(2,1)S(1)}, bf16[26,16,256]{2,1,0:T(8,128)(2,1)S(1)}, u32[]{:S(2)}, u32[]{:S(2)}) collective-permute-start(bf16[26,16,256]{2,1,0:T(8,128)(2,1)S(1)} %get-tuple-element.28.sent), channel_id=1, source_target_pairs={{0,4},{4,0},{8,12},{12,8},{16,20},{20,16},{24,28},{28,24},{1,5},{5... | collective-permute-start | bytes 638984 | tf_op jit(solution)/shard_map/ppermute | solution.py:48
  8.4 4.9 %collective-permute-start.2 = (bf16[16,16,256]{2,1,0:T(8,128)(2,1)S(1)}, bf16[16,16,256]{2,1,0:T(8,128)(2,1)S(1)}, u32[]{:S(2)}, u32[]{:S(2)}) collective-permute-start(bf16[16,16,256]{2,1,0:T(8,128)(2,1)S(1)} %get-tuple-element.30), channel_id=1, source_target_pairs={{0,1},{1,0},{2,3},{3,2},{4,5},{5,4},{6,7},{7,6},{8,9},{9,8},{10,11... | collective-permute-start | bytes 393224 | tf_op jit(solution)/shard_map/ppermute | solution.py:48
  8.4 4.9 %collective-permute-start.3 = (bf16[16,16,256]{2,1,0:T(8,128)(2,1)S(1)}, bf16[16,16,256]{2,1,0:T(8,128)(2,1)S(1)}, u32[]{:S(2)}, u32[]{:S(2)}) collective-permute-start(bf16[16,16,256]{2,1,0:T(8,128)(2,1)S(1)} %get-tuple-element.31), channel_id=1, source_target_pairs={{1,2},{2,1},{5,6},{6,5},{9,10},{10,9},{13,14},{14,13},{17,18},{18,... | collective-permute-start | bytes 393224 | tf_op jit(solution)/shard_map/ppermute | solution.py:48
  16.9 4.4 %collective-permute-start.5 = (bf16[18,16,256]{2,1,0:T(8,128)(2,1)S(1)}, bf16[18,16,256]{2,1,0:T(8,128)(2,1)S(1)}, u32[]{:S(2)}, u32[]{:S(2)}) collective-permute-start(bf16[18,16,256]{2,1,0:T(8,128)(2,1)S(1)} %get-tuple-element.38), channel_id=1, source_target_pairs={{1,2},{2,1},{5,6},{6,5},{9,10},{10,9},{13,14},{14,13},{17,18},{18,... | collective-permute-start | bytes 442376 | tf_op jit(solution)/shard_map/ppermute | solution.py:48
  17.6 3.9 %collective-permute-start.4 = (bf16[18,16,256]{2,1,0:T(8,128)(2,1)S(1)}, bf16[18,16,256]{2,1,0:T(8,128)(2,1)S(1)}, u32[]{:S(2)}, u32[]{:S(2)}) collective-permute-start(bf16[18,16,256]{2,1,0:T(8,128)(2,1)S(1)} %get-tuple-element.32.sent2), channel_id=1, source_target_pairs={{0,1},{1,0},{2,3},{3,2},{4,5},{5,4},{6,7},{7,6},{8,9},{9,8},{10,11... | collective-permute-start | bytes 442376 | tf_op jit(solution)/shard_map/ppermute | solution.py:48
  43.9 7.1 %copy-start = (s32[1,1,16]{2,1,0:T(1,128)S(1)}, s32[1,1,16]{2,1,0:T(1,128)}, u32[]{:S(2)}) copy-start(s32[1,1,16]{2,1,0:T(1,128)} %param.19) | copy-start | bytes 196
  43.9 7.1 %copy-start.1 = (s32[1,1,16]{2,1,0:T(1,128)S(1)}, s32[1,1,16]{2,1,0:T(1,128)}, u32[]{:S(2)}) copy-start(s32[1,1,16]{2,1,0:T(1,128)} %param.18) | copy-start | bytes 196
